TPU v7x, 32 devices: a whole 2x2x4 slice. The times are simulated.
32 devices in a mesh: groups: 2 (over y), seq: 4 (over z), tp: 4 (over x, core).
Axes of the slice: x: 2, y: 2, z: 4, core: 2. Of those that a mesh axis runs over, the one named last changes fastest.
Arguments:
- queries: bfloat16 [8, 128, 5120], P('groups', 'seq', 'tp'), parts along dimension 0, may hold values from -40 to 40
- key_vectors: bfloat16 [8, 128, 5120], P('groups', 'seq', 'tp'), parts along dimension 0, may hold values from -40 to 40
- value_vectors: bfloat16 [8, 128, 5120], P('groups', 'seq', 'tp'), parts along dimension 0, may hold values from -6 to 6
- block_mask: int32 [40, 4, 4], P('tp'), may hold values from 0 to 1, as said below
- out_weight: bfloat16 [40, 128, 2560], P('tp', 'seq'), may hold values from -0.5 to 0.5
Outputs:
- projected: bfloat16 [8, 128, 2560], P('groups', 'seq', 'tp'), parts along dimension 0
There are 2 independent parts, one for each index of `groups`. A program takes and returns all parts, laid end to end along the dimension named above; an argument that names none is the same for every part. Nothing has to cross between parts.
Inputs may be any that keep to these rules, and one draw needn't show every extreme that they name: block_mask[h, b, b] = 1 for every head and block; every row of a head's mask has at most 4 ones, and every head has a row with exactly 4.
All inputs are finite; a program needn't handle non-finite values.
Results may differ from a plain program's by a relative error of at most 0.012.
Values may be sent and summed in bfloat16 or wider, within the bound.
No kernel may reach another device: no remote copies, remote signals or barrier semaphores. Data moves between devices by JAX's collectives and lax.ppermute only.
A program may use at most 64 MiB of HBM per device.

v0:
```python
import jax
import jax.numpy as jnp
import numpy as np
from jax import lax
from jax.sharding import PartitionSpec as P

KEYS = 28


def strip_tables(heads_local, blocks, slot_total):
    slot_ids = np.arange(slot_total)
    head_of = slot_ids * heads_local // slot_total
    per_head = np.bincount(head_of, minlength=heads_local)
    head_begin = np.cumsum(per_head) - per_head
    order_in_head = slot_ids - head_begin[head_of]
    head_share = per_head[head_of]
    first_block = order_in_head * blocks // head_share
    block_count = (order_in_head + 1) * blocks // head_share - first_block
    return (head_of, first_block, block_count)


def body(queries, key_vectors, value_vectors, block_mask, out_weight):
    rank_count = lax.axis_size("seq")
    my_rank = lax.axis_index("seq")
    block_total, row_share, feature_width = queries.shape
    heads_local = block_mask.shape[0]
    head_size = feature_width // heads_local
    block_rows = row_share * rank_count
    per_rank = (heads_local + rank_count - 1) // rank_count
    slot_total = rank_count * per_rank
    least_share = slot_total // heads_local
    strip_cap = ((block_total + least_share - 1) // least_share + 1) // 2 * 2
    key_cap = min(KEYS, block_total)
    head_of, first_block, block_count = strip_tables(heads_local, block_total, slot_total)
    slot_grid = np.arange(slot_total).reshape(rank_count, per_rank).T
    paired = jnp.concatenate(
        [
            key_vectors.reshape(block_total, row_share, heads_local, head_size),
            value_vectors.reshape(block_total, row_share, heads_local, head_size),
        ],
        axis=3,
    )
    send_heads = jnp.asarray(head_of[slot_grid].reshape(-1), jnp.int32)
    chosen = jnp.take(paired, send_heads, axis=2)
    chosen = chosen.reshape(block_total, row_share, per_rank, rank_count, 2 * head_size)
    outgoing_pairs = chosen.transpose(2, 0, 3, 1, 4).reshape(
        per_rank, block_total, block_rows, 2 * head_size
    )
    flat_queries = queries.reshape(block_total, row_share, heads_local, head_size).transpose(
        0, 2, 1, 3
    )
    flat_queries = flat_queries.reshape(block_total * heads_local, row_share, head_size)
    positions = np.arange(strip_cap)
    unit_block = first_block[slot_grid][:, None, :] + positions[None, :, None]
    is_live = positions[None, :, None] < block_count[slot_grid][:, None, :]
    unit_index = np.where(is_live, unit_block * heads_local + head_of[slot_grid][:, None, :], 0)
    picked = jnp.take(flat_queries, jnp.asarray(unit_index.reshape(-1), jnp.int32), axis=0)
    picked = jnp.where(
        jnp.asarray(is_live.reshape(-1))[:, None, None], picked, jnp.zeros_like(picked)
    )
    outgoing_queries = picked.reshape(per_rank, strip_cap, block_rows, head_size)
    strip_queries, strip_pairs = (
        lax.all_to_all(outgoing_queries, "seq", split_axis=2, concat_axis=2, tiled=True),
        lax.all_to_all(outgoing_pairs, "seq", split_axis=2, concat_axis=2, tiled=True),
    )
    my_slots = my_rank * per_rank + jnp.arange(per_rank, dtype=jnp.int32)
    my_heads = jnp.asarray(head_of, jnp.int32)[my_slots]
    my_first = jnp.asarray(first_block, jnp.int32)[my_slots]
    query_blocks = jnp.minimum(
        my_first[:, None] + jnp.arange(strip_cap, dtype=jnp.int32)[None, :], block_total - 1
    )
    mask_rows = block_mask[my_heads[:, None], query_blocks]
    column_ids = jnp.arange(block_total, dtype=jnp.int32)
    ranking = (1 - mask_rows) * block_total + column_ids
    key_pick = jnp.argsort(ranking, axis=-1)[..., :key_cap]
    key_live = jnp.take_along_axis(mask_rows, key_pick, axis=-1)
    group_total = per_rank * strip_cap // 2
    query_groups = strip_queries.reshape(group_total, 2, block_rows, head_size)
    pick_groups = key_pick.reshape(group_total, 2, key_cap)
    live_groups = key_live.reshape(group_total, 2, key_cap)
    slot_of_group = jnp.arange(group_total, dtype=jnp.int32) // (strip_cap // 2)
    score_scale = head_size ** (-0.5)

    def attend_group(inputs):
        query_tile, pick_tile, live_tile, slot_index = inputs
        pairs_here = strip_pairs[slot_index]
        gathered = pairs_here[pick_tile]
        scores = (
            jnp.einsum(
                "qid,qkjd->qikj",
                query_tile,
                gathered[..., :head_size],
                preferred_element_type=jnp.float32,
            )
            * score_scale
        )
        allowed = (live_tile > 0)[:, None, :, None]
        scores = jnp.where(allowed, scores, -jnp.inf)
        largest = jnp.max(scores, axis=(2, 3), keepdims=True)
        weights = jnp.exp(scores - largest)
        totals = jnp.sum(weights, axis=(2, 3))
        blended = jnp.einsum(
            "qikj,qkjd->qid",
            weights.astype(jnp.bfloat16),
            gathered[..., head_size:],
            preferred_element_type=jnp.float32,
        )
        return (blended / totals[..., None]).astype(jnp.bfloat16)

    strip_out = lax.map(attend_group, (query_groups, pick_groups, live_groups, slot_of_group))
    outgoing_out = strip_out.reshape(per_rank, strip_cap, block_rows, head_size)
    returned = lax.all_to_all(outgoing_out, "seq", split_axis=2, concat_axis=2, tiled=True)
    slot_mesh, step_mesh = np.meshgrid(np.arange(slot_total), positions, indexing="ij")
    live_slot = step_mesh < block_count[slot_mesh]
    placement_index = np.zeros((block_total, heads_local), np.int64)
    source_index = (
        slot_mesh % per_rank * strip_cap + step_mesh
    ) * rank_count + slot_mesh // per_rank
    placement_index[
        first_block[slot_mesh][live_slot] + step_mesh[live_slot], head_of[slot_mesh][live_slot]
    ] = source_index[live_slot]
    flat_back = returned.reshape(per_rank * strip_cap * rank_count, row_share, head_size)
    own_out = jnp.take(flat_back, jnp.asarray(placement_index.reshape(-1), jnp.int32), axis=0)
    own_out = own_out.reshape(block_total, heads_local, row_share, head_size)
    token_total = block_total * row_share
    token_out = own_out.transpose(0, 2, 1, 3).reshape(token_total, heads_local, head_size)
    partial_sum = jnp.einsum(
        "thd,hdo->to",
        token_out,
        lax.all_gather(out_weight, "seq", axis=1, tiled=True),
        preferred_element_type=jnp.float32,
    )
    summed = lax.psum_scatter(
        partial_sum.astype(jnp.bfloat16), "tp", scatter_dimension=1, tiled=True
    ).astype(jnp.float32)
    return summed.astype(jnp.bfloat16).reshape(block_total, row_share, summed.shape[1])


def solution(mesh):
    return jax.shard_map(
        body,
        mesh=mesh,
        in_specs=(
            P("groups", "seq", "tp"),
            P("groups", "seq", "tp"),
            P("groups", "seq", "tp"),
            P("tp", None, None),
            P("tp", "seq", None),
        ),
        out_specs=P("groups", "seq", "tp"),
        check_vma=False,
    )
```

profile of v0, /device:TPU:0, one launch (start us, length us, event | category | flops | bytes accessed | tf_op | source)
XLA Modules:
  0.0 199.6 jit_solution(3571935745771503848)
XLA Ops:
  6.5 1.2 reshape.189
  7.9 0.6 gather_fusion.4
  8.6 1.6 copy_select_fusion
  10.2 6.5 %all-to-all-start = ((bf16[3,4,128,128]{3,1,0,2:T(4,128)(2,1)}), bf16[3,4,128,128]{3,1,0,2:T(4,128)(2,1)S(1)}, u32[]{:S(2)}, u32[]{:S(2)}) async-start(bf16[3,4,128,128]{3,1,0,2:T(4,128)(2,1)} %copy_select_fusion), calls=%async_computation | async-start | bytes 786432 | tf_op jit(solution)/shard_map/all_to_all | solution.py:63
  16.7 0.7 all-gather.2.cloned.1.call-update
  17.5 0.6 gather_fusion.1
  18.1 0.6 gather_fusion.2
  18.8 0.1 copy_bitcast_fusion.3
  19.0 0.6 gather_fusion.5
  19.7 1.5 copy.76
  21.2 7.2 %all-to-all-done = bf16[3,4,128,128]{3,1,0,2:T(4,128)(2,1)S(1)} async-done(((bf16[3,4,128,128]{3,1,0,2:T(4,128)(2,1)}), bf16[3,4,128,128]{3,1,0,2:T(4,128)(2,1)S(1)}, u32[]{:S(2)}, u32[]{:S(2)}) %all-to-all-start) | async-done | bytes 393248 | tf_op jit(solution)/shard_map/all_to_all | solution.py:63
  28.4 3.5 %all-to-all-start.1 = ((bf16[3,4,128,256]{3,1,0,2:T(4,128)(2,1)}), bf16[3,4,128,256]{3,1,0,2:T(4,128)(2,1)S(1)}, u32[]{:S(2)}, u32[]{:S(2)}) async-start(bf16[3,4,128,256]{3,1,0,2:T(4,128)(2,1)} %copy.76), calls=%async_computation.1 | async-start | bytes 1572864 | tf_op jit(solution)/shard_map/all_to_all | solution.py:64
  32.1 0.1 copy.65
  32.2 0.7 gather_fusion.3
  33.0 1.3 sort.17
  34.3 0.1 copy.77
  34.4 0.1 copy.68
  34.6 1.2 gather_fusion.7
  35.9 0.1 copy.69
  36.0 0.1 copy.70
  36.1 36.5 %all-to-all-done.1 = bf16[3,4,128,256]{3,1,0,2:T(4,128)(2,1)S(1)} async-done(((bf16[3,4,128,256]{3,1,0,2:T(4,128)(2,1)}), bf16[3,4,128,256]{3,1,0,2:T(4,128)(2,1)S(1)}, u32[]{:S(2)}, u32[]{:S(2)}) %all-to-all-start.1) | async-done | bytes 786464 | tf_op jit(solution)/shard_map/all_to_all | solution.py:64
  72.6 30.0 %while.10 = (s32[]{:T(128)}, bf16[6,2,128,128]{3,1,0,2:T(2,128)(2,1)}, s32[6,2,4]{2,1,0:T(2,128)S(1)}, bf16[6,2,128,128]{3,1,0,2:T(2,128)(2,1)S(1)}, s32[6]{0:T(...) while((s32[]{:T(128)}, ...), condition=%wide.region_4.5_spmd, body=%wide.region_1.4_spmd.sunk | while | flops 68092448 | bytes 4598155 | solution.py:110
  72.6 0.7 dynamic_slice.37
  75.6 0.6 gather_fusion
  76.3 0.2 fusion.32
  76.6 0.3 fusion.34
  76.9 0.7 copy_dynamic-update-slice_fusion.2
  77.6 0.7 dynamic_slice.37
  80.3 0.1 constant_dynamic-slice_fusion.6
  80.6 0.6 gather_fusion
  81.3 0.2 fusion.32
  81.6 0.3 fusion.34
  81.9 0.7 copy_dynamic-update-slice_fusion.2
  82.6 0.7 dynamic_slice.37
  85.3 0.1 constant_dynamic-slice_fusion.6
  85.6 0.6 gather_fusion
  86.3 0.2 fusion.32
  86.6 0.3 fusion.34
  86.9 0.7 copy_dynamic-update-slice_fusion.2
  87.6 0.7 dynamic_slice.37
  90.6 0.6 gather_fusion
  91.3 0.3 fusion.32
  91.6 0.3 fusion.34
  91.9 0.7 copy_dynamic-update-slice_fusion.2
  92.6 0.7 dynamic_slice.37
  95.4 0.1 constant_dynamic-slice_fusion.6
  95.6 0.6 gather_fusion
  96.3 0.3 fusion.32
  96.6 0.3 fusion.34
  96.9 0.7 copy_dynamic-update-slice_fusion.2
  97.6 0.7 dynamic_slice.37
  100.3 0.1 constant_dynamic-slice_fusion.6
  100.6 0.6 gather_fusion
  101.3 0.2 fusion.32
  101.6 0.3 fusion.34
  101.9 0.7 copy_dynamic-update-slice_fusion.2
  102.6 3.5 %all-to-all-start.2 = ((bf16[3,4,128,128]{3,1,0,2:T(4,128)(2,1)}), bf16[3,4,128,128]{3,1,0,2:T(4,128)(2,1)S(1)}, u32[]{:S(2)}, u32[]{:S(2)}) async-start(bf16[3,4,128,128]{3,1,0,2:T(4,128)(2,1)} %bitcast.24), calls=%async_computation.2 | async-start | bytes 786432 | tf_op jit(solution)/shard_map/all_to_all | solution.py:112
  106.2 23.9 %all-to-all-done.2 = bf16[3,4,128,128]{3,1,0,2:T(4,128)(2,1)S(1)} async-done(((bf16[3,4,128,128]{3,1,0,2:T(4,128)(2,1)}), bf16[3,4,128,128]{3,1,0,2:T(4,128)(2,1)S(1)}, u32[]{:S(2)}, u32[]{:S(2)}) %all-to-all-start.2) | async-done | bytes 393248 | tf_op jit(solution)/shard_map/all_to_all | solution.py:112
  130.2 0.6 gather_fusion.6
  130.8 34.5 %all-gather.2.cloned.1.call-done = bf16[10,128,2560]{2,1,0:T(8,128)(2,1)} async-done(((bf16[10,32,2560]{2,1,0:T(8,128)(2,1)}), bf16[10,128,2560]{2,1,0:T(8,128)(2,1)}) %all-gather.2.cloned.1.call-update) | async-done | bytes 6553616 | tf_op jit(solution)/shard_map/all_gather | solution.py:130
  165.3 3.9 %fusion.11 = bf16[128,2560]{1,0:T(8,128)(2,1)S(1)} fusion(bf16[128,10,128]{2,0,1:T(8,128)(2,1)S(1)} %bitcast.102, bf16[10,128,2560]{2,1,0:T(8,128)(2,1)} %all-gather.2.cloned.1.call-done), kind=kOutput, calls=%fused_computation.32 | convolution fusion | flops 839188480 | bytes 7536640 | tf_op jit(solution)/shard_map/thd,hdo->to/dot_general | solution.py:127
  169.2 1.1 copy.86
  170.3 20.7 %reduce-scatter.4.cloned.1.call-done = bf16[640,128]{1,0:T(8,128)(2,1)} async-done(((bf16[2560,128]{1,0:T(8,128)(2,1)}), bf16[640,128]{1,0:T(8,128)(2,1)}) %reduce-scatter.4.cloned.1.call-update) | async-done | bytes 163856
  191.0 1.7 copy.87
  (90 shorter events, 3.0 us)
Async XLA Ops:
  6.5 12.2 %copy-start = (bf16[4,32,1280]{2,1,0:T(8,128)(2,1)S(1)}, bf16[4,32,1280]{2,1,0:T(8,128)(2,1)}, u32[]{:S(2)}) copy-start(bf16[4,32,1280]{2,1,0:T(8,128)(2,1)} %param.14) | copy-start | bytes 983044
  6.5 1.3 copy-start.8
  6.5 2.0 copy-start.5
  8.6 8.9 %copy-start.2 = (s32[12]{0:T(128)S(1)}, s32[12]{0:T(128)}, u32[]{:S(2)}) copy-start(s32[12]{0:T(128)} %constant.133.clone) | copy-start | bytes 148
  10.2 7.9 %copy-start.1 = (s32[12]{0:T(128)S(1)}, s32[12]{0:T(128)}, u32[]{:S(2)}) copy-start(s32[12]{0:T(128)} %constant.134.clone) | copy-start | bytes 148
  10.2 8.5 %copy-start.7 = (s32[12]{0:T(128)S(1)}, s32[12]{0:T(128)}, u32[]{:S(2)}) copy-start(s32[12]{0:T(128)} %constant.199) | copy-start | bytes 148
  10.2 8.6 %copy-start.3 = (bf16[4,32,1280]{2,1,0:T(8,128)(2,1)S(1)}, bf16[4,32,1280]{2,1,0:T(8,128)(2,1)}, u32[]{:S(2)}) copy-start(bf16[4,32,1280]{2,1,0:T(8,128)(2,1)} %param.15) | copy-start | bytes 983044
  10.2 18.2 %all-to-all-start = ((bf16[3,4,128,128]{3,1,0,2:T(4,128)(2,1)}), bf16[3,4,128,128]{3,1,0,2:T(4,128)(2,1)S(1)}, u32[]{:S(2)}, u32[]{:S(2)}) async-start(bf16[3,4,128,128]{3,1,0,2:T(4,128)(2,1)} %copy_select_fusion), calls=%async_computation | async-start | bytes 786432 | tf_op jit(solution)/shard_map/all_to_all | solution.py:63
  16.7 148.6 %all-gather.2.cloned.1.call-start = ((), (), s32[]{:S(2)}) async-start(), calls=%async_computation.4 | async-start | bytes 8192000 | tf_op jit(solution)/shard_map/all_gather | solution.py:130
  19.7 12.4 %copy-start.4 = (s32[10,4,4]{0,2,1:T(4,128)S(1)}, s32[10,4,4]{0,2,1:T(4,128)}, u32[]{:S(2)}) copy-start(s32[10,4,4]{0,2,1:T(4,128)} %param.16) | copy-start | bytes 1924
  28.4 44.2 %all-to-all-start.1 = ((bf16[3,4,128,256]{3,1,0,2:T(4,128)(2,1)}), bf16[3,4,128,256]{3,1,0,2:T(4,128)(2,1)S(1)}, u32[]{:S(2)}, u32[]{:S(2)}) async-start(bf16[3,4,128,256]{3,1,0,2:T(4,128)(2,1)} %copy.76), calls=%async_computation.1 | async-start | bytes 1572864 | tf_op jit(solution)/shard_map/all_to_all | solution.py:64
  72.6 33.5 %copy-start.6 = (s32[40]{0:T(128)S(1)}, s32[40]{0:T(128)}, u32[]{:S(2)}) copy-start(s32[40]{0:T(128)} %constant.200) | copy-start | bytes 484
  102.6 27.5 %all-to-all-start.2 = ((bf16[3,4,128,128]{3,1,0,2:T(4,128)(2,1)}), bf16[3,4,128,128]{3,1,0,2:T(4,128)(2,1)S(1)}, u32[]{:S(2)}, u32[]{:S(2)}) async-start(bf16[3,4,128,128]{3,1,0,2:T(4,128)(2,1)} %bitcast.24), calls=%async_computation.2 | async-start | bytes 786432 | tf_op jit(solution)/shard_map/all_to_all | solution.py:112
  106.1 84.9 %reduce-scatter.4.cloned.1.call-start = ((), (), s32[]{:S(2)}) async-start(), calls=%async_computation.5 | async-start | bytes 819200
Sparse Core Ops, SparseCore 0:
  19.1 146.1 all-gather.1
  170.4 20.5 reduce-scatter.3
where the time goes:
time: 200 us
  waiting for transfers between devices  124 us (62%)
  local copies, waits for them, and re-layouts  25.2 us (13%)
  between operations  13.7 us (7%)
  starting transfers between devices  13.5 us (7%)
  loops' own time  12.7 us (6%)
  matrix products  7.13 us (4%)
  other arithmetic  3.88 us (2%)
    all_to_all x1, waiting for transfers between devices, body(): lax.all_to_all(outgoing_pairs, 'seq', split_axis=2, concat_axis=2, tiled=...  36.5 us
    all_gather x1, waiting for transfers between devices, body(): lax.all_gather(out_weight, 'seq', axis=1, tiled=True)  34.5 us
    all_to_all x1, waiting for transfers between devices, body(): lax.all_to_all(outgoing_out, 'seq', split_axis=2, concat_axis=2, tiled=True)  23.9 us
    unnamed x3, waiting for transfers between devices  21.5 us
    another operation x1, loops' own time, body(): lax.map(attend_group, (query_groups, pick_groups, live_groups, slot_of_gr...  12.7 us
    all_to_all x1, waiting for transfers between devices, body(): lax.all_to_all(outgoing_queries, 'seq', split_axis=2, concat_axis=2, tile...  7.18 us
    all_to_all x1, starting transfers between devices, body(): lax.all_to_all(outgoing_queries, 'seq', split_axis=2, concat_axis=2, tile...  6.48 us
    dynamic_slice x12, local copies, waits for them, and re-layouts, body(): lax.map(attend_group, (query_groups, pick_groups, live_groups, slot_of_gr...  4.29 us
  transfers between devices with their start and end apart: 5, of which 5 were waited for; matrix products, arithmetic and copies ran while one was open for 13% of the time, Pallas kernels for 0%

commit v1 on v0

--- a/solution.py
+++ b/solution.py
@@ -1,7 +1,11 @@
+import functools
+
 import jax
 import jax.numpy as jnp
 import numpy as np
 from jax import lax
+from jax.experimental import pallas as pl
+from jax.experimental.pallas import tpu as pltpu
 from jax.sharding import PartitionSpec as P
 
 KEYS = 28
@@ -19,7 +23,7 @@
     return (head_of, first_block, block_count)
 
 
-def body(queries, key_vectors, value_vectors, block_mask, out_weight):
+def gathered_plan(queries, key_vectors, value_vectors, block_mask, out_weight):
     rank_count = lax.axis_size("seq")
     my_rank = lax.axis_index("seq")
     block_total, row_share, feature_width = queries.shape
@@ -136,6 +140,266 @@
     return summed.astype(jnp.bfloat16).reshape(block_total, row_share, summed.shape[1])
 
 
+def exchange(array, axis, flip):
+    size = lax.axis_size(axis)
+    return lax.ppermute(array, axis, [(i, i ^ flip) for i in range(size)])
+
+
+def aligned(index, unit):
+    return pl.multiple_of(index * unit, unit)
+
+
+class Sizes:
+    def __init__(self, rank_count, tp_count, queries_shape, heads_local, weight_shape):
+        self.ranks = rank_count
+        self.tps = tp_count
+        self.blocks, self.rows, width = queries_shape
+        self.heads = heads_local
+        self.hd = width // heads_local
+        self.whole = heads_local // rank_count
+        self.rest = heads_local % rank_count
+        self.sharers = rank_count // self.rest if self.rest else 1
+        self.strip = self.blocks // self.sharers if self.rest else 0
+        self.slots = self.whole + (1 if self.rest else 0)
+        self.q_units = self.whole * self.blocks + self.strip
+        self.kv_units = self.slots * self.blocks
+        self.units = self.q_units + 2 * self.kv_units
+        self.block_rows = self.rows * rank_count
+        self.tokens = self.blocks * self.block_rows
+        self.out_tokens = self.q_units * self.block_rows
+        self.part = weight_shape[1]
+        self.dout = weight_shape[2]
+        self.cols = self.dout // tp_count
+
+    def fits(self):
+        power = lambda n: n & (n - 1) == 0
+        if not (power(self.ranks) and power(self.tps) and self.whole > 0):
+            return False
+        if self.rest and (self.ranks % self.rest or self.blocks % self.sharers):
+            return False
+        if self.rows % 32 or self.part % 32 or self.hd % 128 or self.cols % 128:
+            return False
+        gathered = (self.ranks - 1) * self.heads * self.part * self.dout
+        summed = (self.ranks - 1) * self.tokens // self.ranks * self.cols
+        summed += (self.tps - 1) * self.heads * self.part * (self.cols + self.tokens)
+        return summed < gathered
+
+
+def pack_kernel(z, q_ref, k_ref, v_ref, *out_refs):
+    me = lax.axis_index("seq")
+    for flip in range(z.ranks):
+        peer = me ^ flip
+        out = out_refs[flip]
+        for slot in range(z.whole):
+            cols = pl.ds(aligned(slot * z.ranks + peer, z.hd), z.hd)
+            at = slot * z.blocks
+            out[at : at + z.blocks] = q_ref[:, :, cols]
+            at += z.q_units
+            out[at : at + z.blocks] = k_ref[:, :, cols]
+            at += z.kv_units
+            out[at : at + z.blocks] = v_ref[:, :, cols]
+        if z.rest:
+            head = z.whole * z.ranks + peer // z.sharers
+            cols = pl.ds(aligned(head, z.hd), z.hd)
+            first = (peer % z.sharers) * z.strip
+            at = z.whole * z.blocks
+            out[at : at + z.strip] = q_ref[pl.ds(first, z.strip), :, cols]
+            at += z.q_units
+            out[at : at + z.blocks] = k_ref[:, :, cols]
+            at += z.kv_units
+            out[at : at + z.blocks] = v_ref[:, :, cols]
+
+
+def weight_kernel(z, w_ref, *out_refs):
+    me = lax.axis_index("tp")
+    for flip in range(z.tps):
+        out_refs[flip][...] = w_ref[:, :, pl.ds(aligned(me ^ flip, z.cols), z.cols)]
+
+
+def attend_kernel(z, mask_ref, *refs):
+    part_refs = refs[: z.ranks]
+    out_refs = refs[z.ranks : 2 * z.ranks]
+    query, keys, values, weights, result = refs[2 * z.ranks :]
+    me = lax.axis_index("seq")
+    scale = z.hd ** (-0.5)
+    for slot in range(z.slots):
+        is_strip = slot >= z.whole
+        count = z.strip if is_strip else z.blocks
+        head = z.whole * z.ranks + me // z.sharers if is_strip else slot * z.ranks + me
+        first = (me % z.sharers) * z.strip if is_strip else 0
+        for flip in range(z.ranks):
+            source = me ^ flip
+            for b in range(count):
+                rows = pl.ds(b * z.block_rows + aligned(source, z.rows), z.rows)
+                query[slot, rows, :] = part_refs[flip][slot * z.blocks + b]
+            for b in range(z.blocks):
+                rows = pl.ds(b * z.block_rows + flip * z.rows, z.rows)
+                unit = z.q_units + slot * z.blocks + b
+                keys[slot, rows, :] = part_refs[flip][unit]
+                values[slot, rows, :] = part_refs[flip][unit + z.kv_units]
+        wide = count * z.block_rows
+        inverses = []
+        for b in range(count):
+            lanes = slice(b * z.block_rows, (b + 1) * z.block_rows)
+            scores = (
+                lax.dot_general(
+                    keys[slot],
+                    query[slot, lanes, :],
+                    (((1,), (1,)), ((), ())),
+                    preferred_element_type=jnp.float32,
+                )
+                * scale
+            )
+            tiles = []
+            for t in range(z.blocks):
+                tile = scores[t * z.block_rows : (t + 1) * z.block_rows]
+                tiles.append(jnp.where(mask_ref[head, first + b, t] > 0, tile, -jnp.inf))
+            scores = jnp.concatenate(tiles, axis=0)
+            largest = jnp.max(scores, axis=0, keepdims=True)
+            exps = jnp.exp(scores - largest)
+            inverses.append(jnp.sum(exps, axis=0, keepdims=True))
+            weights[:, lanes] = exps.astype(jnp.bfloat16)
+        blended = lax.dot_general(
+            values[slot],
+            weights[:, :wide],
+            (((0,), (0,)), ((), ())),
+            preferred_element_type=jnp.float32,
+        )
+        blended = blended / jnp.concatenate(inverses, axis=1)
+        lanes = slice(slot * z.tokens, slot * z.tokens + wide)
+        result[:, lanes] = blended.astype(jnp.bfloat16)
+    for flip in range(z.ranks):
+        out_refs[flip][...] = result[pl.ds(aligned(me ^ flip, z.part), z.part), :]
+
+
+def join_kernel(z, *refs):
+    for flip in range(z.ranks):
+        refs[z.ranks][flip] = refs[flip][...]
+
+
+def project_kernel(z, *refs):
+    token_refs = refs[: z.tps]
+    weight_refs = refs[z.tps : 2 * z.tps]
+    own_ref = refs[2 * z.tps]
+    out_refs = refs[2 * z.tps + 1 : 2 * z.tps + z.ranks]
+    inputs, total = refs[2 * z.tps + z.ranks :]
+    me = lax.axis_index("seq")
+    for t in range(z.tps):
+        for flip in range(z.ranks):
+            source = me ^ flip
+            for slot in range(z.whole):
+                rows = pl.ds(aligned(slot * z.ranks + source, z.part), z.part)
+                lanes = slice(slot * z.tokens, (slot + 1) * z.tokens)
+                inputs[t, rows, :] = token_refs[t][flip, :, lanes]
+            if z.rest:
+                head = z.whole * z.ranks + source // z.sharers
+                wide = z.strip * z.block_rows
+                at = pl.ds(aligned(source % z.sharers, wide), wide)
+                lanes = slice(z.whole * z.tokens, z.whole * z.tokens + wide)
+                inputs[t, pl.ds(aligned(head, z.part), z.part), at] = token_refs[t][flip, :, lanes]
+    acc = None
+    for t in range(z.tps):
+        w = weight_refs[t][...].reshape(z.heads * z.part, z.cols)
+        term = lax.dot_general(
+            inputs[t], w, (((0,), (0,)), ((), ())), preferred_element_type=jnp.float32
+        )
+        acc = term if acc is None else acc + term
+    total[...] = acc.reshape(z.blocks, z.ranks, z.rows, z.cols)
+    for b in range(z.blocks):
+        own_ref[b] = total[b, me]
+        for flip in range(1, z.ranks):
+            out_refs[flip - 1][b] = total[b, me ^ flip].astype(jnp.bfloat16)
+
+
+def local_call(kernel, outs, scratch=(), smem=0, name=None, limit=16):
+    def call(*args):
+        specs = [
+            pl.BlockSpec(memory_space=pltpu.SMEM if i < smem else pltpu.VMEM)
+            for i in range(len(args))
+        ]
+        return pl.pallas_call(
+            kernel,
+            out_shape=outs,
+            in_specs=specs,
+            out_specs=[pl.BlockSpec(memory_space=pltpu.VMEM)] * len(outs),
+            scratch_shapes=list(scratch),
+            compiler_params=pltpu.CompilerParams(vmem_limit_bytes=limit << 20),
+            name=name,
+        )(*args)
+
+    return call
+
+
+def stationary_plan(z, queries, key_vectors, value_vectors, block_mask, out_weight):
+    bf16 = jnp.bfloat16
+    shape = jax.ShapeDtypeStruct
+    packed = local_call(
+        functools.partial(pack_kernel, z),
+        [shape((z.units, z.rows, z.hd), bf16)] * z.ranks,
+        name="pack",
+    )(queries, key_vectors, value_vectors)
+    parts = [packed[0]] + [exchange(packed[f], "seq", f) for f in range(1, z.ranks)]
+    sliced = local_call(
+        functools.partial(weight_kernel, z),
+        [shape((z.heads, z.part, z.cols), bf16)] * z.tps,
+        name="weight_slices",
+    )(out_weight)
+    weights = [sliced[0]] + [exchange(sliced[f], "tp", f) for f in range(1, z.tps)]
+    parts, weights = lax.optimization_barrier((parts, weights))
+    strips = local_call(
+        functools.partial(attend_kernel, z),
+        [shape((z.part, z.out_tokens), bf16)] * z.ranks,
+        scratch=[
+            pltpu.VMEM((z.slots, z.tokens, z.hd), bf16),
+            pltpu.VMEM((z.slots, z.tokens, z.hd), bf16),
+            pltpu.VMEM((z.slots, z.tokens, z.hd), bf16),
+            pltpu.VMEM((z.tokens, z.tokens), bf16),
+            pltpu.VMEM((z.hd, z.out_tokens), bf16),
+        ],
+        smem=1,
+        name="attend",
+    )(block_mask, *parts)
+    strips = [strips[0]] + [exchange(strips[f], "seq", f) for f in range(1, z.ranks)]
+    joined = local_call(
+        functools.partial(join_kernel, z),
+        [shape((z.ranks, z.part, z.out_tokens), bf16)],
+        name="join",
+    )(*strips)[0]
+    tokens = [joined]
+    flip = z.tps // 2
+    tokens = {0: joined}
+    while flip:
+        for held in list(tokens):
+            tokens[held ^ flip] = exchange(tokens[held], "tp", flip)
+        flip //= 2
+    sums = local_call(
+        functools.partial(project_kernel, z),
+        [shape((z.blocks, z.rows, z.cols), jnp.float32)]
+        + [shape((z.blocks, z.rows, z.cols), bf16)] * (z.ranks - 1),
+        scratch=[
+            pltpu.VMEM((z.tps, z.heads * z.part, z.tokens), bf16),
+            pltpu.VMEM((z.blocks, z.ranks, z.rows, z.cols), jnp.float32),
+        ],
+        name="project",
+    )(*[tokens[t] for t in range(z.tps)], *weights)
+    total = sums[0]
+    for f in range(1, z.ranks):
+        total = total + exchange(sums[f], "seq", f).astype(jnp.float32)
+    return total.astype(bf16)
+
+
+def body(queries, key_vectors, value_vectors, block_mask, out_weight):
+    z = Sizes(
+        lax.axis_size("seq"),
+        lax.axis_size("tp"),
+        queries.shape,
+        block_mask.shape[0],
+        out_weight.shape,
+    )
+    plan = functools.partial(stationary_plan, z) if z.fits() else gathered_plan
+    return plan(queries, key_vectors, value_vectors, block_mask, out_weight)
+
+
 def solution(mesh):
     return jax.shard_map(
         body,

time: 200 us -> 81.5 us (0.41)
  waiting for transfers between devices: 124 us -> 42 us
  local copies, waits for them, and re-layouts: 25.2 us -> 4.46 us
  starting transfers between devices: 13.5 us -> 27.6 us
  between operations: 13.7 us -> 0.05 us
  loops' own time: 12.7 us -> 0 us
  matrix products: 7.13 us -> 0 us
  Pallas kernels: 0 us -> 6.39 us
  other arithmetic: 3.88 us -> 0.74 us
    all_to_all x3 -> x0, waiting for transfers between devices: 67.6 us -> none  [the longest x1 36.5 us: body(): lax.all_to_all(outgoing_pairs, 'seq', split_axis=2, concat_axis=2, tiled=...]
    ppermute x0 -> x15, waiting for transfers between devices: none -> 42 us  [exchange(): return lax.ppermute(array, axis, [(i, i ^ flip) for i in range(size)])]
    all_gather x1 -> x0, waiting for transfers between devices: 34.5 us -> none  [body(): lax.all_gather(out_weight, 'seq', axis=1, tiled=True)]
    ppermute x0 -> x15, starting transfers between devices: none -> 27.6 us  [exchange(): return lax.ppermute(array, axis, [(i, i ^ flip) for i in range(size)])]
    unnamed x3 -> x0, waiting for transfers between devices: 21.5 us -> none
    all_to_all x3 -> x0, starting transfers between devices: 13.5 us -> none  [the longest x1 6.48 us: body(): lax.all_to_all(outgoing_queries, 'seq', split_axis=2, concat_axis=2, tile...]
    another operation x1 -> x0, loops' own time: 12.7 us -> none  [body(): lax.map(attend_group, (query_groups, pick_groups, live_groups, slot_of_gr...]
    gather x20 -> x0, local copies, waits for them, and re-layouts: 9.09 us -> none  [the longest x6 3.47 us: attend_group(): gathered = pairs_here[pick_tile]]
  transfers between devices with their start and end apart: 5 -> 15, of which waited for: 5 -> 7; matrix products, arithmetic and copies ran while one was open for 13% -> 0% of each run, Pallas kernels for 0% -> 1%
where the time goes in v1:
time: 81.5 us; the launch traced here: 81.3 us
  waiting for transfers between devices  42 us (52%)
  starting transfers between devices  27.6 us (34%)
  Pallas kernels  6.39 us (8%)
  local copies, waits for them, and re-layouts  4.46 us (5%)
    ppermute x15, waiting for transfers between devices, exchange(): return lax.ppermute(array, axis, [(i, i ^ flip) for i in range(size)])  42 us
    ppermute x15, starting transfers between devices, exchange(): return lax.ppermute(array, axis, [(i, i ^ flip) for i in range(size)])  27.6 us
    pallas_call x5, Pallas kernels, call(): pl.pallas_call(kernel, out_shape=outs, in_specs=specs, out_specs=[pl.Bloc...  6.39 us
    unnamed x11, local copies, waits for them, and re-layouts  4.46 us
  transfers between devices with their start and end apart: 15, of which 7 were waited for; matrix products, arithmetic and copies ran while one was open for 0% of the time, Pallas kernels for 1%

profile of v1, /device:TPU:0, one launch (start us, length us, event | category | flops | bytes accessed | tf_op | source)
XLA Modules:
  0.0 81.3 jit_solution(11530415639129754498)
XLA Ops:
  0.0 0.0 copy-start.1
  0.0 1.0 %copy-done.1 = bf16[4,32,1280]{2,1,0:T(8,128)(2,1)S(1)} copy-done((bf16[4,32,1280]{2,1,0:T(8,128)(2,1)S(1)}, bf16[4,32,1280]{2,1,0:T(8,128)(2,1)}, u32[]{:S(2)}) %copy-start.1) | copy-done | bytes 327704
  1.0 0.0 copy-start.2
  1.0 1.0 %copy-done.2 = bf16[4,32,1280]{2,1,0:T(8,128)(2,1)S(1)} copy-done((bf16[4,32,1280]{2,1,0:T(8,128)(2,1)S(1)}, bf16[4,32,1280]{2,1,0:T(8,128)(2,1)}, u32[]{:S(2)}) %copy-start.2) | copy-done | bytes 327704
  1.9 0.0 copy-start.3
  1.9 1.0 %copy-done.3 = bf16[4,32,1280]{2,1,0:T(8,128)(2,1)S(1)} copy-done((bf16[4,32,1280]{2,1,0:T(8,128)(2,1)S(1)}, bf16[4,32,1280]{2,1,0:T(8,128)(2,1)}, u32[]{:S(2)}) %copy-start.3) | copy-done | bytes 327704
  2.9 0.0 copy-start.4
  2.9 0.9 %pack.1 = (bf16[34,32,128]{2,1,0:T(8,128)(2,1)S(1)}, bf16[34,32,128]{2,1,0:T(8,128)(2,1)S(1)}, bf16[34,32,128]{2,1,0:T(8,128)(2,1)}, bf16[34,32,128]{2,1,0:T(8,128)(2,1)S(1)}) custom-call(bf16[4,32,1280]{2,1,0:T(8,128)(2,1)S(1)} %copy-done.1, bf16[4,32,1280]{2,1,0:T(8,128)(2,1)S(1)} %copy-done.2, bf16[4,32,1280]{2,1,0:T(8,128)(2,1)S(1)} %copy-done.3), custom_call_target="tpu_custom_call" | custom-call | tf_op jit(solution)/shard_map/pack/pallas_call | solution.py:320
  3.9 3.1 %collective-permute-start = (bf16[34,32,128]{2,1,0:T(8,128)(2,1)S(1)}, bf16[34,32,128]{2,1,0:T(8,128)(2,1)S(1)}, u32[]{:S(2)}, u32[]{:S(2)}) collective-permute-start(bf16[34,32,128]{2,1,0:T(8,128)(2,1)S(1)} %get-tuple-element.30), channel_id=1, source_target_pairs={{0,4},{4,0},{8,12},{12,8},{1,5},{5,1},{9,13},{13,9},{2,6},{6,2},{1... | collective-permute-start | bytes 835592 | tf_op jit(solution)/shard_map/ppermute | solution.py:145
  6.9 0.0 copy-start
  6.9 1.4 %copy-done = bf16[10,32,2560]{2,1,0:T(8,128)(2,1)S(1)} copy-done((bf16[10,32,2560]{2,1,0:T(8,128)(2,1)S(1)}, bf16[10,32,2560]{2,1,0:T(8,128)(2,1)}, u32[]{:S(2)}) %copy-start) | copy-done | bytes 1638424
  8.3 1.0 %weight_slices.1 = (bf16[10,32,640]{2,1,0:T(8,128)(2,1)S(1)}, bf16[10,32,640]{2,1,0:T(8,128)(2,1)}, bf16[10,32,640]{2,1,0:T(8,128)(2,1)}, bf16[10,32,640]{2,1,0:T(8,128)(2,1)S(1)}) custom-call(bf16[10,32,2560]{2,1,0:T(8,128)(2,1)S(1)} %copy-done), custom_call_target="tpu_custom_call" | custom-call | tf_op jit(solution)/shard_map/weight_slices/pallas_call | solution.py:320
  9.4 0.0 collective-permute-start.3
  9.4 1.5 %collective-permute-start.4 = (bf16[10,32,640]{2,1,0:T(8,128)(2,1)}, bf16[10,32,640]{2,1,0:T(8,128)(2,1)S(1)}, u32[]{:S(2)}, u32[]{:S(2)}) collective-permute-start(bf16[10,32,640]{2,1,0:T(8,128)(2,1)} %get-tuple-element.35), channel_id=1, source_target_pairs={{0,2},{1,3},{2,0},{3,1},{4,6},{5,7},{6,4},{7,5},{8,10},{9,11},{10,... | collective-permute-start | bytes 1228808 | tf_op jit(solution)/shard_map/ppermute | solution.py:145
  10.8 0.4 collective-permute-start.5
  11.2 2.6 %collective-permute-start.1 = (bf16[34,32,128]{2,1,0:T(8,128)(2,1)}, bf16[34,32,128]{2,1,0:T(8,128)(2,1)S(1)}, u32[]{:S(2)}, u32[]{:S(2)}) collective-permute-start(bf16[34,32,128]{2,1,0:T(8,128)(2,1)} %get-tuple-element.31), channel_id=1, source_target_pairs={{0,8},{4,12},{8,0},{12,4},{1,9},{5,13},{9,1},{13,5},{2,10},{6,14},... | collective-permute-start | bytes 835592 | tf_op jit(solution)/shard_map/ppermute | solution.py:145
  13.8 0.0 collective-permute-done.refs_1_
  13.8 3.5 %collective-permute-start.2 = (bf16[34,32,128]{2,1,0:T(8,128)(2,1)S(1)}, bf16[34,32,128]{2,1,0:T(8,128)(2,1)S(1)}, u32[]{:S(2)}, u32[]{:S(2)}) collective-permute-start(bf16[34,32,128]{2,1,0:T(8,128)(2,1)S(1)} %get-tuple-element.32), channel_id=1, source_target_pairs={{0,12},{4,8},{8,4},{12,0},{1,13},{5,9},{9,5},{13,1},{2,14},{6,10},... | collective-permute-start | bytes 835592 | tf_op jit(solution)/shard_map/ppermute | solution.py:145
  17.3 0.0 copy-done.4
  17.3 0.1 copy.6.mask_ref
  17.4 15.9 %collective-permute-done.1.refs_2_ = bf16[34,32,128]{2,1,0:T(8,128)(2,1)S(1)} collective-permute-done((bf16[34,32,128]{2,1,0:T(8,128)(2,1)}, bf16[34,32,128]{2,1,0:T(8,128)(2,1)S(1)}, u32[]{:S(2)}, u32[]{:S(2)}) %collective-permute-start.1) | collective-permute-done | bytes 278560 | tf_op jit(solution)/shard_map/ppermute | solution.py:145
  33.4 0.0 collective-permute-done.2.refs_3_
  33.4 0.0 collective-permute-done.3.refs_5_
  33.4 0.0 collective-permute-done.4.refs_6_
  33.4 0.0 collective-permute-done.5.refs_7_
  33.4 2.5 %attend.1 = (bf16[32,1280]{1,0:T(8,128)(2,1)S(1)}, bf16[32,1280]{1,0:T(8,128)(2,1)S(1)}, bf16[32,1280]{1,0:T(8,128)(2,1)S(1)}, bf16[32,1280]{1,0:T(8,128)(2,1)S(1)}) custom-call(s32[10,4,4]{2,1,0:T(4,128)S(1)} %copy.6.mask_ref, bf16[34,32,128]{2,1,0:T(8,128)(2,1)S(1)} %get-tuple-element.37.refs_0_, bf16[34,32,128]{2,1,0:T(8,128)(2,1)S(1)} %collective-permute-done.refs_1_, ...), custom_call_target="tpu_custom_call" | custom-call | tf_op jit(solution)/shard_map/attend/pallas_call | solution.py:320
  35.9 6.2 %collective-permute-start.6 = (bf16[32,1280]{1,0:T(8,128)(2,1)S(1)}, bf16[32,1280]{1,0:T(8,128)(2,1)S(1)}, u32[]{:S(2)}, u32[]{:S(2)}) collective-permute-start(bf16[32,1280]{1,0:T(8,128)(2,1)S(1)} %get-tuple-element.42), channel_id=1, source_target_pairs={{0,4},{4,0},{8,12},{12,8},{1,5},{5,1},{9,13},{13,9},{2,6},{6,2},{1... | collective-permute-start | bytes 245768 | tf_op jit(solution)/shard_map/ppermute | solution.py:145
  42.2 1.2 %collective-permute-start.7 = (bf16[32,1280]{1,0:T(8,128)(2,1)S(1)}, bf16[32,1280]{1,0:T(8,128)(2,1)S(1)}, u32[]{:S(2)}, u32[]{:S(2)}) collective-permute-start(bf16[32,1280]{1,0:T(8,128)(2,1)S(1)} %get-tuple-element.43), channel_id=1, source_target_pairs={{0,8},{4,12},{8,0},{12,4},{1,9},{5,13},{9,1},{13,5},{2,10},{6,14},... | collective-permute-start | bytes 245768 | tf_op jit(solution)/shard_map/ppermute | solution.py:145
  43.4 1.4 %collective-permute-start.8 = (bf16[32,1280]{1,0:T(8,128)(2,1)S(1)}, bf16[32,1280]{1,0:T(8,128)(2,1)S(1)}, u32[]{:S(2)}, u32[]{:S(2)}) collective-permute-start(bf16[32,1280]{1,0:T(8,128)(2,1)S(1)} %get-tuple-element.44), channel_id=1, source_target_pairs={{0,12},{4,8},{8,4},{12,0},{1,13},{5,9},{9,5},{13,1},{2,14},{6,10},... | collective-permute-start | bytes 245768 | tf_op jit(solution)/shard_map/ppermute | solution.py:145
  44.7 0.3 collective-permute-done.6.refs_1_
  45.0 6.0 %collective-permute-done.7.refs_2_ = bf16[32,1280]{1,0:T(8,128)(2,1)S(1)} collective-permute-done((bf16[32,1280]{1,0:T(8,128)(2,1)S(1)}, bf16[32,1280]{1,0:T(8,128)(2,1)S(1)}, u32[]{:S(2)}, u32[]{:S(2)}) %collective-permute-start.7) | collective-permute-done | bytes 81952 | tf_op jit(solution)/shard_map/ppermute | solution.py:145
  51.1 0.0 collective-permute-done.8.refs_3_
  51.1 1.6 %collective-permute-start.10 = (bf16[4,32,1280]{2,1,0:T(8,128)(2,1)S(1)}, bf16[4,32,1280]{2,1,0:T(8,128)(2,1)S(1)}, u32[]{:S(2)}, u32[]{:S(2)}) collective-permute-start(bf16[4,32,1280]{2,1,0:T(8,128)(2,1)S(1)} %join.1.refs_0_), channel_id=1, source_target_pairs={{0,2},{1,3},{2,0},{3,1},{4,6},{5,7},{6,4},{7,5},{8,10},{9,11},{10,... | collective-permute-start | bytes 983048 | tf_op jit(solution)/shard_map/ppermute | solution.py:145
  52.7 0.0 collective-permute-start.9
  52.7 5.6 %collective-permute-done.10.refs_2_ = bf16[4,32,1280]{2,1,0:T(8,128)(2,1)S(1)} collective-permute-done((bf16[4,32,1280]{2,1,0:T(8,128)(2,1)S(1)}, bf16[4,32,1280]{2,1,0:T(8,128)(2,1)S(1)}, u32[]{:S(2)}, u32[]{:S(2)}) %collective-permute-start.10) | collective-permute-done | bytes 327712 | tf_op jit(solution)/shard_map/ppermute | solution.py:145
  58.2 0.0 collective-permute-start.11
  58.2 0.0 collective-permute-done.9.refs_1_
  58.2 1.6 %collective-permute-done.11.refs_3_ = bf16[4,32,1280]{2,1,0:T(8,128)(2,1)S(1)} collective-permute-done((bf16[4,32,1280]{2,1,0:T(8,128)(2,1)S(1)}, bf16[4,32,1280]{2,1,0:T(8,128)(2,1)S(1)}, u32[]{:S(2)}, u32[]{:S(2)}) %collective-permute-start.11) | collective-permute-done | bytes 327712 | tf_op jit(solution)/shard_map/ppermute | solution.py:145
  59.9 1.9 %project.1 = (f32[4,32,640]{2,1,0:T(8,128)S(1)}, bf16[4,32,640]{2,1,0:T(8,128)(2,1)S(1)}, bf16[4,32,640]{2,1,0:T(8,128)(2,1)S(1)}, bf16[4,32,640]{2,1,0:T(8,128)(2,1)S(1)}) custom-call(bf16[4,32,1280]{2,1,0:T(8,128)(2,1)S(1)} %join.1.refs_0_, bf16[4,32,1280]{2,1,0:T(8,128)(2,1)S(1)} %collective-permute-done.9.refs_1_, ...), custom_call_target="tpu_custom_call" | custom-call | tf_op jit(solution)/shard_map/project/pallas_call | solution.py:320
  61.7 3.8 %collective-permute-start.12 = (bf16[4,32,640]{2,1,0:T(8,128)(2,1)S(1)}, bf16[4,32,640]{2,1,0:T(8,128)(2,1)S(1)}, u32[]{:S(2)}, u32[]{:S(2)}) collective-permute-start(bf16[4,32,640]{2,1,0:T(8,128)(2,1)S(1)} %get-tuple-element.50), channel_id=1, source_target_pairs={{0,4},{4,0},{8,12},{12,8},{1,5},{5,1},{9,13},{13,9},{2,6},{6,2},{1... | collective-permute-start | bytes 491528 | tf_op jit(solution)/shard_map/ppermute | solution.py:145
  65.5 0.5 collective-permute-start.13
  66.0 2.0 %collective-permute-start.14 = (bf16[4,32,640]{2,1,0:T(8,128)(2,1)S(1)}, bf16[4,32,640]{2,1,0:T(8,128)(2,1)S(1)}, u32[]{:S(2)}, u32[]{:S(2)}) collective-permute-start(bf16[4,32,640]{2,1,0:T(8,128)(2,1)S(1)} %get-tuple-element.52), channel_id=1, source_target_pairs={{0,12},{4,8},{8,4},{12,0},{1,13},{5,9},{9,5},{13,1},{2,14},{6,10},... | collective-permute-start | bytes 491528 | tf_op jit(solution)/shard_map/ppermute | solution.py:145
  68.0 4.7 %collective-permute-done.12 = bf16[4,32,640]{2,1,0:T(8,128)(2,1)S(1)} collective-permute-done((bf16[4,32,640]{2,1,0:T(8,128)(2,1)S(1)}, bf16[4,32,640]{2,1,0:T(8,128)(2,1)S(1)}, u32[]{:S(2)}, u32[]{:S(2)}) %collective-permute-start.12) | collective-permute-done | bytes 163872 | tf_op jit(solution)/shard_map/ppermute | solution.py:145
  72.6 7.9 %collective-permute-done.13 = bf16[4,32,640]{2,1,0:T(8,128)(2,1)S(1)} collective-permute-done((bf16[4,32,640]{2,1,0:T(8,128)(2,1)S(1)}, bf16[4,32,640]{2,1,0:T(8,128)(2,1)S(1)}, u32[]{:S(2)}, u32[]{:S(2)}) %collective-permute-start.13) | collective-permute-done | bytes 163872 | tf_op jit(solution)/shard_map/ppermute | solution.py:145
  80.5 0.0 collective-permute-done.14
  80.5 0.7 add_convert_fusion
  (1 shorter events, 0.0 us)
Async XLA Ops:
  0.0 1.0 %copy-start.1 = (bf16[4,32,1280]{2,1,0:T(8,128)(2,1)S(1)}, bf16[4,32,1280]{2,1,0:T(8,128)(2,1)}, u32[]{:S(2)}) copy-start(bf16[4,32,1280]{2,1,0:T(8,128)(2,1)} %q_ref.1) | copy-start | bytes 983044
  1.0 1.0 %copy-start.2 = (bf16[4,32,1280]{2,1,0:T(8,128)(2,1)S(1)}, bf16[4,32,1280]{2,1,0:T(8,128)(2,1)}, u32[]{:S(2)}) copy-start(bf16[4,32,1280]{2,1,0:T(8,128)(2,1)} %k_ref.1) | copy-start | bytes 983044
  1.9 1.0 %copy-start.3 = (bf16[4,32,1280]{2,1,0:T(8,128)(2,1)S(1)}, bf16[4,32,1280]{2,1,0:T(8,128)(2,1)}, u32[]{:S(2)}) copy-start(bf16[4,32,1280]{2,1,0:T(8,128)(2,1)} %v_ref.1) | copy-start | bytes 983044
  2.9 14.4 %copy-start.4 = (s32[10,4,4]{0,2,1:T(4,128)S(1)}, s32[10,4,4]{0,2,1:T(4,128)}, u32[]{:S(2)}) copy-start(s32[10,4,4]{0,2,1:T(4,128)} %param.8) | copy-start | bytes 1924
  3.9 10.0 %collective-permute-start = (bf16[34,32,128]{2,1,0:T(8,128)(2,1)S(1)}, bf16[34,32,128]{2,1,0:T(8,128)(2,1)S(1)}, u32[]{:S(2)}, u32[]{:S(2)}) collective-permute-start(bf16[34,32,128]{2,1,0:T(8,128)(2,1)S(1)} %get-tuple-element.30), channel_id=1, source_target_pairs={{0,4},{4,0},{8,12},{12,8},{1,5},{5,1},{9,13},{13,9},{2,6},{6,2},{1... | collective-permute-start | bytes 835592 | tf_op jit(solution)/shard_map/ppermute | solution.py:145
  6.9 1.4 %copy-start = (bf16[10,32,2560]{2,1,0:T(8,128)(2,1)S(1)}, bf16[10,32,2560]{2,1,0:T(8,128)(2,1)}, u32[]{:S(2)}) copy-start(bf16[10,32,2560]{2,1,0:T(8,128)(2,1)} %w_ref.1) | copy-start | bytes 4915204
  9.4 24.0 %collective-permute-start.3 = (bf16[10,32,640]{2,1,0:T(8,128)(2,1)}, bf16[10,32,640]{2,1,0:T(8,128)(2,1)S(1)}, u32[]{:S(2)}, u32[]{:S(2)}) collective-permute-start(bf16[10,32,640]{2,1,0:T(8,128)(2,1)} %get-tuple-element.34), channel_id=1, source_target_pairs={{0,1},{1,0},{2,3},{3,2},{4,5},{5,4},{6,7},{7,6},{8,9},{9,8},{10,11... | collective-permute-start | bytes 1228808 | tf_op jit(solution)/shard_map/ppermute | solution.py:145
  9.4 24.0 %collective-permute-start.4 = (bf16[10,32,640]{2,1,0:T(8,128)(2,1)}, bf16[10,32,640]{2,1,0:T(8,128)(2,1)S(1)}, u32[]{:S(2)}, u32[]{:S(2)}) collective-permute-start(bf16[10,32,640]{2,1,0:T(8,128)(2,1)} %get-tuple-element.35), channel_id=1, source_target_pairs={{0,2},{1,3},{2,0},{3,1},{4,6},{5,7},{6,4},{7,5},{8,10},{9,11},{10,... | collective-permute-start | bytes 1228808 | tf_op jit(solution)/shard_map/ppermute | solution.py:145
  10.8 22.5 %collective-permute-start.5 = (bf16[10,32,640]{2,1,0:T(8,128)(2,1)S(1)}, bf16[10,32,640]{2,1,0:T(8,128)(2,1)S(1)}, u32[]{:S(2)}, u32[]{:S(2)}) collective-permute-start(bf16[10,32,640]{2,1,0:T(8,128)(2,1)S(1)} %get-tuple-element.36), channel_id=1, source_target_pairs={{0,3},{1,2},{2,1},{3,0},{4,7},{5,6},{6,5},{7,4},{8,11},{9,10},{10,... | collective-permute-start | bytes 1228808 | tf_op jit(solution)/shard_map/ppermute | solution.py:145
  11.2 22.2 %collective-permute-start.1 = (bf16[34,32,128]{2,1,0:T(8,128)(2,1)}, bf16[34,32,128]{2,1,0:T(8,128)(2,1)S(1)}, u32[]{:S(2)}, u32[]{:S(2)}) collective-permute-start(bf16[34,32,128]{2,1,0:T(8,128)(2,1)} %get-tuple-element.31), channel_id=1, source_target_pairs={{0,8},{4,12},{8,0},{12,4},{1,9},{5,13},{9,1},{13,5},{2,10},{6,14},... | collective-permute-start | bytes 835592 | tf_op jit(solution)/shard_map/ppermute | solution.py:145
  13.8 19.6 %collective-permute-start.2 = (bf16[34,32,128]{2,1,0:T(8,128)(2,1)S(1)}, bf16[34,32,128]{2,1,0:T(8,128)(2,1)S(1)}, u32[]{:S(2)}, u32[]{:S(2)}) collective-permute-start(bf16[34,32,128]{2,1,0:T(8,128)(2,1)S(1)} %get-tuple-element.32), channel_id=1, source_target_pairs={{0,12},{4,8},{8,4},{12,0},{1,13},{5,9},{9,5},{13,1},{2,14},{6,10},... | collective-permute-start | bytes 835592 | tf_op jit(solution)/shard_map/ppermute | solution.py:145
  35.9 9.1 %collective-permute-start.6 = (bf16[32,1280]{1,0:T(8,128)(2,1)S(1)}, bf16[32,1280]{1,0:T(8,128)(2,1)S(1)}, u32[]{:S(2)}, u32[]{:S(2)}) collective-permute-start(bf16[32,1280]{1,0:T(8,128)(2,1)S(1)} %get-tuple-element.42), channel_id=1, source_target_pairs={{0,4},{4,0},{8,12},{12,8},{1,5},{5,1},{9,13},{13,9},{2,6},{6,2},{1... | collective-permute-start | bytes 245768 | tf_op jit(solution)/shard_map/ppermute | solution.py:145
  42.2 8.9 %collective-permute-start.7 = (bf16[32,1280]{1,0:T(8,128)(2,1)S(1)}, bf16[32,1280]{1,0:T(8,128)(2,1)S(1)}, u32[]{:S(2)}, u32[]{:S(2)}) collective-permute-start(bf16[32,1280]{1,0:T(8,128)(2,1)S(1)} %get-tuple-element.43), channel_id=1, source_target_pairs={{0,8},{4,12},{8,0},{12,4},{1,9},{5,13},{9,1},{13,5},{2,10},{6,14},... | collective-permute-start | bytes 245768 | tf_op jit(solution)/shard_map/ppermute | solution.py:145
  43.4 7.7 %collective-permute-start.8 = (bf16[32,1280]{1,0:T(8,128)(2,1)S(1)}, bf16[32,1280]{1,0:T(8,128)(2,1)S(1)}, u32[]{:S(2)}, u32[]{:S(2)}) collective-permute-start(bf16[32,1280]{1,0:T(8,128)(2,1)S(1)} %get-tuple-element.44), channel_id=1, source_target_pairs={{0,12},{4,8},{8,4},{12,0},{1,13},{5,9},{9,5},{13,1},{2,14},{6,10},... | collective-permute-start | bytes 245768 | tf_op jit(solution)/shard_map/ppermute | solution.py:145
  51.1 7.1 %collective-permute-start.10 = (bf16[4,32,1280]{2,1,0:T(8,128)(2,1)S(1)}, bf16[4,32,1280]{2,1,0:T(8,128)(2,1)S(1)}, u32[]{:S(2)}, u32[]{:S(2)}) collective-permute-start(bf16[4,32,1280]{2,1,0:T(8,128)(2,1)S(1)} %join.1.refs_0_), channel_id=1, source_target_pairs={{0,2},{1,3},{2,0},{3,1},{4,6},{5,7},{6,4},{7,5},{8,10},{9,11},{10,... | collective-permute-start | bytes 983048 | tf_op jit(solution)/shard_map/ppermute | solution.py:145
  52.7 5.6 %collective-permute-start.9 = (bf16[4,32,1280]{2,1,0:T(8,128)(2,1)S(1)}, bf16[4,32,1280]{2,1,0:T(8,128)(2,1)S(1)}, u32[]{:S(2)}, u32[]{:S(2)}) collective-permute-start(bf16[4,32,1280]{2,1,0:T(8,128)(2,1)S(1)} %join.1.refs_0_), channel_id=1, source_target_pairs={{0,1},{1,0},{2,3},{3,2},{4,5},{5,4},{6,7},{7,6},{8,9},{9,8},{10,11... | collective-permute-start | bytes 983048 | tf_op jit(solution)/shard_map/ppermute | solution.py:145
  58.2 1.6 %collective-permute-start.11 = (bf16[4,32,1280]{2,1,0:T(8,128)(2,1)S(1)}, bf16[4,32,1280]{2,1,0:T(8,128)(2,1)S(1)}, u32[]{:S(2)}, u32[]{:S(2)}) collective-permute-start(bf16[4,32,1280]{2,1,0:T(8,128)(2,1)S(1)} %collective-permute-done.10.refs_2_), channel_id=1, source_target_pairs={{0,1},{1,0},{2,3},{3,2},{4,5},{5,4},{6,7},{7,6},{8,9},{9,8},{10,11... | collective-permute-start | bytes 983048 | tf_op jit(solution)/shard_map/ppermute | solution.py:145
  61.7 10.9 %collective-permute-start.12 = (bf16[4,32,640]{2,1,0:T(8,128)(2,1)S(1)}, bf16[4,32,640]{2,1,0:T(8,128)(2,1)S(1)}, u32[]{:S(2)}, u32[]{:S(2)}) collective-permute-start(bf16[4,32,640]{2,1,0:T(8,128)(2,1)S(1)} %get-tuple-element.50), channel_id=1, source_target_pairs={{0,4},{4,0},{8,12},{12,8},{1,5},{5,1},{9,13},{13,9},{2,6},{6,2},{1... | collective-permute-start | bytes 491528 | tf_op jit(solution)/shard_map/ppermute | solution.py:145
  65.5 15.0 %collective-permute-start.13 = (bf16[4,32,640]{2,1,0:T(8,128)(2,1)S(1)}, bf16[4,32,640]{2,1,0:T(8,128)(2,1)S(1)}, u32[]{:S(2)}, u32[]{:S(2)}) collective-permute-start(bf16[4,32,640]{2,1,0:T(8,128)(2,1)S(1)} %get-tuple-element.51), channel_id=1, source_target_pairs={{0,8},{4,12},{8,0},{12,4},{1,9},{5,13},{9,1},{13,5},{2,10},{6,14},... | collective-permute-start | bytes 491528 | tf_op jit(solution)/shard_map/ppermute | solution.py:145
  66.0 14.5 %collective-permute-start.14 = (bf16[4,32,640]{2,1,0:T(8,128)(2,1)S(1)}, bf16[4,32,640]{2,1,0:T(8,128)(2,1)S(1)}, u32[]{:S(2)}, u32[]{:S(2)}) collective-permute-start(bf16[4,32,640]{2,1,0:T(8,128)(2,1)S(1)} %get-tuple-element.52), channel_id=1, source_target_pairs={{0,12},{4,8},{8,4},{12,0},{1,13},{5,9},{9,5},{13,1},{2,14},{6,10},... | collective-permute-start | bytes 491528 | tf_op jit(solution)/shard_map/ppermute | solution.py:145

commit v2 on v1

--- a/solution.py
+++ b/solution.py
@@ -7,6 +7,7 @@
 from jax.experimental import pallas as pl
 from jax.experimental.pallas import tpu as pltpu
 from jax.sharding import PartitionSpec as P
+
 
 KEYS = 28
 
@@ -185,35 +186,52 @@
         return summed < gathered
 
 
-def pack_kernel(z, q_ref, k_ref, v_ref, *out_refs):
+def pack_kernel(z, q_hbm, k_hbm, v_hbm, *refs):
+    out_refs = refs[: z.ranks]
+    q_ref, k_ref, v_ref, sems = refs[z.ranks :]
     me = lax.axis_index("seq")
-    for flip in range(z.ranks):
-        peer = me ^ flip
-        out = out_refs[flip]
-        for slot in range(z.whole):
-            cols = pl.ds(aligned(slot * z.ranks + peer, z.hd), z.hd)
-            at = slot * z.blocks
-            out[at : at + z.blocks] = q_ref[:, :, cols]
-            at += z.q_units
-            out[at : at + z.blocks] = k_ref[:, :, cols]
-            at += z.kv_units
-            out[at : at + z.blocks] = v_ref[:, :, cols]
-        if z.rest:
-            head = z.whole * z.ranks + peer // z.sharers
-            cols = pl.ds(aligned(head, z.hd), z.hd)
-            first = (peer % z.sharers) * z.strip
-            at = z.whole * z.blocks
-            out[at : at + z.strip] = q_ref[pl.ds(first, z.strip), :, cols]
-            at += z.q_units
-            out[at : at + z.blocks] = k_ref[:, :, cols]
-            at += z.kv_units
-            out[at : at + z.blocks] = v_ref[:, :, cols]
-
-
-def weight_kernel(z, w_ref, *out_refs):
+    copies = [
+        pltpu.make_async_copy(source, target, sems.at[i])
+        for i, (source, target) in enumerate(
+            ((q_hbm, q_ref), (k_hbm, k_ref), (v_hbm, v_ref))
+        )
+    ]
+    for copy in copies:
+        copy.start()
+    for copy, ref, begin, strip in (
+        (copies[0], q_ref, 0, z.strip),
+        (copies[1], k_ref, z.q_units, z.blocks),
+        (copies[2], v_ref, z.q_units + z.kv_units, z.blocks),
+    ):
+        copy.wait()
+        for flip in range(z.ranks):
+            peer = me ^ flip
+            for slot in range(z.whole):
+                cols = pl.ds(aligned(slot * z.ranks + peer, z.hd), z.hd)
+                at = begin + slot * z.blocks
+                out_refs[flip][at : at + z.blocks] = ref[:, :, cols]
+            if z.rest:
+                cols = pl.ds(aligned(z.whole * z.ranks + peer // z.sharers, z.hd), z.hd)
+                first = (peer % z.sharers) * z.strip if strip < z.blocks else 0
+                at = begin + z.whole * z.blocks
+                out_refs[flip][at : at + strip] = ref[pl.ds(first, strip), :, cols]
+
+
+def weight_kernel(z, w_hbm, *refs):
+    out_refs, sems = refs[: z.tps], refs[z.tps]
     me = lax.axis_index("tp")
-    for flip in range(z.tps):
-        out_refs[flip][...] = w_ref[:, :, pl.ds(aligned(me ^ flip, z.cols), z.cols)]
+    copies = [
+        pltpu.make_async_copy(
+            w_hbm.at[:, :, pl.ds(aligned(me ^ flip, z.cols), z.cols)],
+            out_refs[flip],
+            sems.at[flip],
+        )
+        for flip in range(z.tps)
+    ]
+    for copy in copies:
+        copy.start()
+    for copy in copies:
+        copy.wait()
 
 
 def attend_kernel(z, mask_ref, *refs):
@@ -311,66 +329,77 @@
             out_refs[flip - 1][b] = total[b, me ^ flip].astype(jnp.bfloat16)
 
 
-def local_call(kernel, outs, scratch=(), smem=0, name=None, limit=16):
+def local_call(kernel, outs, scratch=(), places=None, limit=16):
     def call(*args):
-        specs = [
-            pl.BlockSpec(memory_space=pltpu.SMEM if i < smem else pltpu.VMEM)
-            for i in range(len(args))
+        spaces = places or [pltpu.VMEM] * len(args)
+        args = [
+            pltpu.with_memory_space_constraint(arg, space) if space is pltpu.HBM else arg
+            for arg, space in zip(args, spaces)
         ]
         return pl.pallas_call(
             kernel,
             out_shape=outs,
-            in_specs=specs,
+            in_specs=[pl.BlockSpec(memory_space=space) for space in spaces],
             out_specs=[pl.BlockSpec(memory_space=pltpu.VMEM)] * len(outs),
             scratch_shapes=list(scratch),
             compiler_params=pltpu.CompilerParams(vmem_limit_bytes=limit << 20),
-            name=name,
         )(*args)
 
     return call
+
+
+def exchange_all(arrays, axis):
+    got = [arrays[0]]
+    for flip in range(1, len(arrays)):
+        got.append(exchange(arrays[flip], axis, flip))
+    return got
 
 
 def stationary_plan(z, queries, key_vectors, value_vectors, block_mask, out_weight):
     bf16 = jnp.bfloat16
     shape = jax.ShapeDtypeStruct
+    held = pltpu.VMEM(queries.shape, bf16)
     packed = local_call(
         functools.partial(pack_kernel, z),
         [shape((z.units, z.rows, z.hd), bf16)] * z.ranks,
-        name="pack",
+        scratch=[held, held, held, pltpu.SemaphoreType.DMA((3,))],
+        places=[pltpu.HBM] * 3,
     )(queries, key_vectors, value_vectors)
-    parts = [packed[0]] + [exchange(packed[f], "seq", f) for f in range(1, z.ranks)]
+    parts = exchange_all(packed, "seq")
     sliced = local_call(
         functools.partial(weight_kernel, z),
         [shape((z.heads, z.part, z.cols), bf16)] * z.tps,
-        name="weight_slices",
+        scratch=[pltpu.SemaphoreType.DMA((z.tps,))],
+        places=[pltpu.HBM],
     )(out_weight)
-    weights = [sliced[0]] + [exchange(sliced[f], "tp", f) for f in range(1, z.tps)]
+    weights = exchange_all(sliced, "tp")
     parts, weights = lax.optimization_barrier((parts, weights))
+    slot_rows = pltpu.VMEM((z.slots, z.tokens, z.hd), bf16)
     strips = local_call(
         functools.partial(attend_kernel, z),
         [shape((z.part, z.out_tokens), bf16)] * z.ranks,
-        scratch=[
-            pltpu.VMEM((z.slots, z.tokens, z.hd), bf16),
-            pltpu.VMEM((z.slots, z.tokens, z.hd), bf16),
-            pltpu.VMEM((z.slots, z.tokens, z.hd), bf16),
-            pltpu.VMEM((z.tokens, z.tokens), bf16),
-            pltpu.VMEM((z.hd, z.out_tokens), bf16),
-        ],
-        smem=1,
-        name="attend",
+        scratch=[slot_rows, slot_rows, slot_rows]
+        + [pltpu.VMEM((z.tokens, z.tokens), bf16), pltpu.VMEM((z.hd, z.out_tokens), bf16)],
+        places=[pltpu.SMEM] + [pltpu.VMEM] * z.ranks,
     )(block_mask, *parts)
-    strips = [strips[0]] + [exchange(strips[f], "seq", f) for f in range(1, z.ranks)]
-    joined = local_call(
-        functools.partial(join_kernel, z),
-        [shape((z.ranks, z.part, z.out_tokens), bf16)],
-        name="join",
-    )(*strips)[0]
-    tokens = [joined]
+    pieces = exchange_all(strips, "seq")
+
+    def join(arrays):
+        return local_call(
+            functools.partial(join_kernel, z), [shape((z.ranks, z.part, z.out_tokens), bf16)]
+        )(*arrays)[0]
+
+    tokens = {0: join(pieces)}
     flip = z.tps // 2
-    tokens = {0: joined}
+    if flip:
+        far = []
+        for piece in pieces:
+            far.append(exchange(piece, "tp", flip))
+        tokens[flip] = join(far)
+        flip //= 2
     while flip:
-        for held in list(tokens):
-            tokens[held ^ flip] = exchange(tokens[held], "tp", flip)
+        for has in list(tokens):
+            tokens[has ^ flip] = exchange(tokens[has], "tp", flip)
         flip //= 2
     sums = local_call(
         functools.partial(project_kernel, z),
@@ -380,11 +409,11 @@
             pltpu.VMEM((z.tps, z.heads * z.part, z.tokens), bf16),
             pltpu.VMEM((z.blocks, z.ranks, z.rows, z.cols), jnp.float32),
         ],
-        name="project",
     )(*[tokens[t] for t in range(z.tps)], *weights)
-    total = sums[0]
-    for f in range(1, z.ranks):
-        total = total + exchange(sums[f], "seq", f).astype(jnp.float32)
+    got = exchange_all(sums, "seq")
+    total = got[0]
+    for term in got[1:]:
+        total = total + term.astype(jnp.float32)
     return total.astype(bf16)
 
 
@@ -396,8 +425,9 @@
         block_mask.shape[0],
         out_weight.shape,
     )
-    plan = functools.partial(stationary_plan, z) if z.fits() else gathered_plan
-    return plan(queries, key_vectors, value_vectors, block_mask, out_weight)
+    if not z.fits():
+        return gathered_plan(queries, key_vectors, value_vectors, block_mask, out_weight)
+    return stationary_plan(z, queries, key_vectors, value_vectors, block_mask, out_weight)
 
 
 def solution(mesh):

time: 81.5 us -> 75.2 us (0.923)
  waiting for transfers between devices: 42 us -> 36.5 us
  local copies, waits for them, and re-layouts: 4.46 us -> 0.12 us
  Pallas kernels: 6.39 us -> 8.76 us
  starting transfers between devices: 27.6 us -> 28.7 us
    ppermute x15 -> x18, waiting for transfers between devices: 42 us -> 36.5 us  [exchange(): return lax.ppermute(array, axis, [(i, i ^ flip) for i in range(size)])]
    unnamed x11 -> x3, local copies, waits for them, and re-layouts: 4.46 us -> 0.12 us
    pallas_call x5 -> x6, Pallas kernels: 6.39 us -> 8.76 us  [call(): pl.pallas_call(kernel, out_shape=outs, in_specs=[pl.BlockSpec(memory_spac...]
    ppermute x15 -> x18, starting transfers between devices: 27.6 us -> 28.7 us  [exchange(): return lax.ppermute(array, axis, [(i, i ^ flip) for i in range(size)])]
  transfers between devices with their start and end apart: 15 -> 18, of which waited for: 7 -> 7; matrix products, arithmetic and copies ran while one was open for 0% -> 0% of each run, Pallas kernels for 1% -> 3%
where the time goes in v2:
time: 75.2 us; the launch traced here: 74.9 us
  waiting for transfers between devices  36.5 us (49%)
  starting transfers between devices  28.7 us (38%)
  Pallas kernels  8.76 us (12%)
    ppermute x18, waiting for transfers between devices, exchange(): return lax.ppermute(array, axis, [(i, i ^ flip) for i in range(size)])  36.5 us
    ppermute x18, starting transfers between devices, exchange(): return lax.ppermute(array, axis, [(i, i ^ flip) for i in range(size)])  28.7 us
    pallas_call x6, Pallas kernels, call(): pl.pallas_call(kernel, out_shape=outs, in_specs=[pl.BlockSpec(memory_spac...  8.76 us
  transfers between devices with their start and end apart: 18, of which 7 were waited for; matrix products, arithmetic and copies ran while one was open for 0% of the time, Pallas kernels for 3%

profile of v2, /device:TPU:0, one launch (start us, length us, event | category | flops | bytes accessed | tf_op | source)
XLA Modules:
  0.0 74.9 jit_solution(3103939673103439959)
XLA Ops:
  0.0 0.0 copy-start
  0.0 2.0 %shard_map.55 = (bf16[34,32,128]{2,1,0:T(8,128)(2,1)S(1)}, bf16[34,32,128]{2,1,0:T(8,128)(2,1)S(1)}, bf16[34,32,128]{2,1,0:T(8,128)(2,1)}, bf16[34,32,128]{2,1,0:T(8,128)(2,1)S(1)}) custom-call(bf16[4,32,1280]{2,1,0:T(8,128)(2,1)} %q_hbm.1, bf16[4,32,1280]{2,1,0:T(8,128)(2,1)} %k_hbm.1, bf16[4,32,1280]{2,1,0:T(8,128)(2,1)} %v_hbm.1), custom_call_target="tpu_custom_call" | custom-call | tf_op jit(solution)/shard_map/pallas_call | solution.py:339
  2.0 3.1 %collective-permute-start = (bf16[34,32,128]{2,1,0:T(8,128)(2,1)S(1)}, bf16[34,32,128]{2,1,0:T(8,128)(2,1)S(1)}, u32[]{:S(2)}, u32[]{:S(2)}) collective-permute-start(bf16[34,32,128]{2,1,0:T(8,128)(2,1)S(1)} %get-tuple-element.30), channel_id=1, source_target_pairs={{0,4},{4,0},{8,12},{12,8},{1,5},{5,1},{9,13},{13,9},{2,6},{6,2},{1... | collective-permute-start | bytes 835592 | tf_op jit(solution)/shard_map/ppermute | solution.py:146
  5.1 2.3 %shard_map.56 = (bf16[10,32,640]{2,1,0:T(8,128)(2,1)S(1)}, bf16[10,32,640]{2,1,0:T(8,128)(2,1)}, bf16[10,32,640]{2,1,0:T(8,128)(2,1)}, bf16[10,32,640]{2,1,0:T(8,128)(2,1)S(1)}) custom-call(bf16[10,32,2560]{2,1,0:T(8,128)(2,1)} %w_hbm.1), custom_call_target="tpu_custom_call" | custom-call | tf_op jit(solution)/shard_map/pallas_call | solution.py:339
  7.4 0.1 collective-permute-start.3
  7.5 1.6 %collective-permute-start.4 = (bf16[10,32,640]{2,1,0:T(8,128)(2,1)}, bf16[10,32,640]{2,1,0:T(8,128)(2,1)S(1)}, u32[]{:S(2)}, u32[]{:S(2)}) collective-permute-start(bf16[10,32,640]{2,1,0:T(8,128)(2,1)} %get-tuple-element.35), channel_id=1, source_target_pairs={{0,2},{1,3},{2,0},{3,1},{4,6},{5,7},{6,4},{7,5},{8,10},{9,11},{10,... | collective-permute-start | bytes 1228808 | tf_op jit(solution)/shard_map/ppermute | solution.py:146
  9.1 0.3 collective-permute-start.5
  9.4 2.6 %collective-permute-start.1 = (bf16[34,32,128]{2,1,0:T(8,128)(2,1)}, bf16[34,32,128]{2,1,0:T(8,128)(2,1)S(1)}, u32[]{:S(2)}, u32[]{:S(2)}) collective-permute-start(bf16[34,32,128]{2,1,0:T(8,128)(2,1)} %get-tuple-element.31), channel_id=1, source_target_pairs={{0,8},{4,12},{8,0},{12,4},{1,9},{5,13},{9,1},{13,5},{2,10},{6,14},... | collective-permute-start | bytes 835592 | tf_op jit(solution)/shard_map/ppermute | solution.py:146
  11.9 0.0 collective-permute-done.refs_1_
  11.9 3.6 %collective-permute-start.2 = (bf16[34,32,128]{2,1,0:T(8,128)(2,1)S(1)}, bf16[34,32,128]{2,1,0:T(8,128)(2,1)S(1)}, u32[]{:S(2)}, u32[]{:S(2)}) collective-permute-start(bf16[34,32,128]{2,1,0:T(8,128)(2,1)S(1)} %get-tuple-element.32), channel_id=1, source_target_pairs={{0,12},{4,8},{8,4},{12,0},{1,13},{5,9},{9,5},{13,1},{2,14},{6,10},... | collective-permute-start | bytes 835592 | tf_op jit(solution)/shard_map/ppermute | solution.py:146
  15.5 0.0 copy-done
  15.5 0.1 copy.6.mask_ref
  15.7 15.9 %collective-permute-done.1.refs_2_ = bf16[34,32,128]{2,1,0:T(8,128)(2,1)S(1)} collective-permute-done((bf16[34,32,128]{2,1,0:T(8,128)(2,1)}, bf16[34,32,128]{2,1,0:T(8,128)(2,1)S(1)}, u32[]{:S(2)}, u32[]{:S(2)}) %collective-permute-start.1) | collective-permute-done | bytes 278560 | tf_op jit(solution)/shard_map/ppermute | solution.py:146
  31.5 0.0 collective-permute-done.2.refs_3_
  31.5 0.0 collective-permute-done.3.refs_5_
  31.6 0.0 collective-permute-done.4.refs_6_
  31.6 0.0 collective-permute-done.5.refs_7_
  31.6 2.5 %shard_map.57 = (bf16[32,1280]{1,0:T(8,128)(2,1)S(1)}, bf16[32,1280]{1,0:T(8,128)(2,1)S(1)}, bf16[32,1280]{1,0:T(8,128)(2,1)S(1)}, bf16[32,1280]{1,0:T(8,128)(2,1)S(1)}) custom-call(s32[10,4,4]{2,1,0:T(4,128)S(1)} %copy.6.mask_ref, bf16[34,32,128]{2,1,0:T(8,128)(2,1)S(1)} %get-tuple-element.37.refs_0_, ...), custom_call_target="tpu_custom_call" | custom-call | tf_op jit(solution)/shard_map/pallas_call | solution.py:339
  34.1 6.3 %collective-permute-start.6 = (bf16[32,1280]{1,0:T(8,128)(2,1)S(1)}, bf16[32,1280]{1,0:T(8,128)(2,1)S(1)}, u32[]{:S(2)}, u32[]{:S(2)}) collective-permute-start(bf16[32,1280]{1,0:T(8,128)(2,1)S(1)} %get-tuple-element.42), channel_id=1, source_target_pairs={{0,4},{4,0},{8,12},{12,8},{1,5},{5,1},{9,13},{13,9},{2,6},{6,2},{1... | collective-permute-start | bytes 245768 | tf_op jit(solution)/shard_map/ppermute | solution.py:146
  40.4 1.2 %collective-permute-start.7 = (bf16[32,1280]{1,0:T(8,128)(2,1)S(1)}, bf16[32,1280]{1,0:T(8,128)(2,1)S(1)}, u32[]{:S(2)}, u32[]{:S(2)}) collective-permute-start(bf16[32,1280]{1,0:T(8,128)(2,1)S(1)} %get-tuple-element.43), channel_id=1, source_target_pairs={{0,8},{4,12},{8,0},{12,4},{1,9},{5,13},{9,1},{13,5},{2,10},{6,14},... | collective-permute-start | bytes 245768 | tf_op jit(solution)/shard_map/ppermute | solution.py:146
  41.6 1.4 %collective-permute-start.8 = (bf16[32,1280]{1,0:T(8,128)(2,1)S(1)}, bf16[32,1280]{1,0:T(8,128)(2,1)S(1)}, u32[]{:S(2)}, u32[]{:S(2)}) collective-permute-start(bf16[32,1280]{1,0:T(8,128)(2,1)S(1)} %get-tuple-element.44), channel_id=1, source_target_pairs={{0,12},{4,8},{8,4},{12,0},{1,13},{5,9},{9,5},{13,1},{2,14},{6,10},... | collective-permute-start | bytes 245768 | tf_op jit(solution)/shard_map/ppermute | solution.py:146
  43.0 1.5 %collective-permute-start.10 = (bf16[32,1280]{1,0:T(8,128)(2,1)S(1)}, bf16[32,1280]{1,0:T(8,128)(2,1)S(1)}, u32[]{:S(2)}, u32[]{:S(2)}) collective-permute-start(bf16[32,1280]{1,0:T(8,128)(2,1)S(1)} %get-tuple-element.41.refs_0_), channel_id=1, source_target_pairs={{0,2},{1,3},{2,0},{3,1},{4,6},{5,7},{6,4},{7,5},{8,10},{9,11},{10,... | collective-permute-start | bytes 245768 | tf_op jit(solution)/shard_map/ppermute | solution.py:146
  44.5 0.0 collective-permute-done.6.refs_1_
  44.5 0.5 collective-permute-start.11
  45.0 4.4 %collective-permute-done.7.refs_2_ = bf16[32,1280]{1,0:T(8,128)(2,1)S(1)} collective-permute-done((bf16[32,1280]{1,0:T(8,128)(2,1)S(1)}, bf16[32,1280]{1,0:T(8,128)(2,1)S(1)}, u32[]{:S(2)}, u32[]{:S(2)}) %collective-permute-start.7) | collective-permute-done | bytes 81952 | tf_op jit(solution)/shard_map/ppermute | solution.py:146
  49.3 1.5 %collective-permute-start.12 = (bf16[32,1280]{1,0:T(8,128)(2,1)S(1)}, bf16[32,1280]{1,0:T(8,128)(2,1)S(1)}, u32[]{:S(2)}, u32[]{:S(2)}) collective-permute-start(bf16[32,1280]{1,0:T(8,128)(2,1)S(1)} %collective-permute-done.7.refs_2_), channel_id=1, source_target_pairs={{0,2},{1,3},{2,0},{3,1},{4,6},{5,7},{6,4},{7,5},{8,10},{9,11},{10,... | collective-permute-start | bytes 245768 | tf_op jit(solution)/shard_map/ppermute | solution.py:146
  50.8 0.0 collective-permute-done.8.refs_3_
  50.9 0.5 collective-permute-start.13
  51.4 0.1 collective-permute-start.9
  51.5 0.0 collective-permute-done.10.refs_0_
  51.5 0.0 collective-permute-done.11.refs_1_
  51.5 2.3 %collective-permute-done.12.refs_2_ = bf16[32,1280]{1,0:T(8,128)(2,1)S(1)} collective-permute-done((bf16[32,1280]{1,0:T(8,128)(2,1)S(1)}, bf16[32,1280]{1,0:T(8,128)(2,1)S(1)}, u32[]{:S(2)}, u32[]{:S(2)}) %collective-permute-start.12) | collective-permute-done | bytes 81952 | tf_op jit(solution)/shard_map/ppermute | solution.py:146
  53.8 1.5 %collective-permute-done.13.refs_3_ = bf16[32,1280]{1,0:T(8,128)(2,1)S(1)} collective-permute-done((bf16[32,1280]{1,0:T(8,128)(2,1)S(1)}, bf16[32,1280]{1,0:T(8,128)(2,1)S(1)}, u32[]{:S(2)}, u32[]{:S(2)}) %collective-permute-start.13) | collective-permute-done | bytes 81952 | tf_op jit(solution)/shard_map/ppermute | solution.py:146
  55.3 0.1 collective-permute-start.14
  55.4 0.0 collective-permute-done.9.refs_1_
  55.4 1.6 %collective-permute-done.14.refs_3_ = bf16[4,32,1280]{2,1,0:T(8,128)(2,1)S(1)} collective-permute-done((bf16[4,32,1280]{2,1,0:T(8,128)(2,1)S(1)}, bf16[4,32,1280]{2,1,0:T(8,128)(2,1)S(1)}, u32[]{:S(2)}, u32[]{:S(2)}) %collective-permute-start.14) | collective-permute-done | bytes 327712 | tf_op jit(solution)/shard_map/ppermute | solution.py:146
  57.0 1.9 %shard_map.60 = (f32[4,32,640]{2,1,0:T(8,128)S(1)}, bf16[4,32,640]{2,1,0:T(8,128)(2,1)S(1)}, bf16[4,32,640]{2,1,0:T(8,128)(2,1)S(1)}, bf16[4,32,640]{2,1,0:T(8,128)(2,1)S(1)}) custom-call(bf16[4,32,1280]{2,1,0:T(8,128)(2,1)S(1)} %shard_map.58.refs_0_, bf16[4,32,1280]{2,1,0:T(8,128)(2,1)S(1)} %collective-permute-done.9.refs_1_, ...), custom_call_target="tpu_custom_call" | custom-call | tf_op jit(solution)/shard_map/pallas_call | solution.py:339
  58.9 0.2 collective-permute-start.15
  59.1 2.6 %collective-permute-start.16 = (bf16[4,32,640]{2,1,0:T(8,128)(2,1)S(1)}, bf16[4,32,640]{2,1,0:T(8,128)(2,1)S(1)}, u32[]{:S(2)}, u32[]{:S(2)}) collective-permute-start(bf16[4,32,640]{2,1,0:T(8,128)(2,1)S(1)} %get-tuple-element.51), channel_id=1, source_target_pairs={{0,8},{4,12},{8,0},{12,4},{1,9},{5,13},{9,1},{13,5},{2,10},{6,14},... | collective-permute-start | bytes 491528 | tf_op jit(solution)/shard_map/ppermute | solution.py:146
  61.8 1.6 %collective-permute-start.17 = (bf16[4,32,640]{2,1,0:T(8,128)(2,1)S(1)}, bf16[4,32,640]{2,1,0:T(8,128)(2,1)S(1)}, u32[]{:S(2)}, u32[]{:S(2)}) collective-permute-start(bf16[4,32,640]{2,1,0:T(8,128)(2,1)S(1)} %get-tuple-element.52), channel_id=1, source_target_pairs={{0,12},{4,8},{8,4},{12,0},{1,13},{5,9},{9,5},{13,1},{2,14},{6,10},... | collective-permute-start | bytes 491528 | tf_op jit(solution)/shard_map/ppermute | solution.py:146
  63.4 4.7 %collective-permute-done.15 = bf16[4,32,640]{2,1,0:T(8,128)(2,1)S(1)} collective-permute-done((bf16[4,32,640]{2,1,0:T(8,128)(2,1)S(1)}, bf16[4,32,640]{2,1,0:T(8,128)(2,1)S(1)}, u32[]{:S(2)}, u32[]{:S(2)}) %collective-permute-start.15) | collective-permute-done | bytes 163872 | tf_op jit(solution)/shard_map/ppermute | solution.py:146
  68.0 6.1 %collective-permute-done.16 = bf16[4,32,640]{2,1,0:T(8,128)(2,1)S(1)} collective-permute-done((bf16[4,32,640]{2,1,0:T(8,128)(2,1)S(1)}, bf16[4,32,640]{2,1,0:T(8,128)(2,1)S(1)}, u32[]{:S(2)}, u32[]{:S(2)}) %collective-permute-start.16) | collective-permute-done | bytes 163872 | tf_op jit(solution)/shard_map/ppermute | solution.py:146
  74.2 0.0 collective-permute-done.17
  74.2 0.7 add_convert_fusion
  (2 shorter events, 0.0 us)
Async XLA Ops:
  0.0 15.5 %copy-start = (s32[10,4,4]{0,2,1:T(4,128)S(1)}, s32[10,4,4]{0,2,1:T(4,128)}, u32[]{:S(2)}) copy-start(s32[10,4,4]{0,2,1:T(4,128)} %param.8) | copy-start | bytes 1924
  2.0 9.9 %collective-permute-start = (bf16[34,32,128]{2,1,0:T(8,128)(2,1)S(1)}, bf16[34,32,128]{2,1,0:T(8,128)(2,1)S(1)}, u32[]{:S(2)}, u32[]{:S(2)}) collective-permute-start(bf16[34,32,128]{2,1,0:T(8,128)(2,1)S(1)} %get-tuple-element.30), channel_id=1, source_target_pairs={{0,4},{4,0},{8,12},{12,8},{1,5},{5,1},{9,13},{13,9},{2,6},{6,2},{1... | collective-permute-start | bytes 835592 | tf_op jit(solution)/shard_map/ppermute | solution.py:146
  7.4 24.1 %collective-permute-start.3 = (bf16[10,32,640]{2,1,0:T(8,128)(2,1)}, bf16[10,32,640]{2,1,0:T(8,128)(2,1)S(1)}, u32[]{:S(2)}, u32[]{:S(2)}) collective-permute-start(bf16[10,32,640]{2,1,0:T(8,128)(2,1)} %get-tuple-element.34), channel_id=1, source_target_pairs={{0,1},{1,0},{2,3},{3,2},{4,5},{5,4},{6,7},{7,6},{8,9},{9,8},{10,11... | collective-permute-start | bytes 1228808 | tf_op jit(solution)/shard_map/ppermute | solution.py:146
  7.5 24.0 %collective-permute-start.4 = (bf16[10,32,640]{2,1,0:T(8,128)(2,1)}, bf16[10,32,640]{2,1,0:T(8,128)(2,1)S(1)}, u32[]{:S(2)}, u32[]{:S(2)}) collective-permute-start(bf16[10,32,640]{2,1,0:T(8,128)(2,1)} %get-tuple-element.35), channel_id=1, source_target_pairs={{0,2},{1,3},{2,0},{3,1},{4,6},{5,7},{6,4},{7,5},{8,10},{9,11},{10,... | collective-permute-start | bytes 1228808 | tf_op jit(solution)/shard_map/ppermute | solution.py:146
  9.1 22.5 %collective-permute-start.5 = (bf16[10,32,640]{2,1,0:T(8,128)(2,1)S(1)}, bf16[10,32,640]{2,1,0:T(8,128)(2,1)S(1)}, u32[]{:S(2)}, u32[]{:S(2)}) collective-permute-start(bf16[10,32,640]{2,1,0:T(8,128)(2,1)S(1)} %get-tuple-element.36), channel_id=1, source_target_pairs={{0,3},{1,2},{2,1},{3,0},{4,7},{5,6},{6,5},{7,4},{8,11},{9,10},{10,... | collective-permute-start | bytes 1228808 | tf_op jit(solution)/shard_map/ppermute | solution.py:146
  9.4 22.2 %collective-permute-start.1 = (bf16[34,32,128]{2,1,0:T(8,128)(2,1)}, bf16[34,32,128]{2,1,0:T(8,128)(2,1)S(1)}, u32[]{:S(2)}, u32[]{:S(2)}) collective-permute-start(bf16[34,32,128]{2,1,0:T(8,128)(2,1)} %get-tuple-element.31), channel_id=1, source_target_pairs={{0,8},{4,12},{8,0},{12,4},{1,9},{5,13},{9,1},{13,5},{2,10},{6,14},... | collective-permute-start | bytes 835592 | tf_op jit(solution)/shard_map/ppermute | solution.py:146
  11.9 19.6 %collective-permute-start.2 = (bf16[34,32,128]{2,1,0:T(8,128)(2,1)S(1)}, bf16[34,32,128]{2,1,0:T(8,128)(2,1)S(1)}, u32[]{:S(2)}, u32[]{:S(2)}) collective-permute-start(bf16[34,32,128]{2,1,0:T(8,128)(2,1)S(1)} %get-tuple-element.32), channel_id=1, source_target_pairs={{0,12},{4,8},{8,4},{12,0},{1,13},{5,9},{9,5},{13,1},{2,14},{6,10},... | collective-permute-start | bytes 835592 | tf_op jit(solution)/shard_map/ppermute | solution.py:146
  34.1 10.3 %collective-permute-start.6 = (bf16[32,1280]{1,0:T(8,128)(2,1)S(1)}, bf16[32,1280]{1,0:T(8,128)(2,1)S(1)}, u32[]{:S(2)}, u32[]{:S(2)}) collective-permute-start(bf16[32,1280]{1,0:T(8,128)(2,1)S(1)} %get-tuple-element.42), channel_id=1, source_target_pairs={{0,4},{4,0},{8,12},{12,8},{1,5},{5,1},{9,13},{13,9},{2,6},{6,2},{1... | collective-permute-start | bytes 245768 | tf_op jit(solution)/shard_map/ppermute | solution.py:146
  40.4 9.0 %collective-permute-start.7 = (bf16[32,1280]{1,0:T(8,128)(2,1)S(1)}, bf16[32,1280]{1,0:T(8,128)(2,1)S(1)}, u32[]{:S(2)}, u32[]{:S(2)}) collective-permute-start(bf16[32,1280]{1,0:T(8,128)(2,1)S(1)} %get-tuple-element.43), channel_id=1, source_target_pairs={{0,8},{4,12},{8,0},{12,4},{1,9},{5,13},{9,1},{13,5},{2,10},{6,14},... | collective-permute-start | bytes 245768 | tf_op jit(solution)/shard_map/ppermute | solution.py:146
  41.6 9.3 %collective-permute-start.8 = (bf16[32,1280]{1,0:T(8,128)(2,1)S(1)}, bf16[32,1280]{1,0:T(8,128)(2,1)S(1)}, u32[]{:S(2)}, u32[]{:S(2)}) collective-permute-start(bf16[32,1280]{1,0:T(8,128)(2,1)S(1)} %get-tuple-element.44), channel_id=1, source_target_pairs={{0,12},{4,8},{8,4},{12,0},{1,13},{5,9},{9,5},{13,1},{2,14},{6,10},... | collective-permute-start | bytes 245768 | tf_op jit(solution)/shard_map/ppermute | solution.py:146
  43.0 8.5 %collective-permute-start.10 = (bf16[32,1280]{1,0:T(8,128)(2,1)S(1)}, bf16[32,1280]{1,0:T(8,128)(2,1)S(1)}, u32[]{:S(2)}, u32[]{:S(2)}) collective-permute-start(bf16[32,1280]{1,0:T(8,128)(2,1)S(1)} %get-tuple-element.41.refs_0_), channel_id=1, source_target_pairs={{0,2},{1,3},{2,0},{3,1},{4,6},{5,7},{6,4},{7,5},{8,10},{9,11},{10,... | collective-permute-start | bytes 245768 | tf_op jit(solution)/shard_map/ppermute | solution.py:146
  44.5 7.0 %collective-permute-start.11 = (bf16[32,1280]{1,0:T(8,128)(2,1)S(1)}, bf16[32,1280]{1,0:T(8,128)(2,1)S(1)}, u32[]{:S(2)}, u32[]{:S(2)}) collective-permute-start(bf16[32,1280]{1,0:T(8,128)(2,1)S(1)} %collective-permute-done.6.refs_1_), channel_id=1, source_target_pairs={{0,2},{1,3},{2,0},{3,1},{4,6},{5,7},{6,4},{7,5},{8,10},{9,11},{10,... | collective-permute-start | bytes 245768 | tf_op jit(solution)/shard_map/ppermute | solution.py:146
  49.3 4.4 %collective-permute-start.12 = (bf16[32,1280]{1,0:T(8,128)(2,1)S(1)}, bf16[32,1280]{1,0:T(8,128)(2,1)S(1)}, u32[]{:S(2)}, u32[]{:S(2)}) collective-permute-start(bf16[32,1280]{1,0:T(8,128)(2,1)S(1)} %collective-permute-done.7.refs_2_), channel_id=1, source_target_pairs={{0,2},{1,3},{2,0},{3,1},{4,6},{5,7},{6,4},{7,5},{8,10},{9,11},{10,... | collective-permute-start | bytes 245768 | tf_op jit(solution)/shard_map/ppermute | solution.py:146
  50.9 4.4 %collective-permute-start.13 = (bf16[32,1280]{1,0:T(8,128)(2,1)S(1)}, bf16[32,1280]{1,0:T(8,128)(2,1)S(1)}, u32[]{:S(2)}, u32[]{:S(2)}) collective-permute-start(bf16[32,1280]{1,0:T(8,128)(2,1)S(1)} %collective-permute-done.8.refs_3_), channel_id=1, source_target_pairs={{0,2},{1,3},{2,0},{3,1},{4,6},{5,7},{6,4},{7,5},{8,10},{9,11},{10,... | collective-permute-start | bytes 245768 | tf_op jit(solution)/shard_map/ppermute | solution.py:146
  51.4 4.0 %collective-permute-start.9 = (bf16[4,32,1280]{2,1,0:T(8,128)(2,1)S(1)}, bf16[4,32,1280]{2,1,0:T(8,128)(2,1)S(1)}, u32[]{:S(2)}, u32[]{:S(2)}) collective-permute-start(bf16[4,32,1280]{2,1,0:T(8,128)(2,1)S(1)} %shard_map.58.refs_0_), channel_id=1, source_target_pairs={{0,1},{1,0},{2,3},{3,2},{4,5},{5,4},{6,7},{7,6},{8,9},{9,8},{10,11... | collective-permute-start | bytes 983048 | tf_op jit(solution)/shard_map/ppermute | solution.py:146
  55.3 1.7 %collective-permute-start.14 = (bf16[4,32,1280]{2,1,0:T(8,128)(2,1)S(1)}, bf16[4,32,1280]{2,1,0:T(8,128)(2,1)S(1)}, u32[]{:S(2)}, u32[]{:S(2)}) collective-permute-start(bf16[4,32,1280]{2,1,0:T(8,128)(2,1)S(1)} %shard_map.59.refs_2_), channel_id=1, source_target_pairs={{0,1},{1,0},{2,3},{3,2},{4,5},{5,4},{6,7},{7,6},{8,9},{9,8},{10,11... | collective-permute-start | bytes 983048 | tf_op jit(solution)/shard_map/ppermute | solution.py:146
  58.9 9.1 %collective-permute-start.15 = (bf16[4,32,640]{2,1,0:T(8,128)(2,1)S(1)}, bf16[4,32,640]{2,1,0:T(8,128)(2,1)S(1)}, u32[]{:S(2)}, u32[]{:S(2)}) collective-permute-start(bf16[4,32,640]{2,1,0:T(8,128)(2,1)S(1)} %get-tuple-element.50), channel_id=1, source_target_pairs={{0,4},{4,0},{8,12},{12,8},{1,5},{5,1},{9,13},{13,9},{2,6},{6,2},{1... | collective-permute-start | bytes 491528 | tf_op jit(solution)/shard_map/ppermute | solution.py:146
  59.1 15.0 %collective-permute-start.16 = (bf16[4,32,640]{2,1,0:T(8,128)(2,1)S(1)}, bf16[4,32,640]{2,1,0:T(8,128)(2,1)S(1)}, u32[]{:S(2)}, u32[]{:S(2)}) collective-permute-start(bf16[4,32,640]{2,1,0:T(8,128)(2,1)S(1)} %get-tuple-element.51), channel_id=1, source_target_pairs={{0,8},{4,12},{8,0},{12,4},{1,9},{5,13},{9,1},{13,5},{2,10},{6,14},... | collective-permute-start | bytes 491528 | tf_op jit(solution)/shard_map/ppermute | solution.py:146
  61.8 12.4 %collective-permute-start.17 = (bf16[4,32,640]{2,1,0:T(8,128)(2,1)S(1)}, bf16[4,32,640]{2,1,0:T(8,128)(2,1)S(1)}, u32[]{:S(2)}, u32[]{:S(2)}) collective-permute-start(bf16[4,32,640]{2,1,0:T(8,128)(2,1)S(1)} %get-tuple-element.52), channel_id=1, source_target_pairs={{0,12},{4,8},{8,4},{12,0},{1,13},{5,9},{9,5},{13,1},{2,14},{6,10},... | collective-permute-start | bytes 491528 | tf_op jit(solution)/shard_map/ppermute | solution.py:146

commit v3 on v2

--- a/solution.py
+++ b/solution.py
@@ -186,52 +186,51 @@
         return summed < gathered
 
 
+def run_copies(pairs, sems):
+    copies = [pltpu.make_async_copy(a, b, sems.at[i]) for i, (a, b) in enumerate(pairs)]
+    for copy in copies:
+        copy.start()
+    for copy in copies:
+        copy.wait()
+
+
 def pack_kernel(z, q_hbm, k_hbm, v_hbm, *refs):
     out_refs = refs[: z.ranks]
     q_ref, k_ref, v_ref, sems = refs[z.ranks :]
     me = lax.axis_index("seq")
-    copies = [
-        pltpu.make_async_copy(source, target, sems.at[i])
-        for i, (source, target) in enumerate(
-            ((q_hbm, q_ref), (k_hbm, k_ref), (v_hbm, v_ref))
-        )
-    ]
+    arrays = ((q_hbm, q_ref, 0), (k_hbm, k_ref, z.q_units), (v_hbm, v_ref, z.q_units + z.kv_units))
+    copies = []
+    for i, (hbm, ref, _) in enumerate(arrays):
+        for b in range(z.blocks):
+            copies.append(pltpu.make_async_copy(hbm.at[b], ref.at[b], sems.at[i * z.blocks + b]))
     for copy in copies:
         copy.start()
-    for copy, ref, begin, strip in (
-        (copies[0], q_ref, 0, z.strip),
-        (copies[1], k_ref, z.q_units, z.blocks),
-        (copies[2], v_ref, z.q_units + z.kv_units, z.blocks),
-    ):
-        copy.wait()
-        for flip in range(z.ranks):
-            peer = me ^ flip
-            for slot in range(z.whole):
-                cols = pl.ds(aligned(slot * z.ranks + peer, z.hd), z.hd)
-                at = begin + slot * z.blocks
-                out_refs[flip][at : at + z.blocks] = ref[:, :, cols]
-            if z.rest:
+    for i, (_, ref, begin) in enumerate(arrays):
+        for b in range(z.blocks):
+            copies[i * z.blocks + b].wait()
+            for flip in range(z.ranks):
+                for slot in range(z.whole):
+                    cols = pl.ds(aligned(slot * z.ranks + (me ^ flip), z.hd), z.hd)
+                    out_refs[flip][begin + slot * z.blocks + b] = ref[b, :, cols]
+        if z.rest:
+            count = z.strip if i == 0 else z.blocks
+            for flip in range(z.ranks):
+                peer = me ^ flip
                 cols = pl.ds(aligned(z.whole * z.ranks + peer // z.sharers, z.hd), z.hd)
-                first = (peer % z.sharers) * z.strip if strip < z.blocks else 0
+                first = (peer % z.sharers) * z.strip if i == 0 else 0
                 at = begin + z.whole * z.blocks
-                out_refs[flip][at : at + strip] = ref[pl.ds(first, strip), :, cols]
+                out_refs[flip][at : at + count] = ref[pl.ds(first, count), :, cols]
 
 
 def weight_kernel(z, w_hbm, *refs):
     out_refs, sems = refs[: z.tps], refs[z.tps]
     me = lax.axis_index("tp")
-    copies = [
-        pltpu.make_async_copy(
-            w_hbm.at[:, :, pl.ds(aligned(me ^ flip, z.cols), z.cols)],
-            out_refs[flip],
-            sems.at[flip],
-        )
-        for flip in range(z.tps)
-    ]
-    for copy in copies:
-        copy.start()
-    for copy in copies:
-        copy.wait()
+    pairs = []
+    for head in range(z.heads):
+        for flip in range(z.tps):
+            cols = pl.ds(aligned(me ^ flip, z.cols), z.cols)
+            pairs.append((w_hbm.at[head, :, cols], out_refs[flip].at[head]))
+    run_copies(pairs, sems)
 
 
 def attend_kernel(z, mask_ref, *refs):
@@ -271,7 +270,7 @@
             tiles = []
             for t in range(z.blocks):
                 tile = scores[t * z.block_rows : (t + 1) * z.block_rows]
-                tiles.append(jnp.where(mask_ref[head, first + b, t] > 0, tile, -jnp.inf))
+                tiles.append(jnp.where(mask_ref[first + b, t, head] > 0, tile, -jnp.inf))
             scores = jnp.concatenate(tiles, axis=0)
             largest = jnp.max(scores, axis=0, keepdims=True)
             exps = jnp.exp(scores - largest)
@@ -295,14 +294,15 @@
         refs[z.ranks][flip] = refs[flip][...]
 
 
-def project_kernel(z, *refs):
-    token_refs = refs[: z.tps]
-    weight_refs = refs[z.tps : 2 * z.tps]
-    own_ref = refs[2 * z.tps]
-    out_refs = refs[2 * z.tps + 1 : 2 * z.tps + z.ranks]
-    inputs, total = refs[2 * z.tps + z.ranks :]
+def project_kernel(z, count, has_total, is_last, *refs):
+    token_refs, refs = refs[:count], refs[count:]
+    weight_refs, refs = refs[:count], refs[count:]
+    if has_total:
+        before, refs = refs[0], refs[1:]
+    out_refs, inputs = refs[: z.ranks if is_last else 1], refs[z.ranks if is_last else 1]
     me = lax.axis_index("seq")
-    for t in range(z.tps):
+    acc = before[...].reshape(z.tokens, z.cols) if has_total else None
+    for t in range(count):
         for flip in range(z.ranks):
             source = me ^ flip
             for slot in range(z.whole):
@@ -315,21 +315,25 @@
                 at = pl.ds(aligned(source % z.sharers, wide), wide)
                 lanes = slice(z.whole * z.tokens, z.whole * z.tokens + wide)
                 inputs[t, pl.ds(aligned(head, z.part), z.part), at] = token_refs[t][flip, :, lanes]
-    acc = None
-    for t in range(z.tps):
+    for t in range(count):
         w = weight_refs[t][...].reshape(z.heads * z.part, z.cols)
         term = lax.dot_general(
             inputs[t], w, (((0,), (0,)), ((), ())), preferred_element_type=jnp.float32
         )
         acc = term if acc is None else acc + term
-    total[...] = acc.reshape(z.blocks, z.ranks, z.rows, z.cols)
+    acc = acc.reshape(z.blocks, z.ranks, z.rows, z.cols)
+    if not is_last:
+        out_refs[0][...] = acc
+        return
+    total = refs[z.ranks + 1]
+    total[...] = acc
     for b in range(z.blocks):
-        own_ref[b] = total[b, me]
+        out_refs[0][b] = total[b, me]
         for flip in range(1, z.ranks):
-            out_refs[flip - 1][b] = total[b, me ^ flip].astype(jnp.bfloat16)
-
-
-def local_call(kernel, outs, scratch=(), places=None, limit=16):
+            out_refs[flip][b] = total[b, me ^ flip].astype(jnp.bfloat16)
+
+
+def local_call(kernel, outs, scratch=(), places=None, limit=16, flops=1 << 20):
     def call(*args):
         spaces = places or [pltpu.VMEM] * len(args)
         args = [
@@ -343,6 +347,7 @@
             out_specs=[pl.BlockSpec(memory_space=pltpu.VMEM)] * len(outs),
             scratch_shapes=list(scratch),
             compiler_params=pltpu.CompilerParams(vmem_limit_bytes=limit << 20),
+            cost_estimate=pl.CostEstimate(flops=flops, bytes_accessed=1 << 20, transcendentals=0),
         )(*args)
 
     return call
@@ -358,22 +363,21 @@
 def stationary_plan(z, queries, key_vectors, value_vectors, block_mask, out_weight):
     bf16 = jnp.bfloat16
     shape = jax.ShapeDtypeStruct
-    held = pltpu.VMEM(queries.shape, bf16)
     packed = local_call(
         functools.partial(pack_kernel, z),
         [shape((z.units, z.rows, z.hd), bf16)] * z.ranks,
-        scratch=[held, held, held, pltpu.SemaphoreType.DMA((3,))],
+        scratch=[pltpu.VMEM(queries.shape, bf16)] * 3
+        + [pltpu.SemaphoreType.DMA((3 * z.blocks,))],
         places=[pltpu.HBM] * 3,
     )(queries, key_vectors, value_vectors)
     parts = exchange_all(packed, "seq")
     sliced = local_call(
         functools.partial(weight_kernel, z),
         [shape((z.heads, z.part, z.cols), bf16)] * z.tps,
-        scratch=[pltpu.SemaphoreType.DMA((z.tps,))],
+        scratch=[pltpu.SemaphoreType.DMA((z.tps * z.heads,))],
         places=[pltpu.HBM],
     )(out_weight)
     weights = exchange_all(sliced, "tp")
-    parts, weights = lax.optimization_barrier((parts, weights))
     slot_rows = pltpu.VMEM((z.slots, z.tokens, z.hd), bf16)
     strips = local_call(
         functools.partial(attend_kernel, z),
@@ -381,7 +385,8 @@
         scratch=[slot_rows, slot_rows, slot_rows]
         + [pltpu.VMEM((z.tokens, z.tokens), bf16), pltpu.VMEM((z.hd, z.out_tokens), bf16)],
         places=[pltpu.SMEM] + [pltpu.VMEM] * z.ranks,
-    )(block_mask, *parts)
+        flops=4 * z.out_tokens * z.tokens * z.hd,
+    )(block_mask.transpose(1, 2, 0), *parts)
     pieces = exchange_all(strips, "seq")
 
     def join(arrays):
@@ -389,27 +394,46 @@
             functools.partial(join_kernel, z), [shape((z.ranks, z.part, z.out_tokens), bf16)]
         )(*arrays)[0]
 
+    all_shape = (z.blocks, z.ranks, z.rows, z.cols)
+    one_shape = (z.blocks, z.rows, z.cols)
+
+    def project(sources, total, is_last):
+        outs = [shape(all_shape, jnp.float32)]
+        scratch = [pltpu.VMEM((len(sources), z.heads * z.part, z.tokens), bf16)]
+        if is_last:
+            outs = [shape(one_shape, jnp.float32)] + [shape(one_shape, bf16)] * (z.ranks - 1)
+            scratch.append(pltpu.VMEM(all_shape, jnp.float32))
+        return local_call(
+            functools.partial(project_kernel, z, len(sources), total is not None, is_last),
+            outs,
+            scratch=scratch,
+            flops=2 * len(sources) * z.heads * z.part * z.tokens * z.cols,
+        )(
+            *[tokens[t] for t in sources],
+            *[weights[t] for t in sources],
+            *([] if total is None else [total[0]]),
+        )
+
     tokens = {0: join(pieces)}
+    steps = [[0]]
     flip = z.tps // 2
     if flip:
         far = []
         for piece in pieces:
             far.append(exchange(piece, "tp", flip))
         tokens[flip] = join(far)
+        steps.append([flip])
         flip //= 2
     while flip:
         for has in list(tokens):
             tokens[has ^ flip] = exchange(tokens[has], "tp", flip)
+            steps.append([has ^ flip])
         flip //= 2
-    sums = local_call(
-        functools.partial(project_kernel, z),
-        [shape((z.blocks, z.rows, z.cols), jnp.float32)]
-        + [shape((z.blocks, z.rows, z.cols), bf16)] * (z.ranks - 1),
-        scratch=[
-            pltpu.VMEM((z.tps, z.heads * z.part, z.tokens), bf16),
-            pltpu.VMEM((z.blocks, z.ranks, z.rows, z.cols), jnp.float32),
-        ],
-    )(*[tokens[t] for t in range(z.tps)], *weights)
+    sums = None
+    if len(steps) == 4:
+        steps = [steps[0], steps[1] + steps[2], steps[3]]
+    for i, sources in enumerate(steps):
+        sums = project(sources, sums, i == len(steps) - 1)
     got = exchange_all(sums, "seq")
     total = got[0]
     for term in got[1:]:

time: 75.2 us -> 81.5 us (1.084)
  waiting for transfers between devices: 36.5 us -> 46.6 us
  starting transfers between devices: 28.7 us -> 24.6 us
  Pallas kernels: 8.76 us -> 7.88 us
    ppermute x18, waiting for transfers between devices: 36.5 us -> 46.6 us  [exchange(): return lax.ppermute(array, axis, [(i, i ^ flip) for i in range(size)])]
    ppermute x18, starting transfers between devices: 28.7 us -> 24.6 us  [exchange(): return lax.ppermute(array, axis, [(i, i ^ flip) for i in range(size)])]
    pallas_call x6 -> x8, Pallas kernels: 8.76 us -> 7.88 us  [call(): pl.pallas_call(kernel, out_shape=outs, in_specs=[pl.BlockSpec(memory_spac...]
  transfers between devices with their start and end apart: 18 -> 18, of which waited for: 7 -> 8; matrix products, arithmetic and copies ran while one was open for 0% -> 0% of each run, Pallas kernels for 3% -> 4%
where the time goes in v3:
time: 81.5 us; the launch traced here: 80.6 us
  waiting for transfers between devices  46.6 us (57%)
  starting transfers between devices  24.6 us (30%)
  Pallas kernels  7.88 us (10%)
    ppermute x18, waiting for transfers between devices, exchange(): return lax.ppermute(array, axis, [(i, i ^ flip) for i in range(size)])  46.6 us
    ppermute x18, starting transfers between devices, exchange(): return lax.ppermute(array, axis, [(i, i ^ flip) for i in range(size)])  24.6 us
    pallas_call x8, Pallas kernels, call(): pl.pallas_call(kernel, out_shape=outs, in_specs=[pl.BlockSpec(memory_spac...  7.88 us
  transfers between devices with their start and end apart: 18, of which 8 were waited for; matrix products, arithmetic and copies ran while one was open for 0% of the time, Pallas kernels for 4%

profile of v3, /device:TPU:0, one launch (start us, length us, event | category | flops | bytes accessed | tf_op | source)
XLA Modules:
  0.0 80.6 jit_solution(14469468397156227252)
XLA Ops:
  0.0 1.4 %shard_map.55 = (bf16[34,32,128]{2,1,0:T(8,128)(2,1)S(1)}, bf16[34,32,128]{2,1,0:T(8,128)(2,1)S(1)}, bf16[34,32,128]{2,1,0:T(8,128)(2,1)S(1)}, bf16[34,32,128]{2,1,0:T(8,128)(2,1)S(1)}) custom-call(bf16[4,32,1280]{2,1,0:T(8,128)(2,1)} %q_hbm.1, bf16[4,32,1280]{2,1,0:T(8,128)(2,1)} %k_hbm.1, bf16[4,32,1280]{2,1,0:T(8,128)(2,1)} %v_hbm.1), custom_call_target="tpu_custom_call" | custom-call | flops 1048576 | bytes 1048576 | tf_op jit(solution)/shard_map/pallas_call | solution.py:343
  1.4 3.1 %collective-permute-start = (bf16[34,32,128]{2,1,0:T(8,128)(2,1)S(1)}, bf16[34,32,128]{2,1,0:T(8,128)(2,1)S(1)}, u32[]{:S(2)}, u32[]{:S(2)}) collective-permute-start(bf16[34,32,128]{2,1,0:T(8,128)(2,1)S(1)} %get-tuple-element.22), channel_id=1, source_target_pairs={{0,4},{4,0},{8,12},{12,8},{1,5},{5,1},{9,13},{13,9},{2,6},{6,2},{1... | collective-permute-start | bytes 835592 | tf_op jit(solution)/shard_map/ppermute | solution.py:146
  4.5 2.6 %collective-permute-start.1 = (bf16[34,32,128]{2,1,0:T(8,128)(2,1)S(1)}, bf16[34,32,128]{2,1,0:T(8,128)(2,1)S(1)}, u32[]{:S(2)}, u32[]{:S(2)}) collective-permute-start(bf16[34,32,128]{2,1,0:T(8,128)(2,1)S(1)} %get-tuple-element.23), channel_id=1, source_target_pairs={{0,8},{4,12},{8,0},{12,4},{1,9},{5,13},{9,1},{13,5},{2,10},{6,14},... | collective-permute-start | bytes 835592 | tf_op jit(solution)/shard_map/ppermute | solution.py:146
  7.1 0.0 collective-permute-start.2
  7.1 9.3 %collective-permute-done.refs_1_ = bf16[34,32,128]{2,1,0:T(8,128)(2,1)S(1)} collective-permute-done((bf16[34,32,128]{2,1,0:T(8,128)(2,1)S(1)}, bf16[34,32,128]{2,1,0:T(8,128)(2,1)S(1)}, u32[]{:S(2)}, u32[]{:S(2)}) %collective-permute-start) | collective-permute-done | bytes 278560 | tf_op jit(solution)/shard_map/ppermute | solution.py:146
  16.4 10.5 %collective-permute-done.1.refs_2_ = bf16[34,32,128]{2,1,0:T(8,128)(2,1)S(1)} collective-permute-done((bf16[34,32,128]{2,1,0:T(8,128)(2,1)S(1)}, bf16[34,32,128]{2,1,0:T(8,128)(2,1)S(1)}, u32[]{:S(2)}, u32[]{:S(2)}) %collective-permute-start.1) | collective-permute-done | bytes 278560 | tf_op jit(solution)/shard_map/ppermute | solution.py:146
  26.9 0.0 collective-permute-done.2.refs_3_
  26.9 0.0 copy-start
  26.9 0.7 copy-done
  27.6 2.3 %shard_map.56 = (bf16[32,1280]{1,0:T(8,128)(2,1)S(1)}, bf16[32,1280]{1,0:T(8,128)(2,1)S(1)}, bf16[32,1280]{1,0:T(8,128)(2,1)S(1)}, bf16[32,1280]{1,0:T(8,128)(2,1)S(1)}) custom-call(s32[4,4,10]{2,1,0:T(4,128)S(1)} %bitcast.1, bf16[34,32,128]{2,1,0:T(8,128)(2,1)S(1)} %get-tuple-element.21.refs_0_, bf16[34,32,128]{2,1,0:T(8,128)(2,1)S(1)} %collective-permute-done.refs_1_, ...), custom_call_target="tpu_custom_call" | custom-call | flops 335544320 | bytes 1048576 | tf_op jit(solution)/shard_map/pallas_call | solution.py:343
  29.9 5.2 %collective-permute-start.4 = (bf16[32,1280]{1,0:T(8,128)(2,1)S(1)}, bf16[32,1280]{1,0:T(8,128)(2,1)S(1)}, u32[]{:S(2)}, u32[]{:S(2)}) collective-permute-start(bf16[32,1280]{1,0:T(8,128)(2,1)S(1)} %get-tuple-element.26), channel_id=1, source_target_pairs={{0,4},{4,0},{8,12},{12,8},{1,5},{5,1},{9,13},{13,9},{2,6},{6,2},{1... | collective-permute-start | bytes 245768 | tf_op jit(solution)/shard_map/ppermute | solution.py:146
  35.2 1.1 %collective-permute-start.6 = (bf16[32,1280]{1,0:T(8,128)(2,1)S(1)}, bf16[32,1280]{1,0:T(8,128)(2,1)S(1)}, u32[]{:S(2)}, u32[]{:S(2)}) collective-permute-start(bf16[32,1280]{1,0:T(8,128)(2,1)S(1)} %get-tuple-element.27), channel_id=1, source_target_pairs={{0,8},{4,12},{8,0},{12,4},{1,9},{5,13},{9,1},{13,5},{2,10},{6,14},... | collective-permute-start | bytes 245768 | tf_op jit(solution)/shard_map/ppermute | solution.py:146
  36.2 1.4 %collective-permute-start.8 = (bf16[32,1280]{1,0:T(8,128)(2,1)S(1)}, bf16[32,1280]{1,0:T(8,128)(2,1)S(1)}, u32[]{:S(2)}, u32[]{:S(2)}) collective-permute-start(bf16[32,1280]{1,0:T(8,128)(2,1)S(1)} %get-tuple-element.28), channel_id=1, source_target_pairs={{0,12},{4,8},{8,4},{12,0},{1,13},{5,9},{9,5},{13,1},{2,14},{6,10},... | collective-permute-start | bytes 245768 | tf_op jit(solution)/shard_map/ppermute | solution.py:146
  37.6 1.5 %collective-permute-start.3 = (bf16[32,1280]{1,0:T(8,128)(2,1)S(1)}, bf16[32,1280]{1,0:T(8,128)(2,1)S(1)}, u32[]{:S(2)}, u32[]{:S(2)}) collective-permute-start(bf16[32,1280]{1,0:T(8,128)(2,1)S(1)} %get-tuple-element.25.refs_0_), channel_id=1, source_target_pairs={{0,2},{1,3},{2,0},{3,1},{4,6},{5,7},{6,4},{7,5},{8,10},{9,11},{10,... | collective-permute-start | bytes 245768 | tf_op jit(solution)/shard_map/ppermute | solution.py:146
  39.1 0.0 collective-permute-done.4.refs_1_
  39.1 0.7 collective-permute-start.5
  39.9 1.7 %shard_map.58 = (bf16[10,32,640]{2,1,0:T(8,128)(2,1)S(1)}, bf16[10,32,640]{2,1,0:T(8,128)(2,1)S(1)}, bf16[10,32,640]{2,1,0:T(8,128)(2,1)S(1)}, bf16[10,32,640]{2,1,0:T(8,128)(2,1)S(1)}) custom-call(bf16[10,32,2560]{2,1,0:T(8,128)(2,1)} %w_hbm.1), custom_call_target="tpu_custom_call" | custom-call | flops 1048576 | bytes 1048576 | tf_op jit(solution)/shard_map/pallas_call | solution.py:343
  41.6 1.3 %collective-permute-start.13 = (bf16[10,32,640]{2,1,0:T(8,128)(2,1)S(1)}, bf16[10,32,640]{2,1,0:T(8,128)(2,1)S(1)}, u32[]{:S(2)}, u32[]{:S(2)}) collective-permute-start(bf16[10,32,640]{2,1,0:T(8,128)(2,1)S(1)} %get-tuple-element.30), channel_id=1, source_target_pairs={{0,2},{1,3},{2,0},{3,1},{4,6},{5,7},{6,4},{7,5},{8,10},{9,11},{10,... | collective-permute-start | bytes 1228808 | tf_op jit(solution)/shard_map/ppermute | solution.py:146
  43.0 0.3 collective-permute-done.6.refs_2_
  43.3 0.0 collective-permute-start.14
  43.3 0.0 collective-permute-done.8.refs_3_
  43.3 1.5 %collective-permute-start.7 = (bf16[32,1280]{1,0:T(8,128)(2,1)S(1)}, bf16[32,1280]{1,0:T(8,128)(2,1)S(1)}, u32[]{:S(2)}, u32[]{:S(2)}) collective-permute-start(bf16[32,1280]{1,0:T(8,128)(2,1)S(1)} %collective-permute-done.6.refs_2_), channel_id=1, source_target_pairs={{0,2},{1,3},{2,0},{3,1},{4,6},{5,7},{6,4},{7,5},{8,10},{9,11},{10,... | collective-permute-start | bytes 245768 | tf_op jit(solution)/shard_map/ppermute | solution.py:146
  44.8 0.0 collective-permute-done.3.refs_0_
  44.8 0.5 collective-permute-start.9
  45.3 0.0 collective-permute-done.5.refs_1_
  45.3 1.0 %collective-permute-start.11 = (bf16[10,32,640]{2,1,0:T(8,128)(2,1)S(1)}, bf16[10,32,640]{2,1,0:T(8,128)(2,1)S(1)}, u32[]{:S(2)}, u32[]{:S(2)}) collective-permute-start(bf16[10,32,640]{2,1,0:T(8,128)(2,1)S(1)} %get-tuple-element.29), channel_id=1, source_target_pairs={{0,3},{1,2},{2,1},{3,0},{4,7},{5,6},{6,5},{7,4},{8,11},{9,10},{10,... | collective-permute-start | bytes 1228808 | tf_op jit(solution)/shard_map/ppermute | solution.py:146
  46.4 9.4 %collective-permute-done.7.refs_2_ = bf16[32,1280]{1,0:T(8,128)(2,1)S(1)} collective-permute-done((bf16[32,1280]{1,0:T(8,128)(2,1)S(1)}, bf16[32,1280]{1,0:T(8,128)(2,1)S(1)}, u32[]{:S(2)}, u32[]{:S(2)}) %collective-permute-start.7) | collective-permute-done | bytes 81952 | tf_op jit(solution)/shard_map/ppermute | solution.py:146
  55.8 0.0 collective-permute-start.12
  55.8 1.8 %collective-permute-done.9.refs_3_ = bf16[32,1280]{1,0:T(8,128)(2,1)S(1)} collective-permute-done((bf16[32,1280]{1,0:T(8,128)(2,1)S(1)}, bf16[32,1280]{1,0:T(8,128)(2,1)S(1)}, u32[]{:S(2)}, u32[]{:S(2)}) %collective-permute-start.9) | collective-permute-done | bytes 81952 | tf_op jit(solution)/shard_map/ppermute | solution.py:146
  57.6 0.1 collective-permute-start.10
  57.6 0.6 shard_map.60.refs_4_
  58.3 0.0 collective-permute-done.13.refs_2_
  58.3 0.0 collective-permute-done.14.refs_3_
  58.3 0.0 collective-permute-done.12.refs_1_
  58.3 1.0 %shard_map.61.refs_2_ = f32[4,4,32,640]{3,2,1,0:T(8,128)S(1)} custom-call(bf16[4,32,1280]{2,1,0:T(8,128)(2,1)S(1)} %shard_map.57.refs_0_, bf16[4,32,1280]{2,1,0:T(8,128)(2,1)S(1)} %collective-permute-done.12.refs_1_, bf16[10,32,640]{2,1,0:T(8,128)(2,1)S(1)} %collective-permute-done.13.refs_2_, bf16[10,32,640]{2,1,0:T(8,128)(2,1)S(1)} %collective-permute-done.14.refs_3_, ...), custom_call_target="tpu_custom_call" | custom-call | flops 419430400 | bytes 1048576 | tf_op jit(solution)/shard_map/pallas_call | solution.py:343
  59.3 3.7 %collective-permute-done.11.refs_1_ = bf16[10,32,640]{2,1,0:T(8,128)(2,1)S(1)} collective-permute-done((bf16[10,32,640]{2,1,0:T(8,128)(2,1)S(1)}, bf16[10,32,640]{2,1,0:T(8,128)(2,1)S(1)}, u32[]{:S(2)}, u32[]{:S(2)}) %collective-permute-start.11) | collective-permute-done | bytes 409632 | tf_op jit(solution)/shard_map/ppermute | solution.py:146
  63.0 0.0 collective-permute-done.10.refs_0_
  63.0 0.7 shard_map.62
  63.8 1.1 %collective-permute-start.15 = (bf16[4,32,640]{2,1,0:T(8,128)(2,1)S(1)}, bf16[4,32,640]{2,1,0:T(8,128)(2,1)S(1)}, u32[]{:S(2)}, u32[]{:S(2)}) collective-permute-start(bf16[4,32,640]{2,1,0:T(8,128)(2,1)S(1)} %get-tuple-element.34), channel_id=1, source_target_pairs={{0,4},{4,0},{8,12},{12,8},{1,5},{5,1},{9,13},{13,9},{2,6},{6,2},{1... | collective-permute-start | bytes 491528 | tf_op jit(solution)/shard_map/ppermute | solution.py:146
  64.8 2.0 %collective-permute-start.16 = (bf16[4,32,640]{2,1,0:T(8,128)(2,1)S(1)}, bf16[4,32,640]{2,1,0:T(8,128)(2,1)S(1)}, u32[]{:S(2)}, u32[]{:S(2)}) collective-permute-start(bf16[4,32,640]{2,1,0:T(8,128)(2,1)S(1)} %get-tuple-element.35), channel_id=1, source_target_pairs={{0,8},{4,12},{8,0},{12,4},{1,9},{5,13},{9,1},{13,5},{2,10},{6,14},... | collective-permute-start | bytes 491528 | tf_op jit(solution)/shard_map/ppermute | solution.py:146
  66.8 1.4 %collective-permute-start.17 = (bf16[4,32,640]{2,1,0:T(8,128)(2,1)S(1)}, bf16[4,32,640]{2,1,0:T(8,128)(2,1)S(1)}, u32[]{:S(2)}, u32[]{:S(2)}) collective-permute-start(bf16[4,32,640]{2,1,0:T(8,128)(2,1)S(1)} %get-tuple-element.36), channel_id=1, source_target_pairs={{0,12},{4,8},{8,4},{12,0},{1,13},{5,9},{9,5},{13,1},{2,14},{6,10},... | collective-permute-start | bytes 491528 | tf_op jit(solution)/shard_map/ppermute | solution.py:146
  68.2 5.8 %collective-permute-done.15 = bf16[4,32,640]{2,1,0:T(8,128)(2,1)S(1)} collective-permute-done((bf16[4,32,640]{2,1,0:T(8,128)(2,1)S(1)}, bf16[4,32,640]{2,1,0:T(8,128)(2,1)S(1)}, u32[]{:S(2)}, u32[]{:S(2)}) %collective-permute-start.15) | collective-permute-done | bytes 163872 | tf_op jit(solution)/shard_map/ppermute | solution.py:146
  74.0 5.9 %collective-permute-done.16 = bf16[4,32,640]{2,1,0:T(8,128)(2,1)S(1)} collective-permute-done((bf16[4,32,640]{2,1,0:T(8,128)(2,1)S(1)}, bf16[4,32,640]{2,1,0:T(8,128)(2,1)S(1)}, u32[]{:S(2)}, u32[]{:S(2)}) %collective-permute-start.16) | collective-permute-done | bytes 163872 | tf_op jit(solution)/shard_map/ppermute | solution.py:146
  79.9 0.0 collective-permute-done.17
  79.9 0.7 add_convert_fusion
  (2 shorter events, 0.0 us)
Async XLA Ops:
  1.4 15.0 %collective-permute-start = (bf16[34,32,128]{2,1,0:T(8,128)(2,1)S(1)}, bf16[34,32,128]{2,1,0:T(8,128)(2,1)S(1)}, u32[]{:S(2)}, u32[]{:S(2)}) collective-permute-start(bf16[34,32,128]{2,1,0:T(8,128)(2,1)S(1)} %get-tuple-element.22), channel_id=1, source_target_pairs={{0,4},{4,0},{8,12},{12,8},{1,5},{5,1},{9,13},{13,9},{2,6},{6,2},{1... | collective-permute-start | bytes 835592 | tf_op jit(solution)/shard_map/ppermute | solution.py:146
  4.5 22.4 %collective-permute-start.1 = (bf16[34,32,128]{2,1,0:T(8,128)(2,1)S(1)}, bf16[34,32,128]{2,1,0:T(8,128)(2,1)S(1)}, u32[]{:S(2)}, u32[]{:S(2)}) collective-permute-start(bf16[34,32,128]{2,1,0:T(8,128)(2,1)S(1)} %get-tuple-element.23), channel_id=1, source_target_pairs={{0,8},{4,12},{8,0},{12,4},{1,9},{5,13},{9,1},{13,5},{2,10},{6,14},... | collective-permute-start | bytes 835592 | tf_op jit(solution)/shard_map/ppermute | solution.py:146
  7.1 19.8 %collective-permute-start.2 = (bf16[34,32,128]{2,1,0:T(8,128)(2,1)S(1)}, bf16[34,32,128]{2,1,0:T(8,128)(2,1)S(1)}, u32[]{:S(2)}, u32[]{:S(2)}) collective-permute-start(bf16[34,32,128]{2,1,0:T(8,128)(2,1)S(1)} %get-tuple-element.24), channel_id=1, source_target_pairs={{0,12},{4,8},{8,4},{12,0},{1,13},{5,9},{9,5},{13,1},{2,14},{6,10},... | collective-permute-start | bytes 835592 | tf_op jit(solution)/shard_map/ppermute | solution.py:146
  26.9 0.7 copy-start
  29.9 9.2 %collective-permute-start.4 = (bf16[32,1280]{1,0:T(8,128)(2,1)S(1)}, bf16[32,1280]{1,0:T(8,128)(2,1)S(1)}, u32[]{:S(2)}, u32[]{:S(2)}) collective-permute-start(bf16[32,1280]{1,0:T(8,128)(2,1)S(1)} %get-tuple-element.26), channel_id=1, source_target_pairs={{0,4},{4,0},{8,12},{12,8},{1,5},{5,1},{9,13},{13,9},{2,6},{6,2},{1... | collective-permute-start | bytes 245768 | tf_op jit(solution)/shard_map/ppermute | solution.py:146
  35.2 8.1 %collective-permute-start.6 = (bf16[32,1280]{1,0:T(8,128)(2,1)S(1)}, bf16[32,1280]{1,0:T(8,128)(2,1)S(1)}, u32[]{:S(2)}, u32[]{:S(2)}) collective-permute-start(bf16[32,1280]{1,0:T(8,128)(2,1)S(1)} %get-tuple-element.27), channel_id=1, source_target_pairs={{0,8},{4,12},{8,0},{12,4},{1,9},{5,13},{9,1},{13,5},{2,10},{6,14},... | collective-permute-start | bytes 245768 | tf_op jit(solution)/shard_map/ppermute | solution.py:146
  36.2 7.0 %collective-permute-start.8 = (bf16[32,1280]{1,0:T(8,128)(2,1)S(1)}, bf16[32,1280]{1,0:T(8,128)(2,1)S(1)}, u32[]{:S(2)}, u32[]{:S(2)}) collective-permute-start(bf16[32,1280]{1,0:T(8,128)(2,1)S(1)} %get-tuple-element.28), channel_id=1, source_target_pairs={{0,12},{4,8},{8,4},{12,0},{1,13},{5,9},{9,5},{13,1},{2,14},{6,10},... | collective-permute-start | bytes 245768 | tf_op jit(solution)/shard_map/ppermute | solution.py:146
  37.6 7.1 %collective-permute-start.3 = (bf16[32,1280]{1,0:T(8,128)(2,1)S(1)}, bf16[32,1280]{1,0:T(8,128)(2,1)S(1)}, u32[]{:S(2)}, u32[]{:S(2)}) collective-permute-start(bf16[32,1280]{1,0:T(8,128)(2,1)S(1)} %get-tuple-element.25.refs_0_), channel_id=1, source_target_pairs={{0,2},{1,3},{2,0},{3,1},{4,6},{5,7},{6,4},{7,5},{8,10},{9,11},{10,... | collective-permute-start | bytes 245768 | tf_op jit(solution)/shard_map/ppermute | solution.py:146
  39.1 6.2 %collective-permute-start.5 = (bf16[32,1280]{1,0:T(8,128)(2,1)S(1)}, bf16[32,1280]{1,0:T(8,128)(2,1)S(1)}, u32[]{:S(2)}, u32[]{:S(2)}) collective-permute-start(bf16[32,1280]{1,0:T(8,128)(2,1)S(1)} %collective-permute-done.4.refs_1_), channel_id=1, source_target_pairs={{0,2},{1,3},{2,0},{3,1},{4,6},{5,7},{6,4},{7,5},{8,10},{9,11},{10,... | collective-permute-start | bytes 245768 | tf_op jit(solution)/shard_map/ppermute | solution.py:146
  41.6 16.7 %collective-permute-start.13 = (bf16[10,32,640]{2,1,0:T(8,128)(2,1)S(1)}, bf16[10,32,640]{2,1,0:T(8,128)(2,1)S(1)}, u32[]{:S(2)}, u32[]{:S(2)}) collective-permute-start(bf16[10,32,640]{2,1,0:T(8,128)(2,1)S(1)} %get-tuple-element.30), channel_id=1, source_target_pairs={{0,2},{1,3},{2,0},{3,1},{4,6},{5,7},{6,4},{7,5},{8,10},{9,11},{10,... | collective-permute-start | bytes 1228808 | tf_op jit(solution)/shard_map/ppermute | solution.py:146
  43.3 15.0 %collective-permute-start.14 = (bf16[10,32,640]{2,1,0:T(8,128)(2,1)S(1)}, bf16[10,32,640]{2,1,0:T(8,128)(2,1)S(1)}, u32[]{:S(2)}, u32[]{:S(2)}) collective-permute-start(bf16[10,32,640]{2,1,0:T(8,128)(2,1)S(1)} %get-tuple-element.31), channel_id=1, source_target_pairs={{0,1},{1,0},{2,3},{3,2},{4,5},{5,4},{6,7},{7,6},{8,9},{9,8},{10,11... | collective-permute-start | bytes 1228808 | tf_op jit(solution)/shard_map/ppermute | solution.py:146
  43.3 12.5 %collective-permute-start.7 = (bf16[32,1280]{1,0:T(8,128)(2,1)S(1)}, bf16[32,1280]{1,0:T(8,128)(2,1)S(1)}, u32[]{:S(2)}, u32[]{:S(2)}) collective-permute-start(bf16[32,1280]{1,0:T(8,128)(2,1)S(1)} %collective-permute-done.6.refs_2_), channel_id=1, source_target_pairs={{0,2},{1,3},{2,0},{3,1},{4,6},{5,7},{6,4},{7,5},{8,10},{9,11},{10,... | collective-permute-start | bytes 245768 | tf_op jit(solution)/shard_map/ppermute | solution.py:146
  44.8 12.8 %collective-permute-start.9 = (bf16[32,1280]{1,0:T(8,128)(2,1)S(1)}, bf16[32,1280]{1,0:T(8,128)(2,1)S(1)}, u32[]{:S(2)}, u32[]{:S(2)}) collective-permute-start(bf16[32,1280]{1,0:T(8,128)(2,1)S(1)} %collective-permute-done.8.refs_3_), channel_id=1, source_target_pairs={{0,2},{1,3},{2,0},{3,1},{4,6},{5,7},{6,4},{7,5},{8,10},{9,11},{10,... | collective-permute-start | bytes 245768 | tf_op jit(solution)/shard_map/ppermute | solution.py:146
  45.3 17.7 %collective-permute-start.11 = (bf16[10,32,640]{2,1,0:T(8,128)(2,1)S(1)}, bf16[10,32,640]{2,1,0:T(8,128)(2,1)S(1)}, u32[]{:S(2)}, u32[]{:S(2)}) collective-permute-start(bf16[10,32,640]{2,1,0:T(8,128)(2,1)S(1)} %get-tuple-element.29), channel_id=1, source_target_pairs={{0,3},{1,2},{2,1},{3,0},{4,7},{5,6},{6,5},{7,4},{8,11},{9,10},{10,... | collective-permute-start | bytes 1228808 | tf_op jit(solution)/shard_map/ppermute | solution.py:146
  55.8 2.5 %collective-permute-start.12 = (bf16[4,32,1280]{2,1,0:T(8,128)(2,1)S(1)}, bf16[4,32,1280]{2,1,0:T(8,128)(2,1)S(1)}, u32[]{:S(2)}, u32[]{:S(2)}) collective-permute-start(bf16[4,32,1280]{2,1,0:T(8,128)(2,1)S(1)} %shard_map.59.refs_0_), channel_id=1, source_target_pairs={{0,1},{1,0},{2,3},{3,2},{4,5},{5,4},{6,7},{7,6},{8,9},{9,8},{10,11... | collective-permute-start | bytes 983048 | tf_op jit(solution)/shard_map/ppermute | solution.py:146
  57.6 5.5 %collective-permute-start.10 = (bf16[4,32,1280]{2,1,0:T(8,128)(2,1)S(1)}, bf16[4,32,1280]{2,1,0:T(8,128)(2,1)S(1)}, u32[]{:S(2)}, u32[]{:S(2)}) collective-permute-start(bf16[4,32,1280]{2,1,0:T(8,128)(2,1)S(1)} %shard_map.57.refs_0_), channel_id=1, source_target_pairs={{0,1},{1,0},{2,3},{3,2},{4,5},{5,4},{6,7},{7,6},{8,9},{9,8},{10,11... | collective-permute-start | bytes 983048 | tf_op jit(solution)/shard_map/ppermute | solution.py:146
  63.8 10.2 %collective-permute-start.15 = (bf16[4,32,640]{2,1,0:T(8,128)(2,1)S(1)}, bf16[4,32,640]{2,1,0:T(8,128)(2,1)S(1)}, u32[]{:S(2)}, u32[]{:S(2)}) collective-permute-start(bf16[4,32,640]{2,1,0:T(8,128)(2,1)S(1)} %get-tuple-element.34), channel_id=1, source_target_pairs={{0,4},{4,0},{8,12},{12,8},{1,5},{5,1},{9,13},{13,9},{2,6},{6,2},{1... | collective-permute-start | bytes 491528 | tf_op jit(solution)/shard_map/ppermute | solution.py:146
  64.8 15.0 %collective-permute-start.16 = (bf16[4,32,640]{2,1,0:T(8,128)(2,1)S(1)}, bf16[4,32,640]{2,1,0:T(8,128)(2,1)S(1)}, u32[]{:S(2)}, u32[]{:S(2)}) collective-permute-start(bf16[4,32,640]{2,1,0:T(8,128)(2,1)S(1)} %get-tuple-element.35), channel_id=1, source_target_pairs={{0,8},{4,12},{8,0},{12,4},{1,9},{5,13},{9,1},{13,5},{2,10},{6,14},... | collective-permute-start | bytes 491528 | tf_op jit(solution)/shard_map/ppermute | solution.py:146
  66.8 13.0 %collective-permute-start.17 = (bf16[4,32,640]{2,1,0:T(8,128)(2,1)S(1)}, bf16[4,32,640]{2,1,0:T(8,128)(2,1)S(1)}, u32[]{:S(2)}, u32[]{:S(2)}) collective-permute-start(bf16[4,32,640]{2,1,0:T(8,128)(2,1)S(1)} %get-tuple-element.36), channel_id=1, source_target_pairs={{0,12},{4,8},{8,4},{12,0},{1,13},{5,9},{9,5},{13,1},{2,14},{6,10},... | collective-permute-start | bytes 491528 | tf_op jit(solution)/shard_map/ppermute | solution.py:146

commit v4 on v3

--- a/solution.py
+++ b/solution.py
@@ -1,4 +1,5 @@
 import functools
+import math
 
 import jax
 import jax.numpy as jnp
@@ -236,66 +237,77 @@
 def attend_kernel(z, mask_ref, *refs):
     part_refs = refs[: z.ranks]
     out_refs = refs[z.ranks : 2 * z.ranks]
-    query, keys, values, weights, result = refs[2 * z.ranks :]
+    query, keys, values, turned, raw, weights, result = refs[2 * z.ranks :]
     me = lax.axis_index("seq")
-    scale = z.hd ** (-0.5)
+    scale = z.hd ** (-0.5) * math.log2(math.e)
+    pairs = []
     for slot in range(z.slots):
         is_strip = slot >= z.whole
         count = z.strip if is_strip else z.blocks
         head = z.whole * z.ranks + me // z.sharers if is_strip else slot * z.ranks + me
         first = (me % z.sharers) * z.strip if is_strip else 0
+        pairs.extend((slot, b, head, first + b) for b in range(count))
         for flip in range(z.ranks):
-            source = me ^ flip
             for b in range(count):
-                rows = pl.ds(b * z.block_rows + aligned(source, z.rows), z.rows)
+                rows = pl.ds(b * z.block_rows + aligned(me ^ flip, z.rows), z.rows)
                 query[slot, rows, :] = part_refs[flip][slot * z.blocks + b]
             for b in range(z.blocks):
                 rows = pl.ds(b * z.block_rows + flip * z.rows, z.rows)
                 unit = z.q_units + slot * z.blocks + b
                 keys[slot, rows, :] = part_refs[flip][unit]
                 values[slot, rows, :] = part_refs[flip][unit + z.kv_units]
-        wide = count * z.block_rows
-        inverses = []
-        for b in range(count):
-            lanes = slice(b * z.block_rows, (b + 1) * z.block_rows)
-            scores = (
-                lax.dot_general(
-                    keys[slot],
-                    query[slot, lanes, :],
-                    (((1,), (1,)), ((), ())),
-                    preferred_element_type=jnp.float32,
-                )
-                * scale
-            )
-            tiles = []
-            for t in range(z.blocks):
-                tile = scores[t * z.block_rows : (t + 1) * z.block_rows]
-                tiles.append(jnp.where(mask_ref[first + b, t, head] > 0, tile, -jnp.inf))
-            scores = jnp.concatenate(tiles, axis=0)
-            largest = jnp.max(scores, axis=0, keepdims=True)
-            exps = jnp.exp(scores - largest)
-            inverses.append(jnp.sum(exps, axis=0, keepdims=True))
-            weights[:, lanes] = exps.astype(jnp.bfloat16)
-        blended = lax.dot_general(
-            values[slot],
-            weights[:, :wide],
-            (((0,), (0,)), ((), ())),
+
+    def score(i):
+        slot, b, _, _ = pairs[i]
+        raw[i % 2] = lax.dot_general(
+            keys[slot],
+            query[slot, b * z.block_rows : (b + 1) * z.block_rows, :],
+            (((1,), (1,)), ((), ())),
             preferred_element_type=jnp.float32,
         )
-        blended = blended / jnp.concatenate(inverses, axis=1)
-        lanes = slice(slot * z.tokens, slot * z.tokens + wide)
-        result[:, lanes] = blended.astype(jnp.bfloat16)
+
+    def weigh(i):
+        _, _, head, block = pairs[i]
+        spans = [slice(t * z.block_rows, (t + 1) * z.block_rows) for t in range(z.blocks)]
+        allowed = [mask_ref[block, t, head] > 0 for t in range(z.blocks)]
+        largest = None
+        for span, live in zip(spans, allowed):
+            peak = jnp.max(raw[i % 2, span].reshape(-1, 8, z.block_rows), axis=0)
+            peak = jnp.where(live, peak, -jnp.inf)
+            largest = peak if largest is None else jnp.maximum(largest, peak)
+        largest = jnp.max(largest, axis=0, keepdims=True)
+        total = None
+        for span, live in zip(spans, allowed):
+            exps = jnp.exp2((raw[i % 2, span] - jnp.where(live, largest, jnp.inf)) * scale)
+            part = jnp.sum(exps.reshape(-1, 8, z.block_rows), axis=0)
+            total = part if total is None else total + part
+            weights[i % 2, span] = exps.astype(jnp.bfloat16)
+        return jnp.sum(total, axis=0, keepdims=True)
+
+    def blend(i, total):
+        blended = jnp.dot(
+            turned[pairs[i][0]], weights[i % 2], preferred_element_type=jnp.float32
+        )
+        lanes = slice(i * z.block_rows, (i + 1) * z.block_rows)
+        result[:, lanes] = (blended / total).astype(jnp.bfloat16)
+
+    score(0)
+    for slot in range(z.slots):
+        turned[slot] = values[slot].T
+    total = None
+    for i in range(len(pairs)):
+        if i + 1 < len(pairs):
+            score(i + 1)
+        if i:
+            blend(i - 1, total)
+        total = weigh(i)
+    blend(len(pairs) - 1, total)
     for flip in range(z.ranks):
         out_refs[flip][...] = result[pl.ds(aligned(me ^ flip, z.part), z.part), :]
 
 
-def join_kernel(z, *refs):
-    for flip in range(z.ranks):
-        refs[z.ranks][flip] = refs[flip][...]
-
-
 def project_kernel(z, count, has_total, is_last, *refs):
-    token_refs, refs = refs[:count], refs[count:]
+    token_refs, refs = refs[: count * z.ranks], refs[count * z.ranks :]
     weight_refs, refs = refs[:count], refs[count:]
     if has_total:
         before, refs = refs[0], refs[1:]
@@ -308,13 +320,13 @@
             for slot in range(z.whole):
                 rows = pl.ds(aligned(slot * z.ranks + source, z.part), z.part)
                 lanes = slice(slot * z.tokens, (slot + 1) * z.tokens)
-                inputs[t, rows, :] = token_refs[t][flip, :, lanes]
+                inputs[t, rows, :] = token_refs[t * z.ranks + flip][:, lanes]
             if z.rest:
                 head = z.whole * z.ranks + source // z.sharers
                 wide = z.strip * z.block_rows
                 at = pl.ds(aligned(source % z.sharers, wide), wide)
                 lanes = slice(z.whole * z.tokens, z.whole * z.tokens + wide)
-                inputs[t, pl.ds(aligned(head, z.part), z.part), at] = token_refs[t][flip, :, lanes]
+                inputs[t, pl.ds(aligned(head, z.part), z.part), at] = token_refs[t * z.ranks + flip][:, lanes]
     for t in range(count):
         w = weight_refs[t][...].reshape(z.heads * z.part, z.cols)
         term = lax.dot_general(
@@ -383,16 +395,16 @@
         functools.partial(attend_kernel, z),
         [shape((z.part, z.out_tokens), bf16)] * z.ranks,
         scratch=[slot_rows, slot_rows, slot_rows]
-        + [pltpu.VMEM((z.tokens, z.tokens), bf16), pltpu.VMEM((z.hd, z.out_tokens), bf16)],
+        + [
+            pltpu.VMEM((z.slots, z.hd, z.tokens), bf16),
+            pltpu.VMEM((2, z.tokens, z.block_rows), jnp.float32),
+            pltpu.VMEM((2, z.tokens, z.block_rows), bf16),
+            pltpu.VMEM((z.hd, z.out_tokens), bf16),
+        ],
         places=[pltpu.SMEM] + [pltpu.VMEM] * z.ranks,
         flops=4 * z.out_tokens * z.tokens * z.hd,
     )(block_mask.transpose(1, 2, 0), *parts)
     pieces = exchange_all(strips, "seq")
-
-    def join(arrays):
-        return local_call(
-            functools.partial(join_kernel, z), [shape((z.ranks, z.part, z.out_tokens), bf16)]
-        )(*arrays)[0]
 
     all_shape = (z.blocks, z.ranks, z.rows, z.cols)
     one_shape = (z.blocks, z.rows, z.cols)
@@ -409,24 +421,19 @@
             scratch=scratch,
             flops=2 * len(sources) * z.heads * z.part * z.tokens * z.cols,
         )(
-            *[tokens[t] for t in sources],
+            *[piece for t in sources for piece in tokens[t]],
             *[weights[t] for t in sources],
             *([] if total is None else [total[0]]),
         )
 
-    tokens = {0: join(pieces)}
+    tokens = {0: pieces}
     steps = [[0]]
     flip = z.tps // 2
-    if flip:
-        far = []
-        for piece in pieces:
-            far.append(exchange(piece, "tp", flip))
-        tokens[flip] = join(far)
-        steps.append([flip])
-        flip //= 2
     while flip:
         for has in list(tokens):
-            tokens[has ^ flip] = exchange(tokens[has], "tp", flip)
+            tokens[has ^ flip] = []
+            for piece in tokens[has]:
+                tokens[has ^ flip].append(exchange(piece, "tp", flip))
             steps.append([has ^ flip])
         flip //= 2
     sums = None

time: 81.5 us -> 77.5 us (0.951)
  waiting for transfers between devices: 46.6 us -> 36.5 us
  starting transfers between devices: 24.6 us -> 32.5 us
    ppermute x18 -> x24, waiting for transfers between devices: 46.6 us -> 36.5 us  [exchange(): return lax.ppermute(array, axis, [(i, i ^ flip) for i in range(size)])]
    ppermute x18 -> x24, starting transfers between devices: 24.6 us -> 32.5 us  [exchange(): return lax.ppermute(array, axis, [(i, i ^ flip) for i in range(size)])]
    pallas_call x8 -> x6, Pallas kernels: 7.88 us -> 7.43 us  [call(): pl.pallas_call(kernel, out_shape=outs, in_specs=[pl.BlockSpec(memory_spac...]
  transfers between devices with their start and end apart: 18 -> 24, of which waited for: 8 -> 9; matrix products, arithmetic and copies ran while one was open for 0% -> 0% of each run, Pallas kernels for 4% -> 7%
where the time goes in v4:
time: 77.5 us; the launch traced here: 77.3 us
  waiting for transfers between devices  36.5 us (47%)
  starting transfers between devices  32.5 us (42%)
  Pallas kernels  7.43 us (10%)
    ppermute x24, waiting for transfers between devices, exchange(): return lax.ppermute(array, axis, [(i, i ^ flip) for i in range(size)])  36.5 us
    ppermute x24, starting transfers between devices, exchange(): return lax.ppermute(array, axis, [(i, i ^ flip) for i in range(size)])  32.5 us
    pallas_call x6, Pallas kernels, call(): pl.pallas_call(kernel, out_shape=outs, in_specs=[pl.BlockSpec(memory_spac...  7.43 us
  transfers between devices with their start and end apart: 24, of which 9 were waited for; matrix products, arithmetic and copies ran while one was open for 0% of the time, Pallas kernels for 7%

profile of v4, /device:TPU:0, one launch (start us, length us, event | category | flops | bytes accessed | tf_op | source)
XLA Modules:
  0.0 77.3 jit_solution(8281353951577107541)
XLA Ops:
  0.0 0.0 copy-start
  0.0 1.4 %shard_map.55 = (bf16[34,32,128]{2,1,0:T(8,128)(2,1)S(1)}, bf16[34,32,128]{2,1,0:T(8,128)(2,1)S(1)}, bf16[34,32,128]{2,1,0:T(8,128)(2,1)S(1)}, bf16[34,32,128]{2,1,0:T(8,128)(2,1)S(1)}) custom-call(bf16[4,32,1280]{2,1,0:T(8,128)(2,1)} %q_hbm.1, bf16[4,32,1280]{2,1,0:T(8,128)(2,1)} %k_hbm.1, bf16[4,32,1280]{2,1,0:T(8,128)(2,1)} %v_hbm.1), custom_call_target="tpu_custom_call" | custom-call | flops 1048576 | bytes 1048576 | tf_op jit(solution)/shard_map/pallas_call | solution.py:355
  1.4 3.1 %collective-permute-start = (bf16[34,32,128]{2,1,0:T(8,128)(2,1)S(1)}, bf16[34,32,128]{2,1,0:T(8,128)(2,1)S(1)}, u32[]{:S(2)}, u32[]{:S(2)}) collective-permute-start(bf16[34,32,128]{2,1,0:T(8,128)(2,1)S(1)} %get-tuple-element.22), channel_id=1, source_target_pairs={{0,4},{4,0},{8,12},{12,8},{1,5},{5,1},{9,13},{13,9},{2,6},{6,2},{1... | collective-permute-start | bytes 835592 | tf_op jit(solution)/shard_map/ppermute | solution.py:147
  4.5 2.6 %collective-permute-start.1 = (bf16[34,32,128]{2,1,0:T(8,128)(2,1)S(1)}, bf16[34,32,128]{2,1,0:T(8,128)(2,1)S(1)}, u32[]{:S(2)}, u32[]{:S(2)}) collective-permute-start(bf16[34,32,128]{2,1,0:T(8,128)(2,1)S(1)} %get-tuple-element.23), channel_id=1, source_target_pairs={{0,8},{4,12},{8,0},{12,4},{1,9},{5,13},{9,1},{13,5},{2,10},{6,14},... | collective-permute-start | bytes 835592 | tf_op jit(solution)/shard_map/ppermute | solution.py:147
  7.1 0.0 collective-permute-start.2
  7.1 1.7 %shard_map.57 = (bf16[10,32,640]{2,1,0:T(8,128)(2,1)S(1)}, bf16[10,32,640]{2,1,0:T(8,128)(2,1)S(1)}, bf16[10,32,640]{2,1,0:T(8,128)(2,1)S(1)}, bf16[10,32,640]{2,1,0:T(8,128)(2,1)S(1)}) custom-call(bf16[10,32,2560]{2,1,0:T(8,128)(2,1)} %w_hbm.1), custom_call_target="tpu_custom_call" | custom-call | flops 1048576 | bytes 1048576 | tf_op jit(solution)/shard_map/pallas_call | solution.py:355
  8.9 1.8 %collective-permute-start.19 = (bf16[10,32,640]{2,1,0:T(8,128)(2,1)S(1)}, bf16[10,32,640]{2,1,0:T(8,128)(2,1)S(1)}, u32[]{:S(2)}, u32[]{:S(2)}) collective-permute-start(bf16[10,32,640]{2,1,0:T(8,128)(2,1)S(1)} %get-tuple-element.30), channel_id=1, source_target_pairs={{0,2},{1,3},{2,0},{3,1},{4,6},{5,7},{6,4},{7,5},{8,10},{9,11},{10,... | collective-permute-start | bytes 1228808 | tf_op jit(solution)/shard_map/ppermute | solution.py:147
  10.7 0.0 collective-permute-start.20
  10.7 5.8 %collective-permute-done.refs_1_ = bf16[34,32,128]{2,1,0:T(8,128)(2,1)S(1)} collective-permute-done((bf16[34,32,128]{2,1,0:T(8,128)(2,1)S(1)}, bf16[34,32,128]{2,1,0:T(8,128)(2,1)S(1)}, u32[]{:S(2)}, u32[]{:S(2)}) %collective-permute-start) | collective-permute-done | bytes 278560 | tf_op jit(solution)/shard_map/ppermute | solution.py:147
  16.4 10.5 %collective-permute-done.1.refs_2_ = bf16[34,32,128]{2,1,0:T(8,128)(2,1)S(1)} collective-permute-done((bf16[34,32,128]{2,1,0:T(8,128)(2,1)S(1)}, bf16[34,32,128]{2,1,0:T(8,128)(2,1)S(1)}, u32[]{:S(2)}, u32[]{:S(2)}) %collective-permute-start.1) | collective-permute-done | bytes 278560 | tf_op jit(solution)/shard_map/ppermute | solution.py:147
  26.9 0.0 collective-permute-done.2.refs_3_
  26.9 0.0 copy-done
  26.9 1.9 %shard_map.56 = (bf16[32,1280]{1,0:T(8,128)(2,1)S(1)}, bf16[32,1280]{1,0:T(8,128)(2,1)S(1)}, bf16[32,1280]{1,0:T(8,128)(2,1)S(1)}, bf16[32,1280]{1,0:T(8,128)(2,1)S(1)}) custom-call(s32[4,4,10]{2,1,0:T(4,128)S(1)} %bitcast.1, bf16[34,32,128]{2,1,0:T(8,128)(2,1)S(1)} %get-tuple-element.21.refs_0_, bf16[34,32,128]{2,1,0:T(8,128)(2,1)S(1)} %collective-permute-done.refs_1_, ...), custom_call_target="tpu_custom_call" | custom-call | flops 335544320 | bytes 1048576 | tf_op jit(solution)/shard_map/pallas_call | solution.py:355
  28.8 2.5 %collective-permute-start.11 = (bf16[32,1280]{1,0:T(8,128)(2,1)S(1)}, bf16[32,1280]{1,0:T(8,128)(2,1)S(1)}, u32[]{:S(2)}, u32[]{:S(2)}) collective-permute-start(bf16[32,1280]{1,0:T(8,128)(2,1)S(1)} %get-tuple-element.28), channel_id=1, source_target_pairs={{0,12},{4,8},{8,4},{12,0},{1,13},{5,9},{9,5},{13,1},{2,14},{6,10},... | collective-permute-start | bytes 245768 | tf_op jit(solution)/shard_map/ppermute | solution.py:147
  31.4 0.0 collective-permute-start.14
  31.4 5.1 %collective-permute-start.5 = (bf16[32,1280]{1,0:T(8,128)(2,1)S(1)}, bf16[32,1280]{1,0:T(8,128)(2,1)S(1)}, u32[]{:S(2)}, u32[]{:S(2)}) collective-permute-start(bf16[32,1280]{1,0:T(8,128)(2,1)S(1)} %get-tuple-element.26), channel_id=1, source_target_pairs={{0,4},{4,0},{8,12},{12,8},{1,5},{5,1},{9,13},{13,9},{2,6},{6,2},{1... | collective-permute-start | bytes 245768 | tf_op jit(solution)/shard_map/ppermute | solution.py:147
  36.5 0.0 collective-permute-done.11.refs_3_
  36.5 3.9 %collective-permute-start.8 = (bf16[32,1280]{1,0:T(8,128)(2,1)S(1)}, bf16[32,1280]{1,0:T(8,128)(2,1)S(1)}, u32[]{:S(2)}, u32[]{:S(2)}) collective-permute-start(bf16[32,1280]{1,0:T(8,128)(2,1)S(1)} %get-tuple-element.27), channel_id=1, source_target_pairs={{0,8},{4,12},{8,0},{12,4},{1,9},{5,13},{9,1},{13,5},{2,10},{6,14},... | collective-permute-start | bytes 245768 | tf_op jit(solution)/shard_map/ppermute | solution.py:147
  40.4 0.0 collective-permute-done.5.refs_1_
  40.4 1.5 %collective-permute-start.3 = (bf16[32,1280]{1,0:T(8,128)(2,1)S(1)}, bf16[32,1280]{1,0:T(8,128)(2,1)S(1)}, u32[]{:S(2)}, u32[]{:S(2)}) collective-permute-start(bf16[32,1280]{1,0:T(8,128)(2,1)S(1)} %get-tuple-element.25.refs_0_), channel_id=1, source_target_pairs={{0,2},{1,3},{2,0},{3,1},{4,6},{5,7},{6,4},{7,5},{8,10},{9,11},{10,... | collective-permute-start | bytes 245768 | tf_op jit(solution)/shard_map/ppermute | solution.py:147
  41.9 2.8 %collective-permute-done.8.refs_2_ = bf16[32,1280]{1,0:T(8,128)(2,1)S(1)} collective-permute-done((bf16[32,1280]{1,0:T(8,128)(2,1)S(1)}, bf16[32,1280]{1,0:T(8,128)(2,1)S(1)}, u32[]{:S(2)}, u32[]{:S(2)}) %collective-permute-start.8) | collective-permute-done | bytes 81952 | tf_op jit(solution)/shard_map/ppermute | solution.py:147
  44.7 0.1 collective-permute-start.15
  44.7 0.2 collective-permute-done.3.refs_0_
  44.9 1.4 %collective-permute-start.12 = (bf16[32,1280]{1,0:T(8,128)(2,1)S(1)}, bf16[32,1280]{1,0:T(8,128)(2,1)S(1)}, u32[]{:S(2)}, u32[]{:S(2)}) collective-permute-start(bf16[32,1280]{1,0:T(8,128)(2,1)S(1)} %collective-permute-done.11.refs_3_), channel_id=1, source_target_pairs={{0,2},{1,3},{2,0},{3,1},{4,6},{5,7},{6,4},{7,5},{8,10},{9,11},{10,... | collective-permute-start | bytes 245768 | tf_op jit(solution)/shard_map/ppermute | solution.py:147
  46.3 0.0 collective-permute-done.15.refs_4_
  46.3 0.6 collective-permute-start.6
  46.9 0.0 collective-permute-done.19.refs_8_
  46.9 1.4 %collective-permute-start.9 = (bf16[32,1280]{1,0:T(8,128)(2,1)S(1)}, bf16[32,1280]{1,0:T(8,128)(2,1)S(1)}, u32[]{:S(2)}, u32[]{:S(2)}) collective-permute-start(bf16[32,1280]{1,0:T(8,128)(2,1)S(1)} %collective-permute-done.8.refs_2_), channel_id=1, source_target_pairs={{0,2},{1,3},{2,0},{3,1},{4,6},{5,7},{6,4},{7,5},{8,10},{9,11},{10,... | collective-permute-start | bytes 245768 | tf_op jit(solution)/shard_map/ppermute | solution.py:147
  48.3 0.0 collective-permute-done.20.refs_9_
  48.3 0.0 collective-permute-start.16
  48.4 1.9 %collective-permute-done.12.refs_3_ = bf16[32,1280]{1,0:T(8,128)(2,1)S(1)} collective-permute-done((bf16[32,1280]{1,0:T(8,128)(2,1)S(1)}, bf16[32,1280]{1,0:T(8,128)(2,1)S(1)}, u32[]{:S(2)}, u32[]{:S(2)}) %collective-permute-start.12) | collective-permute-done | bytes 81952 | tf_op jit(solution)/shard_map/ppermute | solution.py:147
  50.2 0.0 collective-permute-start.17
  50.2 1.8 %collective-permute-done.6.refs_1_ = bf16[32,1280]{1,0:T(8,128)(2,1)S(1)} collective-permute-done((bf16[32,1280]{1,0:T(8,128)(2,1)S(1)}, bf16[32,1280]{1,0:T(8,128)(2,1)S(1)}, u32[]{:S(2)}, u32[]{:S(2)}) %collective-permute-start.6) | collective-permute-done | bytes 81952 | tf_op jit(solution)/shard_map/ppermute | solution.py:147
  52.0 0.0 collective-permute-start.18
  52.0 1.1 %collective-permute-done.9.refs_2_ = bf16[32,1280]{1,0:T(8,128)(2,1)S(1)} collective-permute-done((bf16[32,1280]{1,0:T(8,128)(2,1)S(1)}, bf16[32,1280]{1,0:T(8,128)(2,1)S(1)}, u32[]{:S(2)}, u32[]{:S(2)}) %collective-permute-start.9) | collective-permute-done | bytes 81952 | tf_op jit(solution)/shard_map/ppermute | solution.py:147
  53.0 0.0 collective-permute-start.4
  53.0 0.0 collective-permute-done.16.refs_5_
  53.0 0.5 collective-permute-start.10
  53.5 0.0 collective-permute-done.17.refs_6_
  53.6 0.1 collective-permute-start.13
  53.6 0.0 collective-permute-done.18.refs_7_
  53.6 0.4 collective-permute-start.7
  54.1 0.6 shard_map.58.refs_10_
  54.7 1.0 %shard_map.59.refs_5_ = f32[4,4,32,640]{3,2,1,0:T(8,128)S(1)} custom-call(bf16[32,1280]{1,0:T(8,128)(2,1)S(1)} %collective-permute-done.3.refs_0_, bf16[32,1280]{1,0:T(8,128)(2,1)S(1)} %collective-permute-done.6.refs_1_, bf16[32,1280]{1,0:T(8,128)(2,1)S(1)} %collective-permute-done.9.refs_2_, bf16[32,1280]{1,0:T(8,128)(2,1)S(1)} %collective-permute-done.12.refs_3_, ...), custom_call_target="tpu_custom_call" | custom-call | flops 419430400 | bytes 1048576 | tf_op jit(solution)/shard_map/pallas_call | solution.py:355
  55.7 0.0 collective-permute-done.14.refs_4_
  55.7 0.0 collective-permute-done.4.refs_0_
  55.8 0.0 collective-permute-done.10.refs_2_
  55.8 0.0 collective-permute-done.13.refs_3_
  55.8 0.0 collective-permute-done.7.refs_1_
  55.8 0.7 shard_map.60
  56.5 5.0 %collective-permute-start.21 = (bf16[4,32,640]{2,1,0:T(8,128)(2,1)S(1)}, bf16[4,32,640]{2,1,0:T(8,128)(2,1)S(1)}, u32[]{:S(2)}, u32[]{:S(2)}) collective-permute-start(bf16[4,32,640]{2,1,0:T(8,128)(2,1)S(1)} %get-tuple-element.34), channel_id=1, source_target_pairs={{0,4},{4,0},{8,12},{12,8},{1,5},{5,1},{9,13},{13,9},{2,6},{6,2},{1... | collective-permute-start | bytes 491528 | tf_op jit(solution)/shard_map/ppermute | solution.py:147
  61.5 0.0 collective-permute-start.22
  61.5 2.4 %collective-permute-start.23 = (bf16[4,32,640]{2,1,0:T(8,128)(2,1)S(1)}, bf16[4,32,640]{2,1,0:T(8,128)(2,1)S(1)}, u32[]{:S(2)}, u32[]{:S(2)}) collective-permute-start(bf16[4,32,640]{2,1,0:T(8,128)(2,1)S(1)} %get-tuple-element.36), channel_id=1, source_target_pairs={{0,12},{4,8},{8,4},{12,0},{1,13},{5,9},{9,5},{13,1},{2,14},{6,10},... | collective-permute-start | bytes 491528 | tf_op jit(solution)/shard_map/ppermute | solution.py:147
  64.0 4.3 %collective-permute-done.21 = bf16[4,32,640]{2,1,0:T(8,128)(2,1)S(1)} collective-permute-done((bf16[4,32,640]{2,1,0:T(8,128)(2,1)S(1)}, bf16[4,32,640]{2,1,0:T(8,128)(2,1)S(1)}, u32[]{:S(2)}, u32[]{:S(2)}) %collective-permute-start.21) | collective-permute-done | bytes 163872 | tf_op jit(solution)/shard_map/ppermute | solution.py:147
  68.2 8.3 %collective-permute-done.22 = bf16[4,32,640]{2,1,0:T(8,128)(2,1)S(1)} collective-permute-done((bf16[4,32,640]{2,1,0:T(8,128)(2,1)S(1)}, bf16[4,32,640]{2,1,0:T(8,128)(2,1)S(1)}, u32[]{:S(2)}, u32[]{:S(2)}) %collective-permute-start.22) | collective-permute-done | bytes 163872 | tf_op jit(solution)/shard_map/ppermute | solution.py:147
  76.5 0.0 collective-permute-done.23
  76.5 0.7 add_convert_fusion
Async XLA Ops:
  0.0 26.9 %copy-start = (s32[10,4,4]{0,2,1:T(4,128)S(1)}, s32[10,4,4]{0,2,1:T(4,128)}, u32[]{:S(2)}) copy-start(s32[10,4,4]{0,2,1:T(4,128)} %param.8) | copy-start | bytes 1924
  1.4 15.0 %collective-permute-start = (bf16[34,32,128]{2,1,0:T(8,128)(2,1)S(1)}, bf16[34,32,128]{2,1,0:T(8,128)(2,1)S(1)}, u32[]{:S(2)}, u32[]{:S(2)}) collective-permute-start(bf16[34,32,128]{2,1,0:T(8,128)(2,1)S(1)} %get-tuple-element.22), channel_id=1, source_target_pairs={{0,4},{4,0},{8,12},{12,8},{1,5},{5,1},{9,13},{13,9},{2,6},{6,2},{1... | collective-permute-start | bytes 835592 | tf_op jit(solution)/shard_map/ppermute | solution.py:147
  4.5 22.4 %collective-permute-start.1 = (bf16[34,32,128]{2,1,0:T(8,128)(2,1)S(1)}, bf16[34,32,128]{2,1,0:T(8,128)(2,1)S(1)}, u32[]{:S(2)}, u32[]{:S(2)}) collective-permute-start(bf16[34,32,128]{2,1,0:T(8,128)(2,1)S(1)} %get-tuple-element.23), channel_id=1, source_target_pairs={{0,8},{4,12},{8,0},{12,4},{1,9},{5,13},{9,1},{13,5},{2,10},{6,14},... | collective-permute-start | bytes 835592 | tf_op jit(solution)/shard_map/ppermute | solution.py:147
  7.1 19.8 %collective-permute-start.2 = (bf16[34,32,128]{2,1,0:T(8,128)(2,1)S(1)}, bf16[34,32,128]{2,1,0:T(8,128)(2,1)S(1)}, u32[]{:S(2)}, u32[]{:S(2)}) collective-permute-start(bf16[34,32,128]{2,1,0:T(8,128)(2,1)S(1)} %get-tuple-element.24), channel_id=1, source_target_pairs={{0,12},{4,8},{8,4},{12,0},{1,13},{5,9},{9,5},{13,1},{2,14},{6,10},... | collective-permute-start | bytes 835592 | tf_op jit(solution)/shard_map/ppermute | solution.py:147
  8.9 38.0 %collective-permute-start.19 = (bf16[10,32,640]{2,1,0:T(8,128)(2,1)S(1)}, bf16[10,32,640]{2,1,0:T(8,128)(2,1)S(1)}, u32[]{:S(2)}, u32[]{:S(2)}) collective-permute-start(bf16[10,32,640]{2,1,0:T(8,128)(2,1)S(1)} %get-tuple-element.30), channel_id=1, source_target_pairs={{0,2},{1,3},{2,0},{3,1},{4,6},{5,7},{6,4},{7,5},{8,10},{9,11},{10,... | collective-permute-start | bytes 1228808 | tf_op jit(solution)/shard_map/ppermute | solution.py:147
  10.7 37.7 %collective-permute-start.20 = (bf16[10,32,640]{2,1,0:T(8,128)(2,1)S(1)}, bf16[10,32,640]{2,1,0:T(8,128)(2,1)S(1)}, u32[]{:S(2)}, u32[]{:S(2)}) collective-permute-start(bf16[10,32,640]{2,1,0:T(8,128)(2,1)S(1)} %get-tuple-element.31), channel_id=1, source_target_pairs={{0,1},{1,0},{2,3},{3,2},{4,5},{5,4},{6,7},{7,6},{8,9},{9,8},{10,11... | collective-permute-start | bytes 1228808 | tf_op jit(solution)/shard_map/ppermute | solution.py:147
  28.8 7.7 %collective-permute-start.11 = (bf16[32,1280]{1,0:T(8,128)(2,1)S(1)}, bf16[32,1280]{1,0:T(8,128)(2,1)S(1)}, u32[]{:S(2)}, u32[]{:S(2)}) collective-permute-start(bf16[32,1280]{1,0:T(8,128)(2,1)S(1)} %get-tuple-element.28), channel_id=1, source_target_pairs={{0,12},{4,8},{8,4},{12,0},{1,13},{5,9},{9,5},{13,1},{2,14},{6,10},... | collective-permute-start | bytes 245768 | tf_op jit(solution)/shard_map/ppermute | solution.py:147
  31.4 24.4 %collective-permute-start.14 = (bf16[10,32,640]{2,1,0:T(8,128)(2,1)S(1)}, bf16[10,32,640]{2,1,0:T(8,128)(2,1)S(1)}, u32[]{:S(2)}, u32[]{:S(2)}) collective-permute-start(bf16[10,32,640]{2,1,0:T(8,128)(2,1)S(1)} %get-tuple-element.29), channel_id=1, source_target_pairs={{0,3},{1,2},{2,1},{3,0},{4,7},{5,6},{6,5},{7,4},{8,11},{9,10},{10,... | collective-permute-start | bytes 1228808 | tf_op jit(solution)/shard_map/ppermute | solution.py:147
  31.4 9.0 %collective-permute-start.5 = (bf16[32,1280]{1,0:T(8,128)(2,1)S(1)}, bf16[32,1280]{1,0:T(8,128)(2,1)S(1)}, u32[]{:S(2)}, u32[]{:S(2)}) collective-permute-start(bf16[32,1280]{1,0:T(8,128)(2,1)S(1)} %get-tuple-element.26), channel_id=1, source_target_pairs={{0,4},{4,0},{8,12},{12,8},{1,5},{5,1},{9,13},{13,9},{2,6},{6,2},{1... | collective-permute-start | bytes 245768 | tf_op jit(solution)/shard_map/ppermute | solution.py:147
  36.5 8.2 %collective-permute-start.8 = (bf16[32,1280]{1,0:T(8,128)(2,1)S(1)}, bf16[32,1280]{1,0:T(8,128)(2,1)S(1)}, u32[]{:S(2)}, u32[]{:S(2)}) collective-permute-start(bf16[32,1280]{1,0:T(8,128)(2,1)S(1)} %get-tuple-element.27), channel_id=1, source_target_pairs={{0,8},{4,12},{8,0},{12,4},{1,9},{5,13},{9,1},{13,5},{2,10},{6,14},... | collective-permute-start | bytes 245768 | tf_op jit(solution)/shard_map/ppermute | solution.py:147
  40.4 4.5 %collective-permute-start.3 = (bf16[32,1280]{1,0:T(8,128)(2,1)S(1)}, bf16[32,1280]{1,0:T(8,128)(2,1)S(1)}, u32[]{:S(2)}, u32[]{:S(2)}) collective-permute-start(bf16[32,1280]{1,0:T(8,128)(2,1)S(1)} %get-tuple-element.25.refs_0_), channel_id=1, source_target_pairs={{0,2},{1,3},{2,0},{3,1},{4,6},{5,7},{6,4},{7,5},{8,10},{9,11},{10,... | collective-permute-start | bytes 245768 | tf_op jit(solution)/shard_map/ppermute | solution.py:147
  44.7 1.7 %collective-permute-start.15 = (bf16[32,1280]{1,0:T(8,128)(2,1)S(1)}, bf16[32,1280]{1,0:T(8,128)(2,1)S(1)}, u32[]{:S(2)}, u32[]{:S(2)}) collective-permute-start(bf16[32,1280]{1,0:T(8,128)(2,1)S(1)} %get-tuple-element.25.refs_0_), channel_id=1, source_target_pairs={{0,1},{1,0},{2,3},{3,2},{4,5},{5,4},{6,7},{7,6},{8,9},{9,8},{10,11... | collective-permute-start | bytes 245768 | tf_op jit(solution)/shard_map/ppermute | solution.py:147
  44.9 5.3 %collective-permute-start.12 = (bf16[32,1280]{1,0:T(8,128)(2,1)S(1)}, bf16[32,1280]{1,0:T(8,128)(2,1)S(1)}, u32[]{:S(2)}, u32[]{:S(2)}) collective-permute-start(bf16[32,1280]{1,0:T(8,128)(2,1)S(1)} %collective-permute-done.11.refs_3_), channel_id=1, source_target_pairs={{0,2},{1,3},{2,0},{3,1},{4,6},{5,7},{6,4},{7,5},{8,10},{9,11},{10,... | collective-permute-start | bytes 245768 | tf_op jit(solution)/shard_map/ppermute | solution.py:147
  46.3 5.6 %collective-permute-start.6 = (bf16[32,1280]{1,0:T(8,128)(2,1)S(1)}, bf16[32,1280]{1,0:T(8,128)(2,1)S(1)}, u32[]{:S(2)}, u32[]{:S(2)}) collective-permute-start(bf16[32,1280]{1,0:T(8,128)(2,1)S(1)} %collective-permute-done.5.refs_1_), channel_id=1, source_target_pairs={{0,2},{1,3},{2,0},{3,1},{4,6},{5,7},{6,4},{7,5},{8,10},{9,11},{10,... | collective-permute-start | bytes 245768 | tf_op jit(solution)/shard_map/ppermute | solution.py:147
  46.9 6.1 %collective-permute-start.9 = (bf16[32,1280]{1,0:T(8,128)(2,1)S(1)}, bf16[32,1280]{1,0:T(8,128)(2,1)S(1)}, u32[]{:S(2)}, u32[]{:S(2)}) collective-permute-start(bf16[32,1280]{1,0:T(8,128)(2,1)S(1)} %collective-permute-done.8.refs_2_), channel_id=1, source_target_pairs={{0,2},{1,3},{2,0},{3,1},{4,6},{5,7},{6,4},{7,5},{8,10},{9,11},{10,... | collective-permute-start | bytes 245768 | tf_op jit(solution)/shard_map/ppermute | solution.py:147
  48.3 4.7 %collective-permute-start.16 = (bf16[32,1280]{1,0:T(8,128)(2,1)S(1)}, bf16[32,1280]{1,0:T(8,128)(2,1)S(1)}, u32[]{:S(2)}, u32[]{:S(2)}) collective-permute-start(bf16[32,1280]{1,0:T(8,128)(2,1)S(1)} %collective-permute-done.5.refs_1_), channel_id=1, source_target_pairs={{0,1},{1,0},{2,3},{3,2},{4,5},{5,4},{6,7},{7,6},{8,9},{9,8},{10,11... | collective-permute-start | bytes 245768 | tf_op jit(solution)/shard_map/ppermute | solution.py:147
  50.2 3.3 %collective-permute-start.17 = (bf16[32,1280]{1,0:T(8,128)(2,1)S(1)}, bf16[32,1280]{1,0:T(8,128)(2,1)S(1)}, u32[]{:S(2)}, u32[]{:S(2)}) collective-permute-start(bf16[32,1280]{1,0:T(8,128)(2,1)S(1)} %collective-permute-done.8.refs_2_), channel_id=1, source_target_pairs={{0,1},{1,0},{2,3},{3,2},{4,5},{5,4},{6,7},{7,6},{8,9},{9,8},{10,11... | collective-permute-start | bytes 245768 | tf_op jit(solution)/shard_map/ppermute | solution.py:147
  52.0 1.7 %collective-permute-start.18 = (bf16[32,1280]{1,0:T(8,128)(2,1)S(1)}, bf16[32,1280]{1,0:T(8,128)(2,1)S(1)}, u32[]{:S(2)}, u32[]{:S(2)}) collective-permute-start(bf16[32,1280]{1,0:T(8,128)(2,1)S(1)} %collective-permute-done.11.refs_3_), channel_id=1, source_target_pairs={{0,1},{1,0},{2,3},{3,2},{4,5},{5,4},{6,7},{7,6},{8,9},{9,8},{10,11... | collective-permute-start | bytes 245768 | tf_op jit(solution)/shard_map/ppermute | solution.py:147
  53.0 2.7 %collective-permute-start.4 = (bf16[32,1280]{1,0:T(8,128)(2,1)S(1)}, bf16[32,1280]{1,0:T(8,128)(2,1)S(1)}, u32[]{:S(2)}, u32[]{:S(2)}) collective-permute-start(bf16[32,1280]{1,0:T(8,128)(2,1)S(1)} %collective-permute-done.3.refs_0_), channel_id=1, source_target_pairs={{0,1},{1,0},{2,3},{3,2},{4,5},{5,4},{6,7},{7,6},{8,9},{9,8},{10,11... | collective-permute-start | bytes 245768 | tf_op jit(solution)/shard_map/ppermute | solution.py:147
  53.0 2.7 %collective-permute-start.10 = (bf16[32,1280]{1,0:T(8,128)(2,1)S(1)}, bf16[32,1280]{1,0:T(8,128)(2,1)S(1)}, u32[]{:S(2)}, u32[]{:S(2)}) collective-permute-start(bf16[32,1280]{1,0:T(8,128)(2,1)S(1)} %collective-permute-done.9.refs_2_), channel_id=1, source_target_pairs={{0,1},{1,0},{2,3},{3,2},{4,5},{5,4},{6,7},{7,6},{8,9},{9,8},{10,11... | collective-permute-start | bytes 245768 | tf_op jit(solution)/shard_map/ppermute | solution.py:147
  53.6 2.2 %collective-permute-start.13 = (bf16[32,1280]{1,0:T(8,128)(2,1)S(1)}, bf16[32,1280]{1,0:T(8,128)(2,1)S(1)}, u32[]{:S(2)}, u32[]{:S(2)}) collective-permute-start(bf16[32,1280]{1,0:T(8,128)(2,1)S(1)} %collective-permute-done.12.refs_3_), channel_id=1, source_target_pairs={{0,1},{1,0},{2,3},{3,2},{4,5},{5,4},{6,7},{7,6},{8,9},{9,8},{10,11... | collective-permute-start | bytes 245768 | tf_op jit(solution)/shard_map/ppermute | solution.py:147
  53.6 2.2 %collective-permute-start.7 = (bf16[32,1280]{1,0:T(8,128)(2,1)S(1)}, bf16[32,1280]{1,0:T(8,128)(2,1)S(1)}, u32[]{:S(2)}, u32[]{:S(2)}) collective-permute-start(bf16[32,1280]{1,0:T(8,128)(2,1)S(1)} %collective-permute-done.6.refs_1_), channel_id=1, source_target_pairs={{0,1},{1,0},{2,3},{3,2},{4,5},{5,4},{6,7},{7,6},{8,9},{9,8},{10,11... | collective-permute-start | bytes 245768 | tf_op jit(solution)/shard_map/ppermute | solution.py:147
  56.5 11.7 %collective-permute-start.21 = (bf16[4,32,640]{2,1,0:T(8,128)(2,1)S(1)}, bf16[4,32,640]{2,1,0:T(8,128)(2,1)S(1)}, u32[]{:S(2)}, u32[]{:S(2)}) collective-permute-start(bf16[4,32,640]{2,1,0:T(8,128)(2,1)S(1)} %get-tuple-element.34), channel_id=1, source_target_pairs={{0,4},{4,0},{8,12},{12,8},{1,5},{5,1},{9,13},{13,9},{2,6},{6,2},{1... | collective-permute-start | bytes 491528 | tf_op jit(solution)/shard_map/ppermute | solution.py:147
  61.5 15.0 %collective-permute-start.22 = (bf16[4,32,640]{2,1,0:T(8,128)(2,1)S(1)}, bf16[4,32,640]{2,1,0:T(8,128)(2,1)S(1)}, u32[]{:S(2)}, u32[]{:S(2)}) collective-permute-start(bf16[4,32,640]{2,1,0:T(8,128)(2,1)S(1)} %get-tuple-element.35), channel_id=1, source_target_pairs={{0,8},{4,12},{8,0},{12,4},{1,9},{5,13},{9,1},{13,5},{2,10},{6,14},... | collective-permute-start | bytes 491528 | tf_op jit(solution)/shard_map/ppermute | solution.py:147
  61.5 15.0 %collective-permute-start.23 = (bf16[4,32,640]{2,1,0:T(8,128)(2,1)S(1)}, bf16[4,32,640]{2,1,0:T(8,128)(2,1)S(1)}, u32[]{:S(2)}, u32[]{:S(2)}) collective-permute-start(bf16[4,32,640]{2,1,0:T(8,128)(2,1)S(1)} %get-tuple-element.36), channel_id=1, source_target_pairs={{0,12},{4,8},{8,4},{12,0},{1,13},{5,9},{9,5},{13,1},{2,14},{6,10},... | collective-permute-start | bytes 491528 | tf_op jit(solution)/shard_map/ppermute | solution.py:147

commit v5 on v4

--- a/solution.py
+++ b/solution.py
@@ -195,9 +195,9 @@
         copy.wait()
 
 
-def pack_kernel(z, q_hbm, k_hbm, v_hbm, *refs):
-    out_refs = refs[: z.ranks]
-    q_ref, k_ref, v_ref, sems = refs[z.ranks :]
+def pack_kernel(z, flips, q_hbm, k_hbm, v_hbm, *refs):
+    out_refs = dict(zip(flips, refs))
+    q_ref, k_ref, v_ref, sems = refs[len(flips) :]
     me = lax.axis_index("seq")
     arrays = ((q_hbm, q_ref, 0), (k_hbm, k_ref, z.q_units), (v_hbm, v_ref, z.q_units + z.kv_units))
     copies = []
@@ -209,13 +209,13 @@
     for i, (_, ref, begin) in enumerate(arrays):
         for b in range(z.blocks):
             copies[i * z.blocks + b].wait()
-            for flip in range(z.ranks):
+            for flip in flips:
                 for slot in range(z.whole):
                     cols = pl.ds(aligned(slot * z.ranks + (me ^ flip), z.hd), z.hd)
                     out_refs[flip][begin + slot * z.blocks + b] = ref[b, :, cols]
         if z.rest:
             count = z.strip if i == 0 else z.blocks
-            for flip in range(z.ranks):
+            for flip in flips:
                 peer = me ^ flip
                 cols = pl.ds(aligned(z.whole * z.ranks + peer // z.sharers, z.hd), z.hd)
                 first = (peer % z.sharers) * z.strip if i == 0 else 0
@@ -375,13 +375,19 @@
 def stationary_plan(z, queries, key_vectors, value_vectors, block_mask, out_weight):
     bf16 = jnp.bfloat16
     shape = jax.ShapeDtypeStruct
-    packed = local_call(
-        functools.partial(pack_kernel, z),
-        [shape((z.units, z.rows, z.hd), bf16)] * z.ranks,
-        scratch=[pltpu.VMEM(queries.shape, bf16)] * 3
-        + [pltpu.SemaphoreType.DMA((3 * z.blocks,))],
-        places=[pltpu.HBM] * 3,
-    )(queries, key_vectors, value_vectors)
+
+    def pack(flips):
+        return local_call(
+            functools.partial(pack_kernel, z, flips),
+            [shape((z.units, z.rows, z.hd), bf16)] * len(flips),
+            scratch=[pltpu.VMEM(queries.shape, bf16)] * 3
+            + [pltpu.SemaphoreType.DMA((3 * z.blocks,))],
+            places=[pltpu.HBM] * 3,
+        )(queries, key_vectors, value_vectors)
+
+    last = z.ranks - 1
+    first_out = pack((last,))
+    packed = list(pack(tuple(range(last)))) + list(first_out)
     parts = exchange_all(packed, "seq")
     sliced = local_call(
         functools.partial(weight_kernel, z),

time: 77.5 us -> 77.6 us (level)
  waiting for transfers between devices: 36.5 us -> 35 us
  Pallas kernels: 7.43 us -> 8.81 us
    ppermute x24, waiting for transfers between devices: 36.5 us -> 35 us  [exchange(): return lax.ppermute(array, axis, [(i, i ^ flip) for i in range(size)])]
    pallas_call x6 -> x7, Pallas kernels: 7.43 us -> 8.81 us  [call(): pl.pallas_call(kernel, out_shape=outs, in_specs=[pl.BlockSpec(memory_spac...]
  transfers between devices with their start and end apart: 24 -> 24, of which waited for: 9 -> 9; matrix products, arithmetic and copies ran while one was open for 0% -> 0% of each run, Pallas kernels for 7% -> 9%
where the time goes in v5:
time: 77.6 us; the launch traced here: 77.2 us
  waiting for transfers between devices  35 us (45%)
  starting transfers between devices  32.5 us (42%)
  Pallas kernels  8.81 us (11%)
    ppermute x24, waiting for transfers between devices, exchange(): return lax.ppermute(array, axis, [(i, i ^ flip) for i in range(size)])  35 us
    ppermute x24, starting transfers between devices, exchange(): return lax.ppermute(array, axis, [(i, i ^ flip) for i in range(size)])  32.5 us
    pallas_call x7, Pallas kernels, call(): pl.pallas_call(kernel, out_shape=outs, in_specs=[pl.BlockSpec(memory_spac...  8.81 us
  transfers between devices with their start and end apart: 24, of which 9 were waited for; matrix products, arithmetic and copies ran while one was open for 0% of the time, Pallas kernels for 9%

profile of v5, /device:TPU:0, one launch (start us, length us, event | category | flops | bytes accessed | tf_op | source)
XLA Modules:
  0.0 77.2 jit_solution(7332095866604469592)
XLA Ops:
  0.0 1.4 %shard_map.55 = (bf16[34,32,128]{2,1,0:T(8,128)(2,1)S(1)}, bf16[34,32,128]{2,1,0:T(8,128)(2,1)S(1)}, bf16[34,32,128]{2,1,0:T(8,128)(2,1)S(1)}) custom-call(bf16[4,32,1280]{2,1,0:T(8,128)(2,1)} %q_hbm.3, bf16[4,32,1280]{2,1,0:T(8,128)(2,1)} %k_hbm.3, bf16[4,32,1280]{2,1,0:T(8,128)(2,1)} %v_hbm.3), custom_call_target="tpu_custom_call" | custom-call | flops 1048576 | bytes 1048576 | tf_op jit(solution)/shard_map/pallas_call | solution.py:355
  1.4 3.1 %collective-permute-start = (bf16[34,32,128]{2,1,0:T(8,128)(2,1)S(1)}, bf16[34,32,128]{2,1,0:T(8,128)(2,1)S(1)}, u32[]{:S(2)}, u32[]{:S(2)}) collective-permute-start(bf16[34,32,128]{2,1,0:T(8,128)(2,1)S(1)} %get-tuple-element.21), channel_id=1, source_target_pairs={{0,4},{4,0},{8,12},{12,8},{1,5},{5,1},{9,13},{13,9},{2,6},{6,2},{1... | collective-permute-start | bytes 835592 | tf_op jit(solution)/shard_map/ppermute | solution.py:147
  4.5 0.0 copy-start
  4.5 2.6 %collective-permute-start.1 = (bf16[34,32,128]{2,1,0:T(8,128)(2,1)S(1)}, bf16[34,32,128]{2,1,0:T(8,128)(2,1)S(1)}, u32[]{:S(2)}, u32[]{:S(2)}) collective-permute-start(bf16[34,32,128]{2,1,0:T(8,128)(2,1)S(1)} %get-tuple-element.22), channel_id=1, source_target_pairs={{0,8},{4,12},{8,0},{12,4},{1,9},{5,13},{9,1},{13,5},{2,10},{6,14},... | collective-permute-start | bytes 835592 | tf_op jit(solution)/shard_map/ppermute | solution.py:147
  7.1 1.4 %shard_map.56 = bf16[34,32,128]{2,1,0:T(8,128)(2,1)S(1)} custom-call(bf16[4,32,1280]{2,1,0:T(8,128)(2,1)} %q_hbm.3, bf16[4,32,1280]{2,1,0:T(8,128)(2,1)} %k_hbm.3, bf16[4,32,1280]{2,1,0:T(8,128)(2,1)} %v_hbm.3), custom_call_target="tpu_custom_call" | custom-call | flops 1048576 | bytes 1048576 | tf_op jit(solution)/shard_map/pallas_call | solution.py:355
  8.5 0.1 collective-permute-start.2
  8.6 1.7 %shard_map.58 = (bf16[10,32,640]{2,1,0:T(8,128)(2,1)S(1)}, bf16[10,32,640]{2,1,0:T(8,128)(2,1)S(1)}, bf16[10,32,640]{2,1,0:T(8,128)(2,1)S(1)}, bf16[10,32,640]{2,1,0:T(8,128)(2,1)S(1)}) custom-call(bf16[10,32,2560]{2,1,0:T(8,128)(2,1)} %w_hbm.1), custom_call_target="tpu_custom_call" | custom-call | flops 1048576 | bytes 1048576 | tf_op jit(solution)/shard_map/pallas_call | solution.py:355
  10.3 1.7 %collective-permute-start.19 = (bf16[10,32,640]{2,1,0:T(8,128)(2,1)S(1)}, bf16[10,32,640]{2,1,0:T(8,128)(2,1)S(1)}, u32[]{:S(2)}, u32[]{:S(2)}) collective-permute-start(bf16[10,32,640]{2,1,0:T(8,128)(2,1)S(1)} %get-tuple-element.28), channel_id=1, source_target_pairs={{0,2},{1,3},{2,0},{3,1},{4,6},{5,7},{6,4},{7,5},{8,10},{9,11},{10,... | collective-permute-start | bytes 1228808 | tf_op jit(solution)/shard_map/ppermute | solution.py:147
  12.1 0.0 collective-permute-start.20
  12.1 4.3 %collective-permute-done.refs_1_ = bf16[34,32,128]{2,1,0:T(8,128)(2,1)S(1)} collective-permute-done((bf16[34,32,128]{2,1,0:T(8,128)(2,1)S(1)}, bf16[34,32,128]{2,1,0:T(8,128)(2,1)S(1)}, u32[]{:S(2)}, u32[]{:S(2)}) %collective-permute-start) | collective-permute-done | bytes 278560 | tf_op jit(solution)/shard_map/ppermute | solution.py:147
  16.4 10.5 %collective-permute-done.1.refs_2_ = bf16[34,32,128]{2,1,0:T(8,128)(2,1)S(1)} collective-permute-done((bf16[34,32,128]{2,1,0:T(8,128)(2,1)S(1)}, bf16[34,32,128]{2,1,0:T(8,128)(2,1)S(1)}, u32[]{:S(2)}, u32[]{:S(2)}) %collective-permute-start.1) | collective-permute-done | bytes 278560 | tf_op jit(solution)/shard_map/ppermute | solution.py:147
  26.9 0.0 collective-permute-done.2.refs_3_
  26.9 0.0 copy-done
  26.9 1.9 %shard_map.57 = (bf16[32,1280]{1,0:T(8,128)(2,1)S(1)}, bf16[32,1280]{1,0:T(8,128)(2,1)S(1)}, bf16[32,1280]{1,0:T(8,128)(2,1)S(1)}, bf16[32,1280]{1,0:T(8,128)(2,1)S(1)}) custom-call(s32[4,4,10]{2,1,0:T(4,128)S(1)} %bitcast.1, bf16[34,32,128]{2,1,0:T(8,128)(2,1)S(1)} %get-tuple-element.20.refs_0_, bf16[34,32,128]{2,1,0:T(8,128)(2,1)S(1)} %collective-permute-done.refs_1_, ...), custom_call_target="tpu_custom_call" | custom-call | flops 335544320 | bytes 1048576 | tf_op jit(solution)/shard_map/pallas_call | solution.py:355
  28.8 2.6 %collective-permute-start.11 = (bf16[32,1280]{1,0:T(8,128)(2,1)S(1)}, bf16[32,1280]{1,0:T(8,128)(2,1)S(1)}, u32[]{:S(2)}, u32[]{:S(2)}) collective-permute-start(bf16[32,1280]{1,0:T(8,128)(2,1)S(1)} %get-tuple-element.26), channel_id=1, source_target_pairs={{0,12},{4,8},{8,4},{12,0},{1,13},{5,9},{9,5},{13,1},{2,14},{6,10},... | collective-permute-start | bytes 245768 | tf_op jit(solution)/shard_map/ppermute | solution.py:147
  31.4 0.0 collective-permute-start.14
  31.4 5.1 %collective-permute-start.5 = (bf16[32,1280]{1,0:T(8,128)(2,1)S(1)}, bf16[32,1280]{1,0:T(8,128)(2,1)S(1)}, u32[]{:S(2)}, u32[]{:S(2)}) collective-permute-start(bf16[32,1280]{1,0:T(8,128)(2,1)S(1)} %get-tuple-element.24), channel_id=1, source_target_pairs={{0,4},{4,0},{8,12},{12,8},{1,5},{5,1},{9,13},{13,9},{2,6},{6,2},{1... | collective-permute-start | bytes 245768 | tf_op jit(solution)/shard_map/ppermute | solution.py:147
  36.5 0.0 collective-permute-done.11.refs_3_
  36.5 3.9 %collective-permute-start.8 = (bf16[32,1280]{1,0:T(8,128)(2,1)S(1)}, bf16[32,1280]{1,0:T(8,128)(2,1)S(1)}, u32[]{:S(2)}, u32[]{:S(2)}) collective-permute-start(bf16[32,1280]{1,0:T(8,128)(2,1)S(1)} %get-tuple-element.25), channel_id=1, source_target_pairs={{0,8},{4,12},{8,0},{12,4},{1,9},{5,13},{9,1},{13,5},{2,10},{6,14},... | collective-permute-start | bytes 245768 | tf_op jit(solution)/shard_map/ppermute | solution.py:147
  40.4 0.0 collective-permute-done.5.refs_1_
  40.4 1.5 %collective-permute-start.3 = (bf16[32,1280]{1,0:T(8,128)(2,1)S(1)}, bf16[32,1280]{1,0:T(8,128)(2,1)S(1)}, u32[]{:S(2)}, u32[]{:S(2)}) collective-permute-start(bf16[32,1280]{1,0:T(8,128)(2,1)S(1)} %get-tuple-element.23.refs_0_), channel_id=1, source_target_pairs={{0,2},{1,3},{2,0},{3,1},{4,6},{5,7},{6,4},{7,5},{8,10},{9,11},{10,... | collective-permute-start | bytes 245768 | tf_op jit(solution)/shard_map/ppermute | solution.py:147
  41.9 2.8 %collective-permute-done.8.refs_2_ = bf16[32,1280]{1,0:T(8,128)(2,1)S(1)} collective-permute-done((bf16[32,1280]{1,0:T(8,128)(2,1)S(1)}, bf16[32,1280]{1,0:T(8,128)(2,1)S(1)}, u32[]{:S(2)}, u32[]{:S(2)}) %collective-permute-start.8) | collective-permute-done | bytes 81952 | tf_op jit(solution)/shard_map/ppermute | solution.py:147
  44.6 0.1 collective-permute-start.15
  44.7 0.2 collective-permute-done.3.refs_0_
  44.9 1.4 %collective-permute-start.12 = (bf16[32,1280]{1,0:T(8,128)(2,1)S(1)}, bf16[32,1280]{1,0:T(8,128)(2,1)S(1)}, u32[]{:S(2)}, u32[]{:S(2)}) collective-permute-start(bf16[32,1280]{1,0:T(8,128)(2,1)S(1)} %collective-permute-done.11.refs_3_), channel_id=1, source_target_pairs={{0,2},{1,3},{2,0},{3,1},{4,6},{5,7},{6,4},{7,5},{8,10},{9,11},{10,... | collective-permute-start | bytes 245768 | tf_op jit(solution)/shard_map/ppermute | solution.py:147
  46.3 0.0 collective-permute-done.15.refs_4_
  46.3 0.6 collective-permute-start.6
  46.9 0.0 collective-permute-done.19.refs_8_
  46.9 1.4 %collective-permute-start.9 = (bf16[32,1280]{1,0:T(8,128)(2,1)S(1)}, bf16[32,1280]{1,0:T(8,128)(2,1)S(1)}, u32[]{:S(2)}, u32[]{:S(2)}) collective-permute-start(bf16[32,1280]{1,0:T(8,128)(2,1)S(1)} %collective-permute-done.8.refs_2_), channel_id=1, source_target_pairs={{0,2},{1,3},{2,0},{3,1},{4,6},{5,7},{6,4},{7,5},{8,10},{9,11},{10,... | collective-permute-start | bytes 245768 | tf_op jit(solution)/shard_map/ppermute | solution.py:147
  48.3 0.0 collective-permute-done.20.refs_9_
  48.3 0.0 collective-permute-start.16
  48.3 1.9 %collective-permute-done.12.refs_3_ = bf16[32,1280]{1,0:T(8,128)(2,1)S(1)} collective-permute-done((bf16[32,1280]{1,0:T(8,128)(2,1)S(1)}, bf16[32,1280]{1,0:T(8,128)(2,1)S(1)}, u32[]{:S(2)}, u32[]{:S(2)}) %collective-permute-start.12) | collective-permute-done | bytes 81952 | tf_op jit(solution)/shard_map/ppermute | solution.py:147
  50.2 0.0 collective-permute-start.17
  50.2 1.8 %collective-permute-done.6.refs_1_ = bf16[32,1280]{1,0:T(8,128)(2,1)S(1)} collective-permute-done((bf16[32,1280]{1,0:T(8,128)(2,1)S(1)}, bf16[32,1280]{1,0:T(8,128)(2,1)S(1)}, u32[]{:S(2)}, u32[]{:S(2)}) %collective-permute-start.6) | collective-permute-done | bytes 81952 | tf_op jit(solution)/shard_map/ppermute | solution.py:147
  51.9 0.0 collective-permute-start.18
  51.9 1.1 %collective-permute-done.9.refs_2_ = bf16[32,1280]{1,0:T(8,128)(2,1)S(1)} collective-permute-done((bf16[32,1280]{1,0:T(8,128)(2,1)S(1)}, bf16[32,1280]{1,0:T(8,128)(2,1)S(1)}, u32[]{:S(2)}, u32[]{:S(2)}) %collective-permute-start.9) | collective-permute-done | bytes 81952 | tf_op jit(solution)/shard_map/ppermute | solution.py:147
  53.0 0.0 collective-permute-start.4
  53.0 0.0 collective-permute-done.16.refs_5_
  53.0 0.5 collective-permute-start.10
  53.5 0.0 collective-permute-done.17.refs_6_
  53.5 0.1 collective-permute-start.13
  53.6 0.0 collective-permute-done.18.refs_7_
  53.6 0.4 collective-permute-start.7
  54.0 0.6 shard_map.59.refs_10_
  54.7 1.0 %shard_map.60.refs_5_ = f32[4,4,32,640]{3,2,1,0:T(8,128)S(1)} custom-call(bf16[32,1280]{1,0:T(8,128)(2,1)S(1)} %collective-permute-done.3.refs_0_, bf16[32,1280]{1,0:T(8,128)(2,1)S(1)} %collective-permute-done.6.refs_1_, bf16[32,1280]{1,0:T(8,128)(2,1)S(1)} %collective-permute-done.9.refs_2_, bf16[32,1280]{1,0:T(8,128)(2,1)S(1)} %collective-permute-done.12.refs_3_, ...), custom_call_target="tpu_custom_call" | custom-call | flops 419430400 | bytes 1048576 | tf_op jit(solution)/shard_map/pallas_call | solution.py:355
  55.7 0.0 collective-permute-done.14.refs_4_
  55.7 0.0 collective-permute-done.4.refs_0_
  55.7 0.0 collective-permute-done.10.refs_2_
  55.7 0.0 collective-permute-done.13.refs_3_
  55.8 0.0 collective-permute-done.7.refs_1_
  55.8 0.7 shard_map.61
  56.5 5.0 %collective-permute-start.21 = (bf16[4,32,640]{2,1,0:T(8,128)(2,1)S(1)}, bf16[4,32,640]{2,1,0:T(8,128)(2,1)S(1)}, u32[]{:S(2)}, u32[]{:S(2)}) collective-permute-start(bf16[4,32,640]{2,1,0:T(8,128)(2,1)S(1)} %get-tuple-element.32), channel_id=1, source_target_pairs={{0,4},{4,0},{8,12},{12,8},{1,5},{5,1},{9,13},{13,9},{2,6},{6,2},{1... | collective-permute-start | bytes 491528 | tf_op jit(solution)/shard_map/ppermute | solution.py:147
  61.5 0.0 collective-permute-start.22
  61.5 2.4 %collective-permute-start.23 = (bf16[4,32,640]{2,1,0:T(8,128)(2,1)S(1)}, bf16[4,32,640]{2,1,0:T(8,128)(2,1)S(1)}, u32[]{:S(2)}, u32[]{:S(2)}) collective-permute-start(bf16[4,32,640]{2,1,0:T(8,128)(2,1)S(1)} %get-tuple-element.34), channel_id=1, source_target_pairs={{0,12},{4,8},{8,4},{12,0},{1,13},{5,9},{9,5},{13,1},{2,14},{6,10},... | collective-permute-start | bytes 491528 | tf_op jit(solution)/shard_map/ppermute | solution.py:147
  63.9 4.3 %collective-permute-done.21 = bf16[4,32,640]{2,1,0:T(8,128)(2,1)S(1)} collective-permute-done((bf16[4,32,640]{2,1,0:T(8,128)(2,1)S(1)}, bf16[4,32,640]{2,1,0:T(8,128)(2,1)S(1)}, u32[]{:S(2)}, u32[]{:S(2)}) %collective-permute-start.21) | collective-permute-done | bytes 163872 | tf_op jit(solution)/shard_map/ppermute | solution.py:147
  68.2 8.3 %collective-permute-done.22 = bf16[4,32,640]{2,1,0:T(8,128)(2,1)S(1)} collective-permute-done((bf16[4,32,640]{2,1,0:T(8,128)(2,1)S(1)}, bf16[4,32,640]{2,1,0:T(8,128)(2,1)S(1)}, u32[]{:S(2)}, u32[]{:S(2)}) %collective-permute-start.22) | collective-permute-done | bytes 163872 | tf_op jit(solution)/shard_map/ppermute | solution.py:147
  76.5 0.0 collective-permute-done.23
  76.5 0.7 add_convert_fusion
Async XLA Ops:
  1.4 15.0 %collective-permute-start = (bf16[34,32,128]{2,1,0:T(8,128)(2,1)S(1)}, bf16[34,32,128]{2,1,0:T(8,128)(2,1)S(1)}, u32[]{:S(2)}, u32[]{:S(2)}) collective-permute-start(bf16[34,32,128]{2,1,0:T(8,128)(2,1)S(1)} %get-tuple-element.21), channel_id=1, source_target_pairs={{0,4},{4,0},{8,12},{12,8},{1,5},{5,1},{9,13},{13,9},{2,6},{6,2},{1... | collective-permute-start | bytes 835592 | tf_op jit(solution)/shard_map/ppermute | solution.py:147
  4.5 22.4 %copy-start = (s32[10,4,4]{0,2,1:T(4,128)S(1)}, s32[10,4,4]{0,2,1:T(4,128)}, u32[]{:S(2)}) copy-start(s32[10,4,4]{0,2,1:T(4,128)} %param.8) | copy-start | bytes 1924
  4.5 22.4 %collective-permute-start.1 = (bf16[34,32,128]{2,1,0:T(8,128)(2,1)S(1)}, bf16[34,32,128]{2,1,0:T(8,128)(2,1)S(1)}, u32[]{:S(2)}, u32[]{:S(2)}) collective-permute-start(bf16[34,32,128]{2,1,0:T(8,128)(2,1)S(1)} %get-tuple-element.22), channel_id=1, source_target_pairs={{0,8},{4,12},{8,0},{12,4},{1,9},{5,13},{9,1},{13,5},{2,10},{6,14},... | collective-permute-start | bytes 835592 | tf_op jit(solution)/shard_map/ppermute | solution.py:147
  8.5 18.4 %collective-permute-start.2 = (bf16[34,32,128]{2,1,0:T(8,128)(2,1)S(1)}, bf16[34,32,128]{2,1,0:T(8,128)(2,1)S(1)}, u32[]{:S(2)}, u32[]{:S(2)}) collective-permute-start(bf16[34,32,128]{2,1,0:T(8,128)(2,1)S(1)} %shard_map.56), channel_id=1, source_target_pairs={{0,12},{4,8},{8,4},{12,0},{1,13},{5,9},{9,5},{13,1},{2,14},{6,10},... | collective-permute-start | bytes 835592 | tf_op jit(solution)/shard_map/ppermute | solution.py:147
  10.3 36.6 %collective-permute-start.19 = (bf16[10,32,640]{2,1,0:T(8,128)(2,1)S(1)}, bf16[10,32,640]{2,1,0:T(8,128)(2,1)S(1)}, u32[]{:S(2)}, u32[]{:S(2)}) collective-permute-start(bf16[10,32,640]{2,1,0:T(8,128)(2,1)S(1)} %get-tuple-element.28), channel_id=1, source_target_pairs={{0,2},{1,3},{2,0},{3,1},{4,6},{5,7},{6,4},{7,5},{8,10},{9,11},{10,... | collective-permute-start | bytes 1228808 | tf_op jit(solution)/shard_map/ppermute | solution.py:147
  12.1 36.3 %collective-permute-start.20 = (bf16[10,32,640]{2,1,0:T(8,128)(2,1)S(1)}, bf16[10,32,640]{2,1,0:T(8,128)(2,1)S(1)}, u32[]{:S(2)}, u32[]{:S(2)}) collective-permute-start(bf16[10,32,640]{2,1,0:T(8,128)(2,1)S(1)} %get-tuple-element.29), channel_id=1, source_target_pairs={{0,1},{1,0},{2,3},{3,2},{4,5},{5,4},{6,7},{7,6},{8,9},{9,8},{10,11... | collective-permute-start | bytes 1228808 | tf_op jit(solution)/shard_map/ppermute | solution.py:147
  28.8 7.7 %collective-permute-start.11 = (bf16[32,1280]{1,0:T(8,128)(2,1)S(1)}, bf16[32,1280]{1,0:T(8,128)(2,1)S(1)}, u32[]{:S(2)}, u32[]{:S(2)}) collective-permute-start(bf16[32,1280]{1,0:T(8,128)(2,1)S(1)} %get-tuple-element.26), channel_id=1, source_target_pairs={{0,12},{4,8},{8,4},{12,0},{1,13},{5,9},{9,5},{13,1},{2,14},{6,10},... | collective-permute-start | bytes 245768 | tf_op jit(solution)/shard_map/ppermute | solution.py:147
  31.4 24.4 %collective-permute-start.14 = (bf16[10,32,640]{2,1,0:T(8,128)(2,1)S(1)}, bf16[10,32,640]{2,1,0:T(8,128)(2,1)S(1)}, u32[]{:S(2)}, u32[]{:S(2)}) collective-permute-start(bf16[10,32,640]{2,1,0:T(8,128)(2,1)S(1)} %get-tuple-element.27), channel_id=1, source_target_pairs={{0,3},{1,2},{2,1},{3,0},{4,7},{5,6},{6,5},{7,4},{8,11},{9,10},{10,... | collective-permute-start | bytes 1228808 | tf_op jit(solution)/shard_map/ppermute | solution.py:147
  31.4 9.0 %collective-permute-start.5 = (bf16[32,1280]{1,0:T(8,128)(2,1)S(1)}, bf16[32,1280]{1,0:T(8,128)(2,1)S(1)}, u32[]{:S(2)}, u32[]{:S(2)}) collective-permute-start(bf16[32,1280]{1,0:T(8,128)(2,1)S(1)} %get-tuple-element.24), channel_id=1, source_target_pairs={{0,4},{4,0},{8,12},{12,8},{1,5},{5,1},{9,13},{13,9},{2,6},{6,2},{1... | collective-permute-start | bytes 245768 | tf_op jit(solution)/shard_map/ppermute | solution.py:147
  36.5 8.1 %collective-permute-start.8 = (bf16[32,1280]{1,0:T(8,128)(2,1)S(1)}, bf16[32,1280]{1,0:T(8,128)(2,1)S(1)}, u32[]{:S(2)}, u32[]{:S(2)}) collective-permute-start(bf16[32,1280]{1,0:T(8,128)(2,1)S(1)} %get-tuple-element.25), channel_id=1, source_target_pairs={{0,8},{4,12},{8,0},{12,4},{1,9},{5,13},{9,1},{13,5},{2,10},{6,14},... | collective-permute-start | bytes 245768 | tf_op jit(solution)/shard_map/ppermute | solution.py:147
  40.4 4.5 %collective-permute-start.3 = (bf16[32,1280]{1,0:T(8,128)(2,1)S(1)}, bf16[32,1280]{1,0:T(8,128)(2,1)S(1)}, u32[]{:S(2)}, u32[]{:S(2)}) collective-permute-start(bf16[32,1280]{1,0:T(8,128)(2,1)S(1)} %get-tuple-element.23.refs_0_), channel_id=1, source_target_pairs={{0,2},{1,3},{2,0},{3,1},{4,6},{5,7},{6,4},{7,5},{8,10},{9,11},{10,... | collective-permute-start | bytes 245768 | tf_op jit(solution)/shard_map/ppermute | solution.py:147
  44.6 1.7 %collective-permute-start.15 = (bf16[32,1280]{1,0:T(8,128)(2,1)S(1)}, bf16[32,1280]{1,0:T(8,128)(2,1)S(1)}, u32[]{:S(2)}, u32[]{:S(2)}) collective-permute-start(bf16[32,1280]{1,0:T(8,128)(2,1)S(1)} %get-tuple-element.23.refs_0_), channel_id=1, source_target_pairs={{0,1},{1,0},{2,3},{3,2},{4,5},{5,4},{6,7},{7,6},{8,9},{9,8},{10,11... | collective-permute-start | bytes 245768 | tf_op jit(solution)/shard_map/ppermute | solution.py:147
  44.9 5.3 %collective-permute-start.12 = (bf16[32,1280]{1,0:T(8,128)(2,1)S(1)}, bf16[32,1280]{1,0:T(8,128)(2,1)S(1)}, u32[]{:S(2)}, u32[]{:S(2)}) collective-permute-start(bf16[32,1280]{1,0:T(8,128)(2,1)S(1)} %collective-permute-done.11.refs_3_), channel_id=1, source_target_pairs={{0,2},{1,3},{2,0},{3,1},{4,6},{5,7},{6,4},{7,5},{8,10},{9,11},{10,... | collective-permute-start | bytes 245768 | tf_op jit(solution)/shard_map/ppermute | solution.py:147
  46.3 5.6 %collective-permute-start.6 = (bf16[32,1280]{1,0:T(8,128)(2,1)S(1)}, bf16[32,1280]{1,0:T(8,128)(2,1)S(1)}, u32[]{:S(2)}, u32[]{:S(2)}) collective-permute-start(bf16[32,1280]{1,0:T(8,128)(2,1)S(1)} %collective-permute-done.5.refs_1_), channel_id=1, source_target_pairs={{0,2},{1,3},{2,0},{3,1},{4,6},{5,7},{6,4},{7,5},{8,10},{9,11},{10,... | collective-permute-start | bytes 245768 | tf_op jit(solution)/shard_map/ppermute | solution.py:147
  46.9 6.1 %collective-permute-start.9 = (bf16[32,1280]{1,0:T(8,128)(2,1)S(1)}, bf16[32,1280]{1,0:T(8,128)(2,1)S(1)}, u32[]{:S(2)}, u32[]{:S(2)}) collective-permute-start(bf16[32,1280]{1,0:T(8,128)(2,1)S(1)} %collective-permute-done.8.refs_2_), channel_id=1, source_target_pairs={{0,2},{1,3},{2,0},{3,1},{4,6},{5,7},{6,4},{7,5},{8,10},{9,11},{10,... | collective-permute-start | bytes 245768 | tf_op jit(solution)/shard_map/ppermute | solution.py:147
  48.3 4.7 %collective-permute-start.16 = (bf16[32,1280]{1,0:T(8,128)(2,1)S(1)}, bf16[32,1280]{1,0:T(8,128)(2,1)S(1)}, u32[]{:S(2)}, u32[]{:S(2)}) collective-permute-start(bf16[32,1280]{1,0:T(8,128)(2,1)S(1)} %collective-permute-done.5.refs_1_), channel_id=1, source_target_pairs={{0,1},{1,0},{2,3},{3,2},{4,5},{5,4},{6,7},{7,6},{8,9},{9,8},{10,11... | collective-permute-start | bytes 245768 | tf_op jit(solution)/shard_map/ppermute | solution.py:147
  50.2 3.3 %collective-permute-start.17 = (bf16[32,1280]{1,0:T(8,128)(2,1)S(1)}, bf16[32,1280]{1,0:T(8,128)(2,1)S(1)}, u32[]{:S(2)}, u32[]{:S(2)}) collective-permute-start(bf16[32,1280]{1,0:T(8,128)(2,1)S(1)} %collective-permute-done.8.refs_2_), channel_id=1, source_target_pairs={{0,1},{1,0},{2,3},{3,2},{4,5},{5,4},{6,7},{7,6},{8,9},{9,8},{10,11... | collective-permute-start | bytes 245768 | tf_op jit(solution)/shard_map/ppermute | solution.py:147
  51.9 1.7 %collective-permute-start.18 = (bf16[32,1280]{1,0:T(8,128)(2,1)S(1)}, bf16[32,1280]{1,0:T(8,128)(2,1)S(1)}, u32[]{:S(2)}, u32[]{:S(2)}) collective-permute-start(bf16[32,1280]{1,0:T(8,128)(2,1)S(1)} %collective-permute-done.11.refs_3_), channel_id=1, source_target_pairs={{0,1},{1,0},{2,3},{3,2},{4,5},{5,4},{6,7},{7,6},{8,9},{9,8},{10,11... | collective-permute-start | bytes 245768 | tf_op jit(solution)/shard_map/ppermute | solution.py:147
  53.0 2.7 %collective-permute-start.4 = (bf16[32,1280]{1,0:T(8,128)(2,1)S(1)}, bf16[32,1280]{1,0:T(8,128)(2,1)S(1)}, u32[]{:S(2)}, u32[]{:S(2)}) collective-permute-start(bf16[32,1280]{1,0:T(8,128)(2,1)S(1)} %collective-permute-done.3.refs_0_), channel_id=1, source_target_pairs={{0,1},{1,0},{2,3},{3,2},{4,5},{5,4},{6,7},{7,6},{8,9},{9,8},{10,11... | collective-permute-start | bytes 245768 | tf_op jit(solution)/shard_map/ppermute | solution.py:147
  53.0 2.7 %collective-permute-start.10 = (bf16[32,1280]{1,0:T(8,128)(2,1)S(1)}, bf16[32,1280]{1,0:T(8,128)(2,1)S(1)}, u32[]{:S(2)}, u32[]{:S(2)}) collective-permute-start(bf16[32,1280]{1,0:T(8,128)(2,1)S(1)} %collective-permute-done.9.refs_2_), channel_id=1, source_target_pairs={{0,1},{1,0},{2,3},{3,2},{4,5},{5,4},{6,7},{7,6},{8,9},{9,8},{10,11... | collective-permute-start | bytes 245768 | tf_op jit(solution)/shard_map/ppermute | solution.py:147
  53.5 2.2 %collective-permute-start.13 = (bf16[32,1280]{1,0:T(8,128)(2,1)S(1)}, bf16[32,1280]{1,0:T(8,128)(2,1)S(1)}, u32[]{:S(2)}, u32[]{:S(2)}) collective-permute-start(bf16[32,1280]{1,0:T(8,128)(2,1)S(1)} %collective-permute-done.12.refs_3_), channel_id=1, source_target_pairs={{0,1},{1,0},{2,3},{3,2},{4,5},{5,4},{6,7},{7,6},{8,9},{9,8},{10,11... | collective-permute-start | bytes 245768 | tf_op jit(solution)/shard_map/ppermute | solution.py:147
  53.6 2.2 %collective-permute-start.7 = (bf16[32,1280]{1,0:T(8,128)(2,1)S(1)}, bf16[32,1280]{1,0:T(8,128)(2,1)S(1)}, u32[]{:S(2)}, u32[]{:S(2)}) collective-permute-start(bf16[32,1280]{1,0:T(8,128)(2,1)S(1)} %collective-permute-done.6.refs_1_), channel_id=1, source_target_pairs={{0,1},{1,0},{2,3},{3,2},{4,5},{5,4},{6,7},{7,6},{8,9},{9,8},{10,11... | collective-permute-start | bytes 245768 | tf_op jit(solution)/shard_map/ppermute | solution.py:147
  56.5 11.7 %collective-permute-start.21 = (bf16[4,32,640]{2,1,0:T(8,128)(2,1)S(1)}, bf16[4,32,640]{2,1,0:T(8,128)(2,1)S(1)}, u32[]{:S(2)}, u32[]{:S(2)}) collective-permute-start(bf16[4,32,640]{2,1,0:T(8,128)(2,1)S(1)} %get-tuple-element.32), channel_id=1, source_target_pairs={{0,4},{4,0},{8,12},{12,8},{1,5},{5,1},{9,13},{13,9},{2,6},{6,2},{1... | collective-permute-start | bytes 491528 | tf_op jit(solution)/shard_map/ppermute | solution.py:147
  61.5 15.0 %collective-permute-start.22 = (bf16[4,32,640]{2,1,0:T(8,128)(2,1)S(1)}, bf16[4,32,640]{2,1,0:T(8,128)(2,1)S(1)}, u32[]{:S(2)}, u32[]{:S(2)}) collective-permute-start(bf16[4,32,640]{2,1,0:T(8,128)(2,1)S(1)} %get-tuple-element.33), channel_id=1, source_target_pairs={{0,8},{4,12},{8,0},{12,4},{1,9},{5,13},{9,1},{13,5},{2,10},{6,14},... | collective-permute-start | bytes 491528 | tf_op jit(solution)/shard_map/ppermute | solution.py:147
  61.5 15.0 %collective-permute-start.23 = (bf16[4,32,640]{2,1,0:T(8,128)(2,1)S(1)}, bf16[4,32,640]{2,1,0:T(8,128)(2,1)S(1)}, u32[]{:S(2)}, u32[]{:S(2)}) collective-permute-start(bf16[4,32,640]{2,1,0:T(8,128)(2,1)S(1)} %get-tuple-element.34), channel_id=1, source_target_pairs={{0,12},{4,8},{8,4},{12,0},{1,13},{5,9},{9,5},{13,1},{2,14},{6,10},... | collective-permute-start | bytes 491528 | tf_op jit(solution)/shard_map/ppermute | solution.py:147
